TPU v7x, 32 devices: a whole 2x2x4 slice. The times are simulated.
32 devices in a mesh: parts: 2 (over x), blk: 16 (over z, y, core).
Axes of the slice: x: 2, y: 2, z: 4, core: 2. Of those that a mesh axis runs over, the one named last changes fastest.
Arguments:
- queries: bfloat16 [256, 4096], P(('parts', 'blk')), parts along dimension 0, may hold values from -48 to 48
- key_cache: bfloat16 [8192, 512], P(('parts', 'blk')), parts along dimension 0, may hold values from -6 to 6
- value_cache: bfloat16 [8192, 512], P(('parts', 'blk')), parts along dimension 0, may hold values from -6 to 6
- tile_page: int32 [8192], P(('parts', 'blk')), parts along dimension 0, may hold values from 0 to 15, never falling along the last dimension, each value on 1 to 512 neighbouring positions
- row_last: int32 [256], P(('parts', 'blk')), parts along dimension 0, may hold values from 0 to 15, as said below
Outputs:
- attention_out: bfloat16 [256, 4096], P(('parts', 'blk')), parts along dimension 0
There are 2 independent parts, one for each index of `parts`. A program takes and returns all parts, laid end to end along the dimension named above; each array names one. Nothing has to cross between parts.
Inputs may be any that keep to these rules, and one draw needn't show every extreme that they name: tile_page never falls along the tile tokens; every page of 0 to 15 has between 1 and 512 tokens, one exactly 512. row_last never falls along the text rows; the first row sees page 0 only and the last row sees every page.
All inputs are finite; a program needn't handle non-finite values.
Results may differ from a plain program's by a relative error of at most 0.00575.
Values may be sent and summed in bfloat16 or wider, within the bound.
No kernel may reach another device: no remote copies, remote signals or barrier semaphores. Data moves between devices by JAX's collectives and lax.ppermute only.
A program may use at most 64 MiB of HBM per device.

v0:
```python
import math

import jax
import jax.numpy as jnp
from jax import lax
from jax.sharding import PartitionSpec as P

HEADS = 32
KV_HEADS = 4
HEAD_DIM = 128


NEGATIVE_FILL = -1e30


def shifted(block, axis, distance):
    devices = range(lax.axis_size(axis))
    route = [((i - distance) % len(devices), i) for i in devices]
    return lax.ppermute(block, axis, route)


def absorb_block(queries, carried, key_cache, value_cache, tile_page):
    run_max, run_sum, last_float, run_out = carried
    row_count = queries.shape[0]
    group_size = HEADS // KV_HEADS
    q_heads = queries.reshape(row_count, KV_HEADS, group_size, HEAD_DIM)
    k_heads = key_cache.reshape(key_cache.shape[0], KV_HEADS, HEAD_DIM)
    v_heads = value_cache.reshape(value_cache.shape[0], KV_HEADS, HEAD_DIM)
    scores = jnp.einsum("rkgd,tkd->rkgt", q_heads, k_heads, preferred_element_type=jnp.float32)
    scores = scores * (1.0 / math.sqrt(HEAD_DIM))
    last_page = last_float.astype(jnp.int32)
    visible = (tile_page[None, :] <= last_page[:, None])[:, None, None, :]
    masked = jnp.where(visible, scores, NEGATIVE_FILL)
    new_max = jnp.maximum(run_max, jnp.max(masked, axis=-1))
    weights = jnp.where(visible, jnp.exp(scores - new_max[..., None]), 0.0)
    factor = jnp.exp(run_max - new_max)
    new_sum = run_sum * factor + jnp.sum(weights, axis=-1)
    update = jnp.einsum(
        "rkgt,tkd->rkgd", weights.astype(jnp.bfloat16), v_heads, preferred_element_type=jnp.float32
    )
    new_out = run_out * factor[..., None] + update
    return (new_max, new_sum, last_float, new_out)


def visit_block(queries, carried, key_cache, value_cache, tile_page):
    return absorb_block(queries, carried, key_cache, value_cache, tile_page)


def fresh_state(last_rows):
    row_count = last_rows.shape[0]
    group_size = HEADS // KV_HEADS
    run_max = jnp.full((row_count, KV_HEADS, group_size), NEGATIVE_FILL, jnp.float32)
    run_sum = jnp.zeros((row_count, KV_HEADS, group_size), jnp.float32)
    run_out = jnp.zeros((row_count, KV_HEADS, group_size, HEAD_DIM), jnp.float32)
    return (run_max, run_sum, last_rows.astype(jnp.float32), run_out)


def finish(carried):
    run_sum = carried[1]
    run_out = carried[3]
    result = (run_out / run_sum[..., None]).astype(jnp.bfloat16)
    return result.reshape(run_out.shape[0], HEADS * HEAD_DIM)


def shards(queries, key_cache, value_cache, tile_page, row_last):
    blocks = lax.axis_size("blk")
    half_rows = queries.shape[0] // 2
    front_rows = queries[:half_rows]
    rear_rows = queries[half_rows:]
    front_last = row_last[:half_rows]
    rear_last = row_last[half_rows:]
    own_rows = jnp.concatenate([front_rows, rear_rows], axis=0)
    own_last = jnp.concatenate([front_last, rear_last], axis=0)
    carried = visit_block(own_rows, fresh_state(own_last), key_cache, value_cache, tile_page)

    def turn(turn_index, carry_pair):
        query_rows, state_tuple = carry_pair
        query_rows = shifted(query_rows, "blk", 1)
        state_tuple = shifted(
            (state_tuple[0], state_tuple[1], state_tuple[2], state_tuple[3]), "blk", 1
        )
        return (query_rows, visit_block(query_rows, state_tuple, key_cache, value_cache, tile_page))

    final_pair = lax.fori_loop(0, blocks - 1, turn, (own_rows, carried))
    done_rows = shifted(finish(final_pair[1]), "blk", 1)
    front_done = done_rows[:half_rows]
    rear_done = done_rows[half_rows:]
    return jnp.concatenate([front_done, rear_done], axis=0)


def solution(mesh):
    placed = (
        P(("parts", "blk"), None),
        P(("parts", "blk"), None),
        P(("parts", "blk"), None),
        P(("parts", "blk")),
        P(("parts", "blk")),
    )
    return jax.shard_map(
        shards, mesh=mesh, in_specs=placed, out_specs=P(("parts", "blk"), None), check_vma=False
    )
```

profile of v0, /device:TPU:0, one launch (start us, length us, event | category | flops | bytes accessed | tf_op | source)
XLA Modules:
  0.0 150.1 jit_solution(10820893675862077489)
XLA Ops:
  0.0 0.8 copy.90
  0.8 1.1 reshape.77
  2.0 0.9 copy-done.1
  5.2 137.7 %while.19 = (s32[]{:T(128)}, bf16[8,4096]{1,0:T(8,128)(2,1)S(1)}, f32[8,4,8]{2,0,1:T(8,128)S(1)}, f32[8,4,8]{2,0,1:T(8,128)S(1)}, f32[8]{0:T(128)S(1)}, /*index=...) while((s32[]{:T(128)}, bf16[8,4096]{1,0:T(8,128)(2,1)S(1)}, ...), condition=%wide.wide.region_5.6_spmd, body=%wide.wide.region_2.5_spmd.sunk | while | flops 34212360 | bytes 2588253 | solution.py:84
  5.7 2.6 %collective-permute-start = (bf16[8,4096]{1,0:T(8,128)(2,1)S(1)}, bf16[8,4096]{1,0:T(8,128)(2,1)S(1)}, u32[]{:S(2)}, u32[]{:S(2)}) collective-permute-start(bf16[8,4096]{1,0:T(8,128)(2,1)S(1)} %get-tuple-element.210), channel_id=1, source_target_pairs={{15,0},{0,1},{1,2},{2,3},{3,4},{4,5},{5,6},{6,7},{7,8},{8,9},{9,10... | collective-permute-start | bytes 196616 | tf_op jit(solution)/shard_map/while/body/eval_jaxpr/ppermute | solution.py:19
  8.4 1.6 %collective-permute-start.3 = (f32[8,4,8]{2,0,1:T(8,128)S(1)}, f32[8,4,8]{2,0,1:T(8,128)S(1)}, u32[]{:S(2)}, u32[]{:S(2)}) collective-permute-start(f32[8,4,8]{2,0,1:T(8,128)S(1)} %get-tuple-element.212), channel_id=1, source_target_pairs={{15,0},{0,1},{1,2},{2,3},{3,4},{4,5},{5,6},{6,7},{7,8},{8,9},{9,10... | collective-permute-start | bytes 3080 | tf_op jit(solution)/shard_map/while/body/eval_jaxpr/ppermute | solution.py:19
  10.0 1.9 %collective-permute-done.2 = f32[8]{0:T(128)S(1)} collective-permute-done((f32[8]{0:T(128)S(1)}, f32[8]{0:T(128)S(1)}, u32[]{:S(2)}, u32[]{:S(2)}) %collective-permute-start.2) | collective-permute-done | bytes 64 | tf_op jit(solution)/shard_map/while/body/eval_jaxpr/ppermute | solution.py:19
  12.0 0.7 collective-permute-done
  13.0 1.2 collective-permute-done.1
  14.5 2.6 %collective-permute-done.4 = f32[8,4,8,128]{3,2,0,1:T(8,128)S(1)} collective-permute-done((f32[8,4,8,128]{3,2,0,1:T(8,128)S(1)}, f32[8,4,8,128]{3,2,0,1:T(8,128)S(1)}, u32[]{:S(2)}, u32[]{:S(2)}) %collective-permute-start.4) | collective-permute-done | bytes 131104 | tf_op jit(solution)/shard_map/while/body/eval_jaxpr/ppermute | solution.py:19
  17.5 1.3 collective-permute-start.3
  18.9 4.2 %collective-permute-done.2 = f32[8]{0:T(128)S(1)} collective-permute-done((f32[8]{0:T(128)S(1)}, f32[8]{0:T(128)S(1)}, u32[]{:S(2)}, u32[]{:S(2)}) %collective-permute-start.2) | collective-permute-done | bytes 64 | tf_op jit(solution)/shard_map/while/body/eval_jaxpr/ppermute | solution.py:19
  23.1 0.7 collective-permute-done
  24.4 1.5 %collective-permute-done.4 = f32[8,4,8,128]{3,2,0,1:T(8,128)S(1)} collective-permute-done((f32[8,4,8,128]{3,2,0,1:T(8,128)S(1)}, f32[8,4,8,128]{3,2,0,1:T(8,128)S(1)}, u32[]{:S(2)}, u32[]{:S(2)}) %collective-permute-start.4) | collective-permute-done | bytes 131104 | tf_op jit(solution)/shard_map/while/body/eval_jaxpr/ppermute | solution.py:19
  26.4 1.3 collective-permute-start.3
  27.8 4.2 %collective-permute-done.2 = f32[8]{0:T(128)S(1)} collective-permute-done((f32[8]{0:T(128)S(1)}, f32[8]{0:T(128)S(1)}, u32[]{:S(2)}, u32[]{:S(2)}) %collective-permute-start.2) | collective-permute-done | bytes 64 | tf_op jit(solution)/shard_map/while/body/eval_jaxpr/ppermute | solution.py:19
  32.0 0.7 collective-permute-done
  33.3 1.5 %collective-permute-done.4 = f32[8,4,8,128]{3,2,0,1:T(8,128)S(1)} collective-permute-done((f32[8,4,8,128]{3,2,0,1:T(8,128)S(1)}, f32[8,4,8,128]{3,2,0,1:T(8,128)S(1)}, u32[]{:S(2)}, u32[]{:S(2)}) %collective-permute-start.4) | collective-permute-done | bytes 131104 | tf_op jit(solution)/shard_map/while/body/eval_jaxpr/ppermute | solution.py:19
  35.4 5.4 %collective-permute-done.2 = f32[8]{0:T(128)S(1)} collective-permute-done((f32[8]{0:T(128)S(1)}, f32[8]{0:T(128)S(1)}, u32[]{:S(2)}, u32[]{:S(2)}) %collective-permute-start.2) | collective-permute-done | bytes 64 | tf_op jit(solution)/shard_map/while/body/eval_jaxpr/ppermute | solution.py:19
  40.9 0.7 collective-permute-done
  42.1 1.2 collective-permute-done.4
  43.8 2.1 %collective-permute-start.3 = (f32[8,4,8]{2,0,1:T(8,128)S(1)}, f32[8,4,8]{2,0,1:T(8,128)S(1)}, u32[]{:S(2)}, u32[]{:S(2)}) collective-permute-start(f32[8,4,8]{2,0,1:T(8,128)S(1)} %get-tuple-element.212), channel_id=1, source_target_pairs={{15,0},{0,1},{1,2},{2,3},{3,4},{4,5},{5,6},{6,7},{7,8},{8,9},{9,10... | collective-permute-start | bytes 3080 | tf_op jit(solution)/shard_map/while/body/eval_jaxpr/ppermute | solution.py:19
  46.0 3.4 %collective-permute-done.2 = f32[8]{0:T(128)S(1)} collective-permute-done((f32[8]{0:T(128)S(1)}, f32[8]{0:T(128)S(1)}, u32[]{:S(2)}, u32[]{:S(2)}) %collective-permute-start.2) | collective-permute-done | bytes 64 | tf_op jit(solution)/shard_map/while/body/eval_jaxpr/ppermute | solution.py:19
  49.4 0.7 collective-permute-done
  50.7 2.3 %collective-permute-done.4 = f32[8,4,8,128]{3,2,0,1:T(8,128)S(1)} collective-permute-done((f32[8,4,8,128]{3,2,0,1:T(8,128)S(1)}, f32[8,4,8,128]{3,2,0,1:T(8,128)S(1)}, u32[]{:S(2)}, u32[]{:S(2)}) %collective-permute-start.4) | collective-permute-done | bytes 131104 | tf_op jit(solution)/shard_map/while/body/eval_jaxpr/ppermute | solution.py:19
  53.5 1.3 collective-permute-start.3
  54.8 4.1 %collective-permute-done.2 = f32[8]{0:T(128)S(1)} collective-permute-done((f32[8]{0:T(128)S(1)}, f32[8]{0:T(128)S(1)}, u32[]{:S(2)}, u32[]{:S(2)}) %collective-permute-start.2) | collective-permute-done | bytes 64 | tf_op jit(solution)/shard_map/while/body/eval_jaxpr/ppermute | solution.py:19
  59.1 0.7 collective-permute-done
  60.3 1.5 %collective-permute-done.4 = f32[8,4,8,128]{3,2,0,1:T(8,128)S(1)} collective-permute-done((f32[8,4,8,128]{3,2,0,1:T(8,128)S(1)}, f32[8,4,8,128]{3,2,0,1:T(8,128)S(1)}, u32[]{:S(2)}, u32[]{:S(2)}) %collective-permute-start.4) | collective-permute-done | bytes 131104 | tf_op jit(solution)/shard_map/while/body/eval_jaxpr/ppermute | solution.py:19
  62.3 1.3 collective-permute-start.3
  63.7 4.2 %collective-permute-done.2 = f32[8]{0:T(128)S(1)} collective-permute-done((f32[8]{0:T(128)S(1)}, f32[8]{0:T(128)S(1)}, u32[]{:S(2)}, u32[]{:S(2)}) %collective-permute-start.2) | collective-permute-done | bytes 64 | tf_op jit(solution)/shard_map/while/body/eval_jaxpr/ppermute | solution.py:19
  68.0 0.7 collective-permute-done
  69.2 1.5 %collective-permute-done.4 = f32[8,4,8,128]{3,2,0,1:T(8,128)S(1)} collective-permute-done((f32[8,4,8,128]{3,2,0,1:T(8,128)S(1)}, f32[8,4,8,128]{3,2,0,1:T(8,128)S(1)}, u32[]{:S(2)}, u32[]{:S(2)}) %collective-permute-start.4) | collective-permute-done | bytes 131104 | tf_op jit(solution)/shard_map/while/body/eval_jaxpr/ppermute | solution.py:19
  71.2 1.0 collective-permute-start.3
  72.2 4.5 %collective-permute-done.2 = f32[8]{0:T(128)S(1)} collective-permute-done((f32[8]{0:T(128)S(1)}, f32[8]{0:T(128)S(1)}, u32[]{:S(2)}, u32[]{:S(2)}) %collective-permute-start.2) | collective-permute-done | bytes 64 | tf_op jit(solution)/shard_map/while/body/eval_jaxpr/ppermute | solution.py:19
  76.8 0.7 collective-permute-done
  78.1 1.2 collective-permute-done.4
  79.7 2.1 %collective-permute-start.3 = (f32[8,4,8]{2,0,1:T(8,128)S(1)}, f32[8,4,8]{2,0,1:T(8,128)S(1)}, u32[]{:S(2)}, u32[]{:S(2)}) collective-permute-start(f32[8,4,8]{2,0,1:T(8,128)S(1)} %get-tuple-element.212), channel_id=1, source_target_pairs={{15,0},{0,1},{1,2},{2,3},{3,4},{4,5},{5,6},{6,7},{7,8},{8,9},{9,10... | collective-permute-start | bytes 3080 | tf_op jit(solution)/shard_map/while/body/eval_jaxpr/ppermute | solution.py:19
  81.9 3.4 %collective-permute-done.2 = f32[8]{0:T(128)S(1)} collective-permute-done((f32[8]{0:T(128)S(1)}, f32[8]{0:T(128)S(1)}, u32[]{:S(2)}, u32[]{:S(2)}) %collective-permute-start.2) | collective-permute-done | bytes 64 | tf_op jit(solution)/shard_map/while/body/eval_jaxpr/ppermute | solution.py:19
  85.3 0.7 collective-permute-done
  86.6 2.3 %collective-permute-done.4 = f32[8,4,8,128]{3,2,0,1:T(8,128)S(1)} collective-permute-done((f32[8,4,8,128]{3,2,0,1:T(8,128)S(1)}, f32[8,4,8,128]{3,2,0,1:T(8,128)S(1)}, u32[]{:S(2)}, u32[]{:S(2)}) %collective-permute-start.4) | collective-permute-done | bytes 131104 | tf_op jit(solution)/shard_map/while/body/eval_jaxpr/ppermute | solution.py:19
  89.4 1.3 collective-permute-start.3
  90.8 4.1 %collective-permute-done.2 = f32[8]{0:T(128)S(1)} collective-permute-done((f32[8]{0:T(128)S(1)}, f32[8]{0:T(128)S(1)}, u32[]{:S(2)}, u32[]{:S(2)}) %collective-permute-start.2) | collective-permute-done | bytes 64 | tf_op jit(solution)/shard_map/while/body/eval_jaxpr/ppermute | solution.py:19
  95.0 0.7 collective-permute-done
  96.3 1.5 %collective-permute-done.4 = f32[8,4,8,128]{3,2,0,1:T(8,128)S(1)} collective-permute-done((f32[8,4,8,128]{3,2,0,1:T(8,128)S(1)}, f32[8,4,8,128]{3,2,0,1:T(8,128)S(1)}, u32[]{:S(2)}, u32[]{:S(2)}) %collective-permute-start.4) | collective-permute-done | bytes 131104 | tf_op jit(solution)/shard_map/while/body/eval_jaxpr/ppermute | solution.py:19
  98.3 1.3 collective-permute-start.3
  99.7 4.1 %collective-permute-done.2 = f32[8]{0:T(128)S(1)} collective-permute-done((f32[8]{0:T(128)S(1)}, f32[8]{0:T(128)S(1)}, u32[]{:S(2)}, u32[]{:S(2)}) %collective-permute-start.2) | collective-permute-done | bytes 64 | tf_op jit(solution)/shard_map/while/body/eval_jaxpr/ppermute | solution.py:19
  105.1 1.5 %collective-permute-done.4 = f32[8,4,8,128]{3,2,0,1:T(8,128)S(1)} collective-permute-done((f32[8,4,8,128]{3,2,0,1:T(8,128)S(1)}, f32[8,4,8,128]{3,2,0,1:T(8,128)S(1)}, u32[]{:S(2)}, u32[]{:S(2)}) %collective-permute-start.4) | collective-permute-done | bytes 131104 | tf_op jit(solution)/shard_map/while/body/eval_jaxpr/ppermute | solution.py:19
  107.1 1.0 collective-permute-start.3
  108.2 4.5 %collective-permute-done.2 = f32[8]{0:T(128)S(1)} collective-permute-done((f32[8]{0:T(128)S(1)}, f32[8]{0:T(128)S(1)}, u32[]{:S(2)}, u32[]{:S(2)}) %collective-permute-start.2) | collective-permute-done | bytes 64 | tf_op jit(solution)/shard_map/while/body/eval_jaxpr/ppermute | solution.py:19
  114.0 1.2 collective-permute-done.4
  115.7 2.1 %collective-permute-start.3 = (f32[8,4,8]{2,0,1:T(8,128)S(1)}, f32[8,4,8]{2,0,1:T(8,128)S(1)}, u32[]{:S(2)}, u32[]{:S(2)}) collective-permute-start(f32[8,4,8]{2,0,1:T(8,128)S(1)} %get-tuple-element.212), channel_id=1, source_target_pairs={{15,0},{0,1},{1,2},{2,3},{3,4},{4,5},{5,6},{6,7},{7,8},{8,9},{9,10... | collective-permute-start | bytes 3080 | tf_op jit(solution)/shard_map/while/body/eval_jaxpr/ppermute | solution.py:19
  117.8 3.4 %collective-permute-done.2 = f32[8]{0:T(128)S(1)} collective-permute-done((f32[8]{0:T(128)S(1)}, f32[8]{0:T(128)S(1)}, u32[]{:S(2)}, u32[]{:S(2)}) %collective-permute-start.2) | collective-permute-done | bytes 64 | tf_op jit(solution)/shard_map/while/body/eval_jaxpr/ppermute | solution.py:19
  121.3 0.7 collective-permute-done
  122.5 2.3 %collective-permute-done.4 = f32[8,4,8,128]{3,2,0,1:T(8,128)S(1)} collective-permute-done((f32[8,4,8,128]{3,2,0,1:T(8,128)S(1)}, f32[8,4,8,128]{3,2,0,1:T(8,128)S(1)}, u32[]{:S(2)}, u32[]{:S(2)}) %collective-permute-start.4) | collective-permute-done | bytes 131104 | tf_op jit(solution)/shard_map/while/body/eval_jaxpr/ppermute | solution.py:19
  125.3 1.3 collective-permute-start.3
  126.7 4.2 %collective-permute-done.2 = f32[8]{0:T(128)S(1)} collective-permute-done((f32[8]{0:T(128)S(1)}, f32[8]{0:T(128)S(1)}, u32[]{:S(2)}, u32[]{:S(2)}) %collective-permute-start.2) | collective-permute-done | bytes 64 | tf_op jit(solution)/shard_map/while/body/eval_jaxpr/ppermute | solution.py:19
  130.9 0.7 collective-permute-done
  132.2 1.5 %collective-permute-done.4 = f32[8,4,8,128]{3,2,0,1:T(8,128)S(1)} collective-permute-done((f32[8,4,8,128]{3,2,0,1:T(8,128)S(1)}, f32[8,4,8,128]{3,2,0,1:T(8,128)S(1)}, u32[]{:S(2)}, u32[]{:S(2)}) %collective-permute-start.4) | collective-permute-done | bytes 131104 | tf_op jit(solution)/shard_map/while/body/eval_jaxpr/ppermute | solution.py:19
  134.2 1.3 collective-permute-start.3
  135.6 4.1 %collective-permute-done.2 = f32[8]{0:T(128)S(1)} collective-permute-done((f32[8]{0:T(128)S(1)}, f32[8]{0:T(128)S(1)}, u32[]{:S(2)}, u32[]{:S(2)}) %collective-permute-start.2) | collective-permute-done | bytes 64 | tf_op jit(solution)/shard_map/while/body/eval_jaxpr/ppermute | solution.py:19
  139.8 0.7 collective-permute-done
  141.1 1.5 %collective-permute-done.4 = f32[8,4,8,128]{3,2,0,1:T(8,128)S(1)} collective-permute-done((f32[8,4,8,128]{3,2,0,1:T(8,128)S(1)}, f32[8,4,8,128]{3,2,0,1:T(8,128)S(1)}, u32[]{:S(2)}, u32[]{:S(2)}) %collective-permute-start.4) | collective-permute-done | bytes 131104 | tf_op jit(solution)/shard_map/while/body/eval_jaxpr/ppermute | solution.py:19
  143.1 6.4 %collective-permute-done.5 = bf16[8,4096]{1,0:T(8,128)(2,1)S(1)} collective-permute-done((bf16[8,4096]{1,0:T(8,128)(2,1)S(1)}, bf16[8,4096]{1,0:T(8,128)(2,1)S(1)}, u32[]{:S(2)}, u32[]{:S(2)}) %collective-permute-start.5) | collective-permute-done | bytes 65568 | tf_op jit(solution)/shard_map/ppermute | solution.py:19
  (247 shorter events, 21.1 us)
Async XLA Ops:
  5.2 6.8 %collective-permute-start.2 = (f32[8]{0:T(128)S(1)}, f32[8]{0:T(128)S(1)}, u32[]{:S(2)}, u32[]{:S(2)}) collective-permute-start(f32[8]{0:T(128)S(1)} %get-tuple-element.213), channel_id=1, source_target_pairs={{15,0},{0,1},{1,2},{2,3},{3,4},{4,5},{5,6},{6,7},{7,8},{8,9},{9,10... | collective-permute-start | bytes 104 | tf_op jit(solution)/shard_map/while/body/eval_jaxpr/ppermute | solution.py:19
  5.7 7.0 %collective-permute-start = (bf16[8,4096]{1,0:T(8,128)(2,1)S(1)}, bf16[8,4096]{1,0:T(8,128)(2,1)S(1)}, u32[]{:S(2)}, u32[]{:S(2)}) collective-permute-start(bf16[8,4096]{1,0:T(8,128)(2,1)S(1)} %get-tuple-element.210), channel_id=1, source_target_pairs={{15,0},{0,1},{1,2},{2,3},{3,4},{4,5},{5,6},{6,7},{7,8},{8,9},{9,10... | collective-permute-start | bytes 196616 | tf_op jit(solution)/shard_map/while/body/eval_jaxpr/ppermute | solution.py:19
  8.3 5.9 %collective-permute-start.1 = (f32[8,4,8]{2,0,1:T(8,128)S(1)}, f32[8,4,8]{2,0,1:T(8,128)S(1)}, u32[]{:S(2)}, u32[]{:S(2)}) collective-permute-start(f32[8,4,8]{2,0,1:T(8,128)S(1)} %get-tuple-element.211), channel_id=1, source_target_pairs={{15,0},{0,1},{1,2},{2,3},{3,4},{4,5},{5,6},{6,7},{7,8},{8,9},{9,10... | collective-permute-start | bytes 3080 | tf_op jit(solution)/shard_map/while/body/eval_jaxpr/ppermute | solution.py:19
  8.4 6.0 %collective-permute-start.3 = (f32[8,4,8]{2,0,1:T(8,128)S(1)}, f32[8,4,8]{2,0,1:T(8,128)S(1)}, u32[]{:S(2)}, u32[]{:S(2)}) collective-permute-start(f32[8,4,8]{2,0,1:T(8,128)S(1)} %get-tuple-element.212), channel_id=1, source_target_pairs={{15,0},{0,1},{1,2},{2,3},{3,4},{4,5},{5,6},{6,7},{7,8},{8,9},{9,10... | collective-permute-start | bytes 3080 | tf_op jit(solution)/shard_map/while/body/eval_jaxpr/ppermute | solution.py:19
  10.0 7.1 %collective-permute-start.4 = (f32[8,4,8,128]{3,2,0,1:T(8,128)S(1)}, f32[8,4,8,128]{3,2,0,1:T(8,128)S(1)}, u32[]{:S(2)}, u32[]{:S(2)}) collective-permute-start(f32[8,4,8,128]{3,2,0,1:T(8,128)S(1)} %get-tuple-element.214), channel_id=1, source_target_pairs={{15,0},{0,1},{1,2},{2,3},{3,4},{4,5},{5,6},{6,7},{7,8},{8,9},{9,10... | collective-permute-start | bytes 393224 | tf_op jit(solution)/shard_map/while/body/eval_jaxpr/ppermute | solution.py:19
  17.3 5.7 %collective-permute-start.2 = (f32[8]{0:T(128)S(1)}, f32[8]{0:T(128)S(1)}, u32[]{:S(2)}, u32[]{:S(2)}) collective-permute-start(f32[8]{0:T(128)S(1)} %get-tuple-element.213), channel_id=1, source_target_pairs={{15,0},{0,1},{1,2},{2,3},{3,4},{4,5},{5,6},{6,7},{7,8},{8,9},{9,10... | collective-permute-start | bytes 104 | tf_op jit(solution)/shard_map/while/body/eval_jaxpr/ppermute | solution.py:19
  17.4 6.4 %collective-permute-start = (bf16[8,4096]{1,0:T(8,128)(2,1)S(1)}, bf16[8,4096]{1,0:T(8,128)(2,1)S(1)}, u32[]{:S(2)}, u32[]{:S(2)}) collective-permute-start(bf16[8,4096]{1,0:T(8,128)(2,1)S(1)} %get-tuple-element.210), channel_id=1, source_target_pairs={{15,0},{0,1},{1,2},{2,3},{3,4},{4,5},{5,6},{6,7},{7,8},{8,9},{9,10... | collective-permute-start | bytes 196616 | tf_op jit(solution)/shard_map/while/body/eval_jaxpr/ppermute | solution.py:19
  17.5 6.7 %collective-permute-start.1 = (f32[8,4,8]{2,0,1:T(8,128)S(1)}, f32[8,4,8]{2,0,1:T(8,128)S(1)}, u32[]{:S(2)}, u32[]{:S(2)}) collective-permute-start(f32[8,4,8]{2,0,1:T(8,128)S(1)} %get-tuple-element.211), channel_id=1, source_target_pairs={{15,0},{0,1},{1,2},{2,3},{3,4},{4,5},{5,6},{6,7},{7,8},{8,9},{9,10... | collective-permute-start | bytes 3080 | tf_op jit(solution)/shard_map/while/body/eval_jaxpr/ppermute | solution.py:19
  17.5 6.9 %collective-permute-start.3 = (f32[8,4,8]{2,0,1:T(8,128)S(1)}, f32[8,4,8]{2,0,1:T(8,128)S(1)}, u32[]{:S(2)}, u32[]{:S(2)}) collective-permute-start(f32[8,4,8]{2,0,1:T(8,128)S(1)} %get-tuple-element.212), channel_id=1, source_target_pairs={{15,0},{0,1},{1,2},{2,3},{3,4},{4,5},{5,6},{6,7},{7,8},{8,9},{9,10... | collective-permute-start | bytes 3080 | tf_op jit(solution)/shard_map/while/body/eval_jaxpr/ppermute | solution.py:19
  18.8 7.1 %collective-permute-start.4 = (f32[8,4,8,128]{3,2,0,1:T(8,128)S(1)}, f32[8,4,8,128]{3,2,0,1:T(8,128)S(1)}, u32[]{:S(2)}, u32[]{:S(2)}) collective-permute-start(f32[8,4,8,128]{3,2,0,1:T(8,128)S(1)} %get-tuple-element.214), channel_id=1, source_target_pairs={{15,0},{0,1},{1,2},{2,3},{3,4},{4,5},{5,6},{6,7},{7,8},{8,9},{9,10... | collective-permute-start | bytes 393224 | tf_op jit(solution)/shard_map/while/body/eval_jaxpr/ppermute | solution.py:19
  26.2 5.7 %collective-permute-start.2 = (f32[8]{0:T(128)S(1)}, f32[8]{0:T(128)S(1)}, u32[]{:S(2)}, u32[]{:S(2)}) collective-permute-start(f32[8]{0:T(128)S(1)} %get-tuple-element.213), channel_id=1, source_target_pairs={{15,0},{0,1},{1,2},{2,3},{3,4},{4,5},{5,6},{6,7},{7,8},{8,9},{9,10... | collective-permute-start | bytes 104 | tf_op jit(solution)/shard_map/while/body/eval_jaxpr/ppermute | solution.py:19
  26.3 6.4 %collective-permute-start = (bf16[8,4096]{1,0:T(8,128)(2,1)S(1)}, bf16[8,4096]{1,0:T(8,128)(2,1)S(1)}, u32[]{:S(2)}, u32[]{:S(2)}) collective-permute-start(bf16[8,4096]{1,0:T(8,128)(2,1)S(1)} %get-tuple-element.210), channel_id=1, source_target_pairs={{15,0},{0,1},{1,2},{2,3},{3,4},{4,5},{5,6},{6,7},{7,8},{8,9},{9,10... | collective-permute-start | bytes 196616 | tf_op jit(solution)/shard_map/while/body/eval_jaxpr/ppermute | solution.py:19
  26.3 6.7 %collective-permute-start.1 = (f32[8,4,8]{2,0,1:T(8,128)S(1)}, f32[8,4,8]{2,0,1:T(8,128)S(1)}, u32[]{:S(2)}, u32[]{:S(2)}) collective-permute-start(f32[8,4,8]{2,0,1:T(8,128)S(1)} %get-tuple-element.211), channel_id=1, source_target_pairs={{15,0},{0,1},{1,2},{2,3},{3,4},{4,5},{5,6},{6,7},{7,8},{8,9},{9,10... | collective-permute-start | bytes 3080 | tf_op jit(solution)/shard_map/while/body/eval_jaxpr/ppermute | solution.py:19
  26.4 6.9 %collective-permute-start.3 = (f32[8,4,8]{2,0,1:T(8,128)S(1)}, f32[8,4,8]{2,0,1:T(8,128)S(1)}, u32[]{:S(2)}, u32[]{:S(2)}) collective-permute-start(f32[8,4,8]{2,0,1:T(8,128)S(1)} %get-tuple-element.212), channel_id=1, source_target_pairs={{15,0},{0,1},{1,2},{2,3},{3,4},{4,5},{5,6},{6,7},{7,8},{8,9},{9,10... | collective-permute-start | bytes 3080 | tf_op jit(solution)/shard_map/while/body/eval_jaxpr/ppermute | solution.py:19
  27.7 7.1 %collective-permute-start.4 = (f32[8,4,8,128]{3,2,0,1:T(8,128)S(1)}, f32[8,4,8,128]{3,2,0,1:T(8,128)S(1)}, u32[]{:S(2)}, u32[]{:S(2)}) collective-permute-start(f32[8,4,8,128]{3,2,0,1:T(8,128)S(1)} %get-tuple-element.214), channel_id=1, source_target_pairs={{15,0},{0,1},{1,2},{2,3},{3,4},{4,5},{5,6},{6,7},{7,8},{8,9},{9,10... | collective-permute-start | bytes 393224 | tf_op jit(solution)/shard_map/while/body/eval_jaxpr/ppermute | solution.py:19
  35.1 6.4 %collective-permute-start = (bf16[8,4096]{1,0:T(8,128)(2,1)S(1)}, bf16[8,4096]{1,0:T(8,128)(2,1)S(1)}, u32[]{:S(2)}, u32[]{:S(2)}) collective-permute-start(bf16[8,4096]{1,0:T(8,128)(2,1)S(1)} %get-tuple-element.210), channel_id=1, source_target_pairs={{15,0},{0,1},{1,2},{2,3},{3,4},{4,5},{5,6},{6,7},{7,8},{8,9},{9,10... | collective-permute-start | bytes 196616 | tf_op jit(solution)/shard_map/while/body/eval_jaxpr/ppermute | solution.py:19
  35.2 6.7 %collective-permute-start.1 = (f32[8,4,8]{2,0,1:T(8,128)S(1)}, f32[8,4,8]{2,0,1:T(8,128)S(1)}, u32[]{:S(2)}, u32[]{:S(2)}) collective-permute-start(f32[8,4,8]{2,0,1:T(8,128)S(1)} %get-tuple-element.211), channel_id=1, source_target_pairs={{15,0},{0,1},{1,2},{2,3},{3,4},{4,5},{5,6},{6,7},{7,8},{8,9},{9,10... | collective-permute-start | bytes 3080 | tf_op jit(solution)/shard_map/while/body/eval_jaxpr/ppermute | solution.py:19
  35.3 6.9 %collective-permute-start.3 = (f32[8,4,8]{2,0,1:T(8,128)S(1)}, f32[8,4,8]{2,0,1:T(8,128)S(1)}, u32[]{:S(2)}, u32[]{:S(2)}) collective-permute-start(f32[8,4,8]{2,0,1:T(8,128)S(1)} %get-tuple-element.212), channel_id=1, source_target_pairs={{15,0},{0,1},{1,2},{2,3},{3,4},{4,5},{5,6},{6,7},{7,8},{8,9},{9,10... | collective-permute-start | bytes 3080 | tf_op jit(solution)/shard_map/while/body/eval_jaxpr/ppermute | solution.py:19
  35.3 8.0 %collective-permute-start.4 = (f32[8,4,8,128]{3,2,0,1:T(8,128)S(1)}, f32[8,4,8,128]{3,2,0,1:T(8,128)S(1)}, u32[]{:S(2)}, u32[]{:S(2)}) collective-permute-start(f32[8,4,8,128]{3,2,0,1:T(8,128)S(1)} %get-tuple-element.214), channel_id=1, source_target_pairs={{15,0},{0,1},{1,2},{2,3},{3,4},{4,5},{5,6},{6,7},{7,8},{8,9},{9,10... | collective-permute-start | bytes 393224 | tf_op jit(solution)/shard_map/while/body/eval_jaxpr/ppermute | solution.py:19
  43.7 6.4 %collective-permute-start = (bf16[8,4096]{1,0:T(8,128)(2,1)S(1)}, bf16[8,4096]{1,0:T(8,128)(2,1)S(1)}, u32[]{:S(2)}, u32[]{:S(2)}) collective-permute-start(bf16[8,4096]{1,0:T(8,128)(2,1)S(1)} %get-tuple-element.210), channel_id=1, source_target_pairs={{15,0},{0,1},{1,2},{2,3},{3,4},{4,5},{5,6},{6,7},{7,8},{8,9},{9,10... | collective-permute-start | bytes 196616 | tf_op jit(solution)/shard_map/while/body/eval_jaxpr/ppermute | solution.py:19
  43.7 6.7 %collective-permute-start.1 = (f32[8,4,8]{2,0,1:T(8,128)S(1)}, f32[8,4,8]{2,0,1:T(8,128)S(1)}, u32[]{:S(2)}, u32[]{:S(2)}) collective-permute-start(f32[8,4,8]{2,0,1:T(8,128)S(1)} %get-tuple-element.211), channel_id=1, source_target_pairs={{15,0},{0,1},{1,2},{2,3},{3,4},{4,5},{5,6},{6,7},{7,8},{8,9},{9,10... | collective-permute-start | bytes 3080 | tf_op jit(solution)/shard_map/while/body/eval_jaxpr/ppermute | solution.py:19
  43.8 6.9 %collective-permute-start.3 = (f32[8,4,8]{2,0,1:T(8,128)S(1)}, f32[8,4,8]{2,0,1:T(8,128)S(1)}, u32[]{:S(2)}, u32[]{:S(2)}) collective-permute-start(f32[8,4,8]{2,0,1:T(8,128)S(1)} %get-tuple-element.212), channel_id=1, source_target_pairs={{15,0},{0,1},{1,2},{2,3},{3,4},{4,5},{5,6},{6,7},{7,8},{8,9},{9,10... | collective-permute-start | bytes 3080 | tf_op jit(solution)/shard_map/while/body/eval_jaxpr/ppermute | solution.py:19
  45.9 7.1 %collective-permute-start.4 = (f32[8,4,8,128]{3,2,0,1:T(8,128)S(1)}, f32[8,4,8,128]{3,2,0,1:T(8,128)S(1)}, u32[]{:S(2)}, u32[]{:S(2)}) collective-permute-start(f32[8,4,8,128]{3,2,0,1:T(8,128)S(1)} %get-tuple-element.214), channel_id=1, source_target_pairs={{15,0},{0,1},{1,2},{2,3},{3,4},{4,5},{5,6},{6,7},{7,8},{8,9},{9,10... | collective-permute-start | bytes 393224 | tf_op jit(solution)/shard_map/while/body/eval_jaxpr/ppermute | solution.py:19
  53.3 6.4 %collective-permute-start = (bf16[8,4096]{1,0:T(8,128)(2,1)S(1)}, bf16[8,4096]{1,0:T(8,128)(2,1)S(1)}, u32[]{:S(2)}, u32[]{:S(2)}) collective-permute-start(bf16[8,4096]{1,0:T(8,128)(2,1)S(1)} %get-tuple-element.210), channel_id=1, source_target_pairs={{15,0},{0,1},{1,2},{2,3},{3,4},{4,5},{5,6},{6,7},{7,8},{8,9},{9,10... | collective-permute-start | bytes 196616 | tf_op jit(solution)/shard_map/while/body/eval_jaxpr/ppermute | solution.py:19
  53.4 6.7 %collective-permute-start.1 = (f32[8,4,8]{2,0,1:T(8,128)S(1)}, f32[8,4,8]{2,0,1:T(8,128)S(1)}, u32[]{:S(2)}, u32[]{:S(2)}) collective-permute-start(f32[8,4,8]{2,0,1:T(8,128)S(1)} %get-tuple-element.211), channel_id=1, source_target_pairs={{15,0},{0,1},{1,2},{2,3},{3,4},{4,5},{5,6},{6,7},{7,8},{8,9},{9,10... | collective-permute-start | bytes 3080 | tf_op jit(solution)/shard_map/while/body/eval_jaxpr/ppermute | solution.py:19
  53.5 6.9 %collective-permute-start.3 = (f32[8,4,8]{2,0,1:T(8,128)S(1)}, f32[8,4,8]{2,0,1:T(8,128)S(1)}, u32[]{:S(2)}, u32[]{:S(2)}) collective-permute-start(f32[8,4,8]{2,0,1:T(8,128)S(1)} %get-tuple-element.212), channel_id=1, source_target_pairs={{15,0},{0,1},{1,2},{2,3},{3,4},{4,5},{5,6},{6,7},{7,8},{8,9},{9,10... | collective-permute-start | bytes 3080 | tf_op jit(solution)/shard_map/while/body/eval_jaxpr/ppermute | solution.py:19
  54.8 7.1 %collective-permute-start.4 = (f32[8,4,8,128]{3,2,0,1:T(8,128)S(1)}, f32[8,4,8,128]{3,2,0,1:T(8,128)S(1)}, u32[]{:S(2)}, u32[]{:S(2)}) collective-permute-start(f32[8,4,8,128]{3,2,0,1:T(8,128)S(1)} %get-tuple-element.214), channel_id=1, source_target_pairs={{15,0},{0,1},{1,2},{2,3},{3,4},{4,5},{5,6},{6,7},{7,8},{8,9},{9,10... | collective-permute-start | bytes 393224 | tf_op jit(solution)/shard_map/while/body/eval_jaxpr/ppermute | solution.py:19
  62.2 6.4 %collective-permute-start = (bf16[8,4096]{1,0:T(8,128)(2,1)S(1)}, bf16[8,4096]{1,0:T(8,128)(2,1)S(1)}, u32[]{:S(2)}, u32[]{:S(2)}) collective-permute-start(bf16[8,4096]{1,0:T(8,128)(2,1)S(1)} %get-tuple-element.210), channel_id=1, source_target_pairs={{15,0},{0,1},{1,2},{2,3},{3,4},{4,5},{5,6},{6,7},{7,8},{8,9},{9,10... | collective-permute-start | bytes 196616 | tf_op jit(solution)/shard_map/while/body/eval_jaxpr/ppermute | solution.py:19
  62.3 6.7 %collective-permute-start.1 = (f32[8,4,8]{2,0,1:T(8,128)S(1)}, f32[8,4,8]{2,0,1:T(8,128)S(1)}, u32[]{:S(2)}, u32[]{:S(2)}) collective-permute-start(f32[8,4,8]{2,0,1:T(8,128)S(1)} %get-tuple-element.211), channel_id=1, source_target_pairs={{15,0},{0,1},{1,2},{2,3},{3,4},{4,5},{5,6},{6,7},{7,8},{8,9},{9,10... | collective-permute-start | bytes 3080 | tf_op jit(solution)/shard_map/while/body/eval_jaxpr/ppermute | solution.py:19
  62.3 6.9 %collective-permute-start.3 = (f32[8,4,8]{2,0,1:T(8,128)S(1)}, f32[8,4,8]{2,0,1:T(8,128)S(1)}, u32[]{:S(2)}, u32[]{:S(2)}) collective-permute-start(f32[8,4,8]{2,0,1:T(8,128)S(1)} %get-tuple-element.212), channel_id=1, source_target_pairs={{15,0},{0,1},{1,2},{2,3},{3,4},{4,5},{5,6},{6,7},{7,8},{8,9},{9,10... | collective-permute-start | bytes 3080 | tf_op jit(solution)/shard_map/while/body/eval_jaxpr/ppermute | solution.py:19
  63.7 7.1 %collective-permute-start.4 = (f32[8,4,8,128]{3,2,0,1:T(8,128)S(1)}, f32[8,4,8,128]{3,2,0,1:T(8,128)S(1)}, u32[]{:S(2)}, u32[]{:S(2)}) collective-permute-start(f32[8,4,8,128]{3,2,0,1:T(8,128)S(1)} %get-tuple-element.214), channel_id=1, source_target_pairs={{15,0},{0,1},{1,2},{2,3},{3,4},{4,5},{5,6},{6,7},{7,8},{8,9},{9,10... | collective-permute-start | bytes 393224 | tf_op jit(solution)/shard_map/while/body/eval_jaxpr/ppermute | solution.py:19
  71.1 6.4 %collective-permute-start = (bf16[8,4096]{1,0:T(8,128)(2,1)S(1)}, bf16[8,4096]{1,0:T(8,128)(2,1)S(1)}, u32[]{:S(2)}, u32[]{:S(2)}) collective-permute-start(bf16[8,4096]{1,0:T(8,128)(2,1)S(1)} %get-tuple-element.210), channel_id=1, source_target_pairs={{15,0},{0,1},{1,2},{2,3},{3,4},{4,5},{5,6},{6,7},{7,8},{8,9},{9,10... | collective-permute-start | bytes 196616 | tf_op jit(solution)/shard_map/while/body/eval_jaxpr/ppermute | solution.py:19
  71.1 6.7 %collective-permute-start.1 = (f32[8,4,8]{2,0,1:T(8,128)S(1)}, f32[8,4,8]{2,0,1:T(8,128)S(1)}, u32[]{:S(2)}, u32[]{:S(2)}) collective-permute-start(f32[8,4,8]{2,0,1:T(8,128)S(1)} %get-tuple-element.211), channel_id=1, source_target_pairs={{15,0},{0,1},{1,2},{2,3},{3,4},{4,5},{5,6},{6,7},{7,8},{8,9},{9,10... | collective-permute-start | bytes 3080 | tf_op jit(solution)/shard_map/while/body/eval_jaxpr/ppermute | solution.py:19
  71.2 6.9 %collective-permute-start.3 = (f32[8,4,8]{2,0,1:T(8,128)S(1)}, f32[8,4,8]{2,0,1:T(8,128)S(1)}, u32[]{:S(2)}, u32[]{:S(2)}) collective-permute-start(f32[8,4,8]{2,0,1:T(8,128)S(1)} %get-tuple-element.212), channel_id=1, source_target_pairs={{15,0},{0,1},{1,2},{2,3},{3,4},{4,5},{5,6},{6,7},{7,8},{8,9},{9,10... | collective-permute-start | bytes 3080 | tf_op jit(solution)/shard_map/while/body/eval_jaxpr/ppermute | solution.py:19
  72.2 7.1 %collective-permute-start.4 = (f32[8,4,8,128]{3,2,0,1:T(8,128)S(1)}, f32[8,4,8,128]{3,2,0,1:T(8,128)S(1)}, u32[]{:S(2)}, u32[]{:S(2)}) collective-permute-start(f32[8,4,8,128]{3,2,0,1:T(8,128)S(1)} %get-tuple-element.214), channel_id=1, source_target_pairs={{15,0},{0,1},{1,2},{2,3},{3,4},{4,5},{5,6},{6,7},{7,8},{8,9},{9,10... | collective-permute-start | bytes 393224 | tf_op jit(solution)/shard_map/while/body/eval_jaxpr/ppermute | solution.py:19
  79.6 6.4 %collective-permute-start = (bf16[8,4096]{1,0:T(8,128)(2,1)S(1)}, bf16[8,4096]{1,0:T(8,128)(2,1)S(1)}, u32[]{:S(2)}, u32[]{:S(2)}) collective-permute-start(bf16[8,4096]{1,0:T(8,128)(2,1)S(1)} %get-tuple-element.210), channel_id=1, source_target_pairs={{15,0},{0,1},{1,2},{2,3},{3,4},{4,5},{5,6},{6,7},{7,8},{8,9},{9,10... | collective-permute-start | bytes 196616 | tf_op jit(solution)/shard_map/while/body/eval_jaxpr/ppermute | solution.py:19
  79.7 6.7 %collective-permute-start.1 = (f32[8,4,8]{2,0,1:T(8,128)S(1)}, f32[8,4,8]{2,0,1:T(8,128)S(1)}, u32[]{:S(2)}, u32[]{:S(2)}) collective-permute-start(f32[8,4,8]{2,0,1:T(8,128)S(1)} %get-tuple-element.211), channel_id=1, source_target_pairs={{15,0},{0,1},{1,2},{2,3},{3,4},{4,5},{5,6},{6,7},{7,8},{8,9},{9,10... | collective-permute-start | bytes 3080 | tf_op jit(solution)/shard_map/while/body/eval_jaxpr/ppermute | solution.py:19
  79.7 6.9 %collective-permute-start.3 = (f32[8,4,8]{2,0,1:T(8,128)S(1)}, f32[8,4,8]{2,0,1:T(8,128)S(1)}, u32[]{:S(2)}, u32[]{:S(2)}) collective-permute-start(f32[8,4,8]{2,0,1:T(8,128)S(1)} %get-tuple-element.212), channel_id=1, source_target_pairs={{15,0},{0,1},{1,2},{2,3},{3,4},{4,5},{5,6},{6,7},{7,8},{8,9},{9,10... | collective-permute-start | bytes 3080 | tf_op jit(solution)/shard_map/while/body/eval_jaxpr/ppermute | solution.py:19
  81.8 7.1 %collective-permute-start.4 = (f32[8,4,8,128]{3,2,0,1:T(8,128)S(1)}, f32[8,4,8,128]{3,2,0,1:T(8,128)S(1)}, u32[]{:S(2)}, u32[]{:S(2)}) collective-permute-start(f32[8,4,8,128]{3,2,0,1:T(8,128)S(1)} %get-tuple-element.214), channel_id=1, source_target_pairs={{15,0},{0,1},{1,2},{2,3},{3,4},{4,5},{5,6},{6,7},{7,8},{8,9},{9,10... | collective-permute-start | bytes 393224 | tf_op jit(solution)/shard_map/while/body/eval_jaxpr/ppermute | solution.py:19
  89.3 6.4 %collective-permute-start = (bf16[8,4096]{1,0:T(8,128)(2,1)S(1)}, bf16[8,4096]{1,0:T(8,128)(2,1)S(1)}, u32[]{:S(2)}, u32[]{:S(2)}) collective-permute-start(bf16[8,4096]{1,0:T(8,128)(2,1)S(1)} %get-tuple-element.210), channel_id=1, source_target_pairs={{15,0},{0,1},{1,2},{2,3},{3,4},{4,5},{5,6},{6,7},{7,8},{8,9},{9,10... | collective-permute-start | bytes 196616 | tf_op jit(solution)/shard_map/while/body/eval_jaxpr/ppermute | solution.py:19
  89.3 6.7 %collective-permute-start.1 = (f32[8,4,8]{2,0,1:T(8,128)S(1)}, f32[8,4,8]{2,0,1:T(8,128)S(1)}, u32[]{:S(2)}, u32[]{:S(2)}) collective-permute-start(f32[8,4,8]{2,0,1:T(8,128)S(1)} %get-tuple-element.211), channel_id=1, source_target_pairs={{15,0},{0,1},{1,2},{2,3},{3,4},{4,5},{5,6},{6,7},{7,8},{8,9},{9,10... | collective-permute-start | bytes 3080 | tf_op jit(solution)/shard_map/while/body/eval_jaxpr/ppermute | solution.py:19
  89.4 6.9 %collective-permute-start.3 = (f32[8,4,8]{2,0,1:T(8,128)S(1)}, f32[8,4,8]{2,0,1:T(8,128)S(1)}, u32[]{:S(2)}, u32[]{:S(2)}) collective-permute-start(f32[8,4,8]{2,0,1:T(8,128)S(1)} %get-tuple-element.212), channel_id=1, source_target_pairs={{15,0},{0,1},{1,2},{2,3},{3,4},{4,5},{5,6},{6,7},{7,8},{8,9},{9,10... | collective-permute-start | bytes 3080 | tf_op jit(solution)/shard_map/while/body/eval_jaxpr/ppermute | solution.py:19
  90.7 7.1 %collective-permute-start.4 = (f32[8,4,8,128]{3,2,0,1:T(8,128)S(1)}, f32[8,4,8,128]{3,2,0,1:T(8,128)S(1)}, u32[]{:S(2)}, u32[]{:S(2)}) collective-permute-start(f32[8,4,8,128]{3,2,0,1:T(8,128)S(1)} %get-tuple-element.214), channel_id=1, source_target_pairs={{15,0},{0,1},{1,2},{2,3},{3,4},{4,5},{5,6},{6,7},{7,8},{8,9},{9,10... | collective-permute-start | bytes 393224 | tf_op jit(solution)/shard_map/while/body/eval_jaxpr/ppermute | solution.py:19
  98.1 6.4 %collective-permute-start = (bf16[8,4096]{1,0:T(8,128)(2,1)S(1)}, bf16[8,4096]{1,0:T(8,128)(2,1)S(1)}, u32[]{:S(2)}, u32[]{:S(2)}) collective-permute-start(bf16[8,4096]{1,0:T(8,128)(2,1)S(1)} %get-tuple-element.210), channel_id=1, source_target_pairs={{15,0},{0,1},{1,2},{2,3},{3,4},{4,5},{5,6},{6,7},{7,8},{8,9},{9,10... | collective-permute-start | bytes 196616 | tf_op jit(solution)/shard_map/while/body/eval_jaxpr/ppermute | solution.py:19
  98.2 6.7 %collective-permute-start.1 = (f32[8,4,8]{2,0,1:T(8,128)S(1)}, f32[8,4,8]{2,0,1:T(8,128)S(1)}, u32[]{:S(2)}, u32[]{:S(2)}) collective-permute-start(f32[8,4,8]{2,0,1:T(8,128)S(1)} %get-tuple-element.211), channel_id=1, source_target_pairs={{15,0},{0,1},{1,2},{2,3},{3,4},{4,5},{5,6},{6,7},{7,8},{8,9},{9,10... | collective-permute-start | bytes 3080 | tf_op jit(solution)/shard_map/while/body/eval_jaxpr/ppermute | solution.py:19
  98.3 6.9 %collective-permute-start.3 = (f32[8,4,8]{2,0,1:T(8,128)S(1)}, f32[8,4,8]{2,0,1:T(8,128)S(1)}, u32[]{:S(2)}, u32[]{:S(2)}) collective-permute-start(f32[8,4,8]{2,0,1:T(8,128)S(1)} %get-tuple-element.212), channel_id=1, source_target_pairs={{15,0},{0,1},{1,2},{2,3},{3,4},{4,5},{5,6},{6,7},{7,8},{8,9},{9,10... | collective-permute-start | bytes 3080 | tf_op jit(solution)/shard_map/while/body/eval_jaxpr/ppermute | solution.py:19
  99.6 7.1 %collective-permute-start.4 = (f32[8,4,8,128]{3,2,0,1:T(8,128)S(1)}, f32[8,4,8,128]{3,2,0,1:T(8,128)S(1)}, u32[]{:S(2)}, u32[]{:S(2)}) collective-permute-start(f32[8,4,8,128]{3,2,0,1:T(8,128)S(1)} %get-tuple-element.214), channel_id=1, source_target_pairs={{15,0},{0,1},{1,2},{2,3},{3,4},{4,5},{5,6},{6,7},{7,8},{8,9},{9,10... | collective-permute-start | bytes 393224 | tf_op jit(solution)/shard_map/while/body/eval_jaxpr/ppermute | solution.py:19
  107.0 6.4 %collective-permute-start = (bf16[8,4096]{1,0:T(8,128)(2,1)S(1)}, bf16[8,4096]{1,0:T(8,128)(2,1)S(1)}, u32[]{:S(2)}, u32[]{:S(2)}) collective-permute-start(bf16[8,4096]{1,0:T(8,128)(2,1)S(1)} %get-tuple-element.210), channel_id=1, source_target_pairs={{15,0},{0,1},{1,2},{2,3},{3,4},{4,5},{5,6},{6,7},{7,8},{8,9},{9,10... | collective-permute-start | bytes 196616 | tf_op jit(solution)/shard_map/while/body/eval_jaxpr/ppermute | solution.py:19
  107.1 6.7 %collective-permute-start.1 = (f32[8,4,8]{2,0,1:T(8,128)S(1)}, f32[8,4,8]{2,0,1:T(8,128)S(1)}, u32[]{:S(2)}, u32[]{:S(2)}) collective-permute-start(f32[8,4,8]{2,0,1:T(8,128)S(1)} %get-tuple-element.211), channel_id=1, source_target_pairs={{15,0},{0,1},{1,2},{2,3},{3,4},{4,5},{5,6},{6,7},{7,8},{8,9},{9,10... | collective-permute-start | bytes 3080 | tf_op jit(solution)/shard_map/while/body/eval_jaxpr/ppermute | solution.py:19
  107.1 6.9 %collective-permute-start.3 = (f32[8,4,8]{2,0,1:T(8,128)S(1)}, f32[8,4,8]{2,0,1:T(8,128)S(1)}, u32[]{:S(2)}, u32[]{:S(2)}) collective-permute-start(f32[8,4,8]{2,0,1:T(8,128)S(1)} %get-tuple-element.212), channel_id=1, source_target_pairs={{15,0},{0,1},{1,2},{2,3},{3,4},{4,5},{5,6},{6,7},{7,8},{8,9},{9,10... | collective-permute-start | bytes 3080 | tf_op jit(solution)/shard_map/while/body/eval_jaxpr/ppermute | solution.py:19
  108.1 7.1 %collective-permute-start.4 = (f32[8,4,8,128]{3,2,0,1:T(8,128)S(1)}, f32[8,4,8,128]{3,2,0,1:T(8,128)S(1)}, u32[]{:S(2)}, u32[]{:S(2)}) collective-permute-start(f32[8,4,8,128]{3,2,0,1:T(8,128)S(1)} %get-tuple-element.214), channel_id=1, source_target_pairs={{15,0},{0,1},{1,2},{2,3},{3,4},{4,5},{5,6},{6,7},{7,8},{8,9},{9,10... | collective-permute-start | bytes 393224 | tf_op jit(solution)/shard_map/while/body/eval_jaxpr/ppermute | solution.py:19
  115.5 6.4 %collective-permute-start = (bf16[8,4096]{1,0:T(8,128)(2,1)S(1)}, bf16[8,4096]{1,0:T(8,128)(2,1)S(1)}, u32[]{:S(2)}, u32[]{:S(2)}) collective-permute-start(bf16[8,4096]{1,0:T(8,128)(2,1)S(1)} %get-tuple-element.210), channel_id=1, source_target_pairs={{15,0},{0,1},{1,2},{2,3},{3,4},{4,5},{5,6},{6,7},{7,8},{8,9},{9,10... | collective-permute-start | bytes 196616 | tf_op jit(solution)/shard_map/while/body/eval_jaxpr/ppermute | solution.py:19
  115.6 6.7 %collective-permute-start.1 = (f32[8,4,8]{2,0,1:T(8,128)S(1)}, f32[8,4,8]{2,0,1:T(8,128)S(1)}, u32[]{:S(2)}, u32[]{:S(2)}) collective-permute-start(f32[8,4,8]{2,0,1:T(8,128)S(1)} %get-tuple-element.211), channel_id=1, source_target_pairs={{15,0},{0,1},{1,2},{2,3},{3,4},{4,5},{5,6},{6,7},{7,8},{8,9},{9,10... | collective-permute-start | bytes 3080 | tf_op jit(solution)/shard_map/while/body/eval_jaxpr/ppermute | solution.py:19
  115.7 6.9 %collective-permute-start.3 = (f32[8,4,8]{2,0,1:T(8,128)S(1)}, f32[8,4,8]{2,0,1:T(8,128)S(1)}, u32[]{:S(2)}, u32[]{:S(2)}) collective-permute-start(f32[8,4,8]{2,0,1:T(8,128)S(1)} %get-tuple-element.212), channel_id=1, source_target_pairs={{15,0},{0,1},{1,2},{2,3},{3,4},{4,5},{5,6},{6,7},{7,8},{8,9},{9,10... | collective-permute-start | bytes 3080 | tf_op jit(solution)/shard_map/while/body/eval_jaxpr/ppermute | solution.py:19
  117.8 7.1 %collective-permute-start.4 = (f32[8,4,8,128]{3,2,0,1:T(8,128)S(1)}, f32[8,4,8,128]{3,2,0,1:T(8,128)S(1)}, u32[]{:S(2)}, u32[]{:S(2)}) collective-permute-start(f32[8,4,8,128]{3,2,0,1:T(8,128)S(1)} %get-tuple-element.214), channel_id=1, source_target_pairs={{15,0},{0,1},{1,2},{2,3},{3,4},{4,5},{5,6},{6,7},{7,8},{8,9},{9,10... | collective-permute-start | bytes 393224 | tf_op jit(solution)/shard_map/while/body/eval_jaxpr/ppermute | solution.py:19
  125.2 6.4 %collective-permute-start = (bf16[8,4096]{1,0:T(8,128)(2,1)S(1)}, bf16[8,4096]{1,0:T(8,128)(2,1)S(1)}, u32[]{:S(2)}, u32[]{:S(2)}) collective-permute-start(bf16[8,4096]{1,0:T(8,128)(2,1)S(1)} %get-tuple-element.210), channel_id=1, source_target_pairs={{15,0},{0,1},{1,2},{2,3},{3,4},{4,5},{5,6},{6,7},{7,8},{8,9},{9,10... | collective-permute-start | bytes 196616 | tf_op jit(solution)/shard_map/while/body/eval_jaxpr/ppermute | solution.py:19
  125.3 6.7 %collective-permute-start.1 = (f32[8,4,8]{2,0,1:T(8,128)S(1)}, f32[8,4,8]{2,0,1:T(8,128)S(1)}, u32[]{:S(2)}, u32[]{:S(2)}) collective-permute-start(f32[8,4,8]{2,0,1:T(8,128)S(1)} %get-tuple-element.211), channel_id=1, source_target_pairs={{15,0},{0,1},{1,2},{2,3},{3,4},{4,5},{5,6},{6,7},{7,8},{8,9},{9,10... | collective-permute-start | bytes 3080 | tf_op jit(solution)/shard_map/while/body/eval_jaxpr/ppermute | solution.py:19
  125.3 6.9 %collective-permute-start.3 = (f32[8,4,8]{2,0,1:T(8,128)S(1)}, f32[8,4,8]{2,0,1:T(8,128)S(1)}, u32[]{:S(2)}, u32[]{:S(2)}) collective-permute-start(f32[8,4,8]{2,0,1:T(8,128)S(1)} %get-tuple-element.212), channel_id=1, source_target_pairs={{15,0},{0,1},{1,2},{2,3},{3,4},{4,5},{5,6},{6,7},{7,8},{8,9},{9,10... | collective-permute-start | bytes 3080 | tf_op jit(solution)/shard_map/while/body/eval_jaxpr/ppermute | solution.py:19
  126.7 7.1 %collective-permute-start.4 = (f32[8,4,8,128]{3,2,0,1:T(8,128)S(1)}, f32[8,4,8,128]{3,2,0,1:T(8,128)S(1)}, u32[]{:S(2)}, u32[]{:S(2)}) collective-permute-start(f32[8,4,8,128]{3,2,0,1:T(8,128)S(1)} %get-tuple-element.214), channel_id=1, source_target_pairs={{15,0},{0,1},{1,2},{2,3},{3,4},{4,5},{5,6},{6,7},{7,8},{8,9},{9,10... | collective-permute-start | bytes 393224 | tf_op jit(solution)/shard_map/while/body/eval_jaxpr/ppermute | solution.py:19
  134.1 6.4 %collective-permute-start = (bf16[8,4096]{1,0:T(8,128)(2,1)S(1)}, bf16[8,4096]{1,0:T(8,128)(2,1)S(1)}, u32[]{:S(2)}, u32[]{:S(2)}) collective-permute-start(bf16[8,4096]{1,0:T(8,128)(2,1)S(1)} %get-tuple-element.210), channel_id=1, source_target_pairs={{15,0},{0,1},{1,2},{2,3},{3,4},{4,5},{5,6},{6,7},{7,8},{8,9},{9,10... | collective-permute-start | bytes 196616 | tf_op jit(solution)/shard_map/while/body/eval_jaxpr/ppermute | solution.py:19
  134.1 6.7 %collective-permute-start.1 = (f32[8,4,8]{2,0,1:T(8,128)S(1)}, f32[8,4,8]{2,0,1:T(8,128)S(1)}, u32[]{:S(2)}, u32[]{:S(2)}) collective-permute-start(f32[8,4,8]{2,0,1:T(8,128)S(1)} %get-tuple-element.211), channel_id=1, source_target_pairs={{15,0},{0,1},{1,2},{2,3},{3,4},{4,5},{5,6},{6,7},{7,8},{8,9},{9,10... | collective-permute-start | bytes 3080 | tf_op jit(solution)/shard_map/while/body/eval_jaxpr/ppermute | solution.py:19
  134.2 6.9 %collective-permute-start.3 = (f32[8,4,8]{2,0,1:T(8,128)S(1)}, f32[8,4,8]{2,0,1:T(8,128)S(1)}, u32[]{:S(2)}, u32[]{:S(2)}) collective-permute-start(f32[8,4,8]{2,0,1:T(8,128)S(1)} %get-tuple-element.212), channel_id=1, source_target_pairs={{15,0},{0,1},{1,2},{2,3},{3,4},{4,5},{5,6},{6,7},{7,8},{8,9},{9,10... | collective-permute-start | bytes 3080 | tf_op jit(solution)/shard_map/while/body/eval_jaxpr/ppermute | solution.py:19
  135.5 7.1 %collective-permute-start.4 = (f32[8,4,8,128]{3,2,0,1:T(8,128)S(1)}, f32[8,4,8,128]{3,2,0,1:T(8,128)S(1)}, u32[]{:S(2)}, u32[]{:S(2)}) collective-permute-start(f32[8,4,8,128]{3,2,0,1:T(8,128)S(1)} %get-tuple-element.214), channel_id=1, source_target_pairs={{15,0},{0,1},{1,2},{2,3},{3,4},{4,5},{5,6},{6,7},{7,8},{8,9},{9,10... | collective-permute-start | bytes 393224 | tf_op jit(solution)/shard_map/while/body/eval_jaxpr/ppermute | solution.py:19
  143.0 6.4 %collective-permute-start.5 = (bf16[8,4096]{1,0:T(8,128)(2,1)S(1)}, bf16[8,4096]{1,0:T(8,128)(2,1)S(1)}, u32[]{:S(2)}, u32[]{:S(2)}) collective-permute-start(bf16[8,4096]{1,0:T(8,128)(2,1)S(1)} %bitcast.45), channel_id=1, source_target_pairs={{15,0},{0,1},{1,2},{2,3},{3,4},{4,5},{5,6},{6,7},{7,8},{8,9},{9,10... | collective-permute-start | bytes 196616 | tf_op jit(solution)/shard_map/ppermute | solution.py:19
  (16 other events, 72.3 us)
where the time goes:
time: 150 us
  waiting for transfers between devices  103 us (69%)
  starting transfers between devices  27.3 us (18%)
  matrix products  8.34 us (6%)
  local copies, waits for them, and re-layouts  5.02 us (3%)
  other arithmetic  4.93 us (3%)
  loops' own time  1.5 us (1%)
    ppermute x76, waiting for transfers between devices, shifted(): return lax.ppermute(block, axis, route)  103 us
    ppermute x76, starting transfers between devices, shifted(): return lax.ppermute(block, axis, route)  27.3 us
    dot_general x16, matrix products, absorb_block(): jnp.einsum('rkgd,tkd->rkgt', q_heads, k_heads, preferred_element_type=jnp...  4.58 us
    dot_general x16, matrix products, absorb_block(): jnp.einsum('rkgt,tkd->rkgd', weights.astype(jnp.bfloat16), v_heads, prefe...  3.75 us
    unnamed x10, local copies, waits for them, and re-layouts  3.61 us
    reduce_sum x16, other arithmetic, absorb_block(): new_sum = run_sum * factor + jnp.sum(weights, axis=-1)  3.26 us
  transfers between devices with their start and end apart: 76, of which 47 were waited for; matrix products, arithmetic and copies ran while one was open for 6% of the time, Pallas kernels for 0%

commit v1 on v0

v1 whole, which is shorter than its diff:
```python
import functools
import math

import jax
import jax.numpy as jnp
from jax import lax
from jax.experimental import pallas as pl
from jax.experimental.pallas import tpu as pltpu
from jax.sharding import PartitionSpec as P

HEADS = 32
KV_HEADS = 4
GROUP = HEADS // KV_HEADS
HEAD_DIM = 128
WIDTH = HEADS * HEAD_DIM
KV_WIDTH = KV_HEADS * HEAD_DIM
LANES = 128
SHARE = 4
FAR = -(2.0**100)
EXP2_SCALE = math.log2(math.e) / math.sqrt(HEAD_DIM)


def swapped(block, distance):
    devices = lax.axis_size("blk")
    return lax.ppermute(block, "blk", [(i, i ^ distance) for i in range(devices)])


def partial_kernel(n_q, n_kv, *refs):
    q_refs, kv_refs, out_refs = refs[:n_q], refs[n_q : n_q + n_kv], refs[n_q + n_kv :]
    rows = q_refs[0].shape[0]
    tokens = kv_refs[0].shape[0] - 8
    lane = lax.broadcasted_iota(jnp.int32, (rows, LANES), 1)
    token_lane = lax.broadcasted_iota(jnp.int32, (tokens, LANES), 1).astype(jnp.float32)
    pick = jnp.where(
        lax.broadcasted_iota(jnp.int32, (8, LANES), 0) == 0, 1.0, 0.0
    ).astype(jnp.bfloat16)
    hides = []
    for ref in kv_refs:
        pages = ref[tokens:, :tokens]
        column = lax.dot_general(
            pages, pick, (((0,), (0,)), ((), ())), preferred_element_type=jnp.float32
        )
        hides.append(jnp.where(column > token_lane, FAR, 0.0).astype(jnp.bfloat16))
    ones = jnp.ones((tokens, LANES), jnp.bfloat16)
    stats = [[jnp.zeros((rows, LANES), jnp.float32)] * 3 for _ in range(n_q)]
    last = [ref[:, WIDTH:].astype(jnp.float32) for ref in q_refs]
    for kv in range(KV_HEADS):
        parts = []
        for i, ref in enumerate(q_refs):
            for g in range(GROUP):
                head = kv * GROUP + g
                q = ref[:, head * HEAD_DIM : (head + 1) * HEAD_DIM].astype(jnp.float32)
                parts.append(jnp.concatenate([q, last[i]], axis=1))
        q_all = jnp.concatenate(parts, axis=0).astype(jnp.bfloat16)
        scores = []
        for ref, hide in zip(kv_refs, hides):
            k = ref[:tokens, kv * HEAD_DIM : (kv + 1) * HEAD_DIM]
            scores.append(
                lax.dot_general(
                    q_all,
                    jnp.concatenate([k, hide], axis=1),
                    (((1,), (1,)), ((), ())),
                    preferred_element_type=jnp.float32,
                )
            )
        top = functools.reduce(
            jnp.maximum, [jnp.max(s, axis=1, keepdims=True) for s in scores]
        )
        top = top.astype(jnp.bfloat16).astype(jnp.float32)
        total = None
        for s, ref in zip(scores, kv_refs):
            weights = jnp.exp2((s - top) * EXP2_SCALE).astype(jnp.bfloat16)
            start = KV_WIDTH + kv * HEAD_DIM
            v = jnp.concatenate([ref[:tokens, start : start + HEAD_DIM], ones], axis=1)
            part = jnp.dot(weights, v, preferred_element_type=jnp.float32)
            total = part if total is None else total + part
        for i, ref in enumerate(out_refs):
            for g in range(GROUP):
                head = kv * GROUP + g
                at = slice((i * GROUP + g) * rows, (i * GROUP + g + 1) * rows)
                ref[:, head * HEAD_DIM : (head + 1) * HEAD_DIM] = total[
                    at, :HEAD_DIM
                ].astype(jnp.bfloat16)
                mass = total[at, HEAD_DIM:]
                high = mass.astype(jnp.bfloat16).astype(jnp.float32)
                here = lane == head
                stats[i][0] = jnp.where(here, top[at], stats[i][0])
                stats[i][1] = jnp.where(here, high, stats[i][1])
                stats[i][2] = jnp.where(here, mass - high, stats[i][2])
    for i, ref in enumerate(out_refs):
        for j in range(3):
            ref[:, WIDTH + j * LANES : WIDTH + (j + 1) * LANES] = stats[i][j].astype(
                jnp.bfloat16
            )


def partial_call(q_blocks, kv_blocks):
    n_q, n_kv = len(q_blocks), len(kv_blocks)
    rows = q_blocks[0].shape[0]
    vmem = pl.BlockSpec(memory_space=pltpu.VMEM)
    return pl.pallas_call(
        functools.partial(partial_kernel, n_q, n_kv),
        out_shape=[jax.ShapeDtypeStruct((rows, WIDTH + 3 * LANES), jnp.bfloat16)] * n_q,
        in_specs=[vmem] * (n_q + n_kv),
        out_specs=[vmem] * n_q,
    )(*q_blocks, *kv_blocks)


def merge_kernel(n, *refs):
    parts, out_ref = refs[:n], refs[n]
    tops, masses = [], []
    for ref in parts:
        stat = [
            ref[:, WIDTH + j * LANES : WIDTH + (j + 1) * LANES].astype(jnp.float32)
            for j in range(3)
        ]
        tops.append(stat[0])
        masses.append(stat[1] + stat[2])
    top = functools.reduce(jnp.maximum, tops)
    factors = [jnp.exp2((t - top) * EXP2_SCALE) for t in tops]
    total = functools.reduce(jnp.add, [f * m for f, m in zip(factors, masses)])
    shares = [f / total for f in factors]
    for head in range(HEADS):
        at = slice(head * HEAD_DIM, (head + 1) * HEAD_DIM)
        value = functools.reduce(
            jnp.add,
            [
                share[:, head : head + 1] * ref[:, at].astype(jnp.float32)
                for share, ref in zip(shares, parts)
            ],
        )
        out_ref[:, at] = value.astype(jnp.bfloat16)


def merge_call(parts):
    rows = parts[0].shape[0]
    vmem = pl.BlockSpec(memory_space=pltpu.VMEM)
    return pl.pallas_call(
        functools.partial(merge_kernel, len(parts)),
        out_shape=jax.ShapeDtypeStruct((rows, WIDTH), jnp.bfloat16),
        in_specs=[vmem] * len(parts),
        out_specs=vmem,
    )(*parts)


def shards(queries, key_cache, value_cache, tile_page, row_last):
    groups = lax.axis_size("blk") // SHARE
    rows, tokens = queries.shape[0], key_cache.shape[0]
    page_lane = lax.broadcasted_iota(jnp.int32, (rows, LANES), 1)
    seen = (page_lane == row_last[:, None]).astype(jnp.bfloat16)
    own_q = jnp.concatenate([queries, seen], axis=1)
    pages = jnp.pad(
        tile_page.astype(jnp.bfloat16)[None, :], ((0, 7), (0, 2 * KV_WIDTH - tokens))
    )
    own_kv = jnp.concatenate(
        [jnp.concatenate([key_cache, value_cache], axis=1), pages], axis=0
    )
    across = swapped(own_kv, 2)
    kv_blocks = [own_kv, swapped(own_kv, 1), across, swapped(across, 1)]
    q_blocks = [own_q] + [swapped(own_q, SHARE * d) for d in range(1, groups)]
    partials = []
    for start in range(0, groups, 4):
        partials += partial_call(q_blocks[start : start + 4], kv_blocks)
    parts = [partials[0]] + [
        swapped(partials[d], SHARE * d) for d in range(1, groups)
    ]
    return merge_call(parts)


def solution(mesh):
    placed = (
        P(("parts", "blk"), None),
        P(("parts", "blk"), None),
        P(("parts", "blk"), None),
        P(("parts", "blk")),
        P(("parts", "blk")),
    )
    return jax.shard_map(
        shards, mesh=mesh, in_specs=placed, out_specs=P(("parts", "blk"), None), check_vma=False
    )
```

time: 150 us -> 45.7 us (0.30)
  waiting for transfers between devices: 103 us -> 23.1 us
  starting transfers between devices: 27.3 us -> 12 us
  matrix products: 8.34 us -> 0 us
  Pallas kernels: 0 us -> 6.16 us
  other arithmetic: 4.93 us -> 1.87 us
  local copies, waits for them, and re-layouts: 5.02 us -> 2.28 us
  loops' own time: 1.5 us -> 0 us
    ppermute x76 -> x9, waiting for transfers between devices: 103 us -> 23.1 us  [swapped(): lax.ppermute(block, 'blk', [(i, i ^ distance) for i in range(devices)])]
    ppermute x76 -> x9, starting transfers between devices: 27.3 us -> 12 us  [swapped(): lax.ppermute(block, 'blk', [(i, i ^ distance) for i in range(devices)])]
    dot_general x32 -> x0, matrix products: 8.34 us -> none  [the longest x16 4.58 us: absorb_block(): jnp.einsum('rkgd,tkd->rkgt', q_heads, k_heads, preferred_element_type=jnp...]
    pallas_call x0 -> x2, Pallas kernels: none -> 6.16 us  [the longest x1 4.26 us: partial_call(): pl.pallas_call(functools.partial(partial_kernel, n_q, n_kv), out_shape=[j...]
    reduce_sum x16 -> x0, other arithmetic: 3.26 us -> none  [absorb_block(): new_sum = run_sum * factor + jnp.sum(weights, axis=-1)]
    another operation x1 -> x0, loops' own time: 1.5 us -> none  [shards(): final_pair = lax.fori_loop(0, blocks - 1, turn, (own_rows, carried))]
    unnamed x10 -> x26, local copies, waits for them, and re-layouts: 3.61 us -> 2.27 us
  transfers between devices with their start and end apart: 76 -> 9, of which waited for: 47 -> 5; matrix products, arithmetic and copies ran while one was open for 6% -> 0% of each run, Pallas kernels for 0% -> 0%
where the time goes in v1:
time: 45.7 us; the launch traced here: 45.5 us
  waiting for transfers between devices  23.1 us (51%)
  starting transfers between devices  12 us (26%)
  Pallas kernels  6.16 us (13%)
  local copies, waits for them, and re-layouts  2.28 us (5%)
  other arithmetic  1.87 us (4%)
    ppermute x9, waiting for transfers between devices, swapped(): lax.ppermute(block, 'blk', [(i, i ^ distance) for i in range(devices)])  23.1 us
    ppermute x9, starting transfers between devices, swapped(): lax.ppermute(block, 'blk', [(i, i ^ distance) for i in range(devices)])  12 us
    pallas_call x1, Pallas kernels, partial_call(): pl.pallas_call(functools.partial(partial_kernel, n_q, n_kv), out_shape=[j...  4.26 us
    unnamed x26, local copies, waits for them, and re-layouts  2.27 us
    pallas_call x1, Pallas kernels, merge_call(): pl.pallas_call(functools.partial(merge_kernel, len(parts)), out_shape=jax...  1.9 us
    concatenate x1, other arithmetic, shards(): jnp.concatenate([jnp.concatenate([key_cache, value_cache], axis=1), pages...  1.08 us
  transfers between devices with their start and end apart: 9, of which 5 were waited for; matrix products, arithmetic and copies ran while one was open for 0% of the time, Pallas kernels for 0%

profile of v1, /device:TPU:0, one launch (start us, length us, event | category | flops | bytes accessed | tf_op | source)
XLA Modules:
  0.0 45.5 jit_solution(4450039480652782561)
XLA Ops:
  0.0 0.0 copy-start.12
  0.0 0.0 copy-start.11
  0.0 0.7 %convert_element_type.9 = bf16[256]{0:T(256)(128)(2,1)S(1)} convert(s32[256]{0:T(256)} %param.8) | non-fusion elementwise | flops 256 | bytes 1536 | tf_op jit(solution)/shard_map/convert_element_type | solution.py:153
  0.7 1.1 %fusion.1.refs_4_ = bf16[264,1024]{1,0:T(8,128)(2,1)S(1)} fusion(bf16[1,256]{1,0:T(2,128)(2,1)S(1)} %broadcast_in_dim.4, bf16[256,512]{1,0:T(8,128)(2,1)} %param.7, bf16[256,512]{1,0:T(8,128)(2,1)} %param.6), kind=kLoop, calls=%fused_computation.2 | loop fusion | flops 2162688 | bytes 1065472 | tf_op jit(solution)/shard_map/concatenate | solution.py:155
  1.8 0.0 copy-start
  1.8 3.1 %collective-permute-start.4 = (bf16[264,1024]{1,0:T(8,128)(2,1)S(1)}, bf16[264,1024]{1,0:T(8,128)(2,1)S(1)}, u32[]{:S(2)}, u32[]{:S(2)}) collective-permute-start(bf16[264,1024]{1,0:T(8,128)(2,1)S(1)} %fusion.1.refs_4_), channel_id=1, source_target_pairs={{0,2},{1,3},{2,0},{3,1},{4,6},{5,7},{6,4},{7,5},{8,10},{9,11},{10,... | collective-permute-start | bytes 1622024 | tf_op jit(solution)/shard_map/ppermute | solution.py:25
  4.9 0.0 collective-permute-start.3
  4.9 0.0 copy-done.12
  4.9 0.1 fusion.2
  5.0 12.2 %collective-permute-done.4.refs_6_ = bf16[264,1024]{1,0:T(8,128)(2,1)S(1)} collective-permute-done((bf16[264,1024]{1,0:T(8,128)(2,1)S(1)}, bf16[264,1024]{1,0:T(8,128)(2,1)S(1)}, u32[]{:S(2)}, u32[]{:S(2)}) %collective-permute-start.4) | collective-permute-done | bytes 540704 | tf_op jit(solution)/shard_map/ppermute | solution.py:25
  17.2 0.0 copy-start.1
  17.2 0.0 collective-permute-start.5
  17.2 0.0 copy-done.11
  17.2 0.0 copy-start.4
  17.2 3.9 %collective-permute-start.2 = (bf16[8,4224]{1,0:T(8,128)(2,1)S(1)}, bf16[8,4224]{1,0:T(8,128)(2,1)S(1)}, u32[]{:S(2)}, u32[]{:S(2)}) collective-permute-start(bf16[8,4224]{1,0:T(8,128)(2,1)S(1)} %pad_maximum_fusion.refs_0_), channel_id=1, source_target_pairs={{0,12},{1,13},{2,14},{3,15},{4,8},{5,9},{6,10},{7,11},{8,4},{9,5},... | collective-permute-start | bytes 202760 | tf_op jit(solution)/shard_map/ppermute | solution.py:25
  21.1 0.0 collective-permute-start.1
  21.1 0.6 %collective-permute-start = (bf16[8,4224]{1,0:T(8,128)(2,1)S(1)}, bf16[8,4224]{1,0:T(8,128)(2,1)S(1)}, u32[]{:S(2)}, u32[]{:S(2)}) collective-permute-start(bf16[8,4224]{1,0:T(8,128)(2,1)S(1)} %pad_maximum_fusion.refs_0_), channel_id=1, source_target_pairs={{0,4},{1,5},{2,6},{3,7},{4,0},{5,1},{6,2},{7,3},{8,12},{9,13},{10,... | collective-permute-start | bytes 202760 | tf_op jit(solution)/shard_map/ppermute | solution.py:25
  21.7 2.4 %collective-permute-done.2.refs_3_ = bf16[8,4224]{1,0:T(8,128)(2,1)S(1)} collective-permute-done((bf16[8,4224]{1,0:T(8,128)(2,1)S(1)}, bf16[8,4224]{1,0:T(8,128)(2,1)S(1)}, u32[]{:S(2)}, u32[]{:S(2)}) %collective-permute-start.2) | collective-permute-done | bytes 67616 | tf_op jit(solution)/shard_map/ppermute | solution.py:25
  24.1 0.0 copy-start.8
  24.1 3.2 %collective-permute-done.1.refs_2_ = bf16[8,4224]{1,0:T(8,128)(2,1)S(1)} collective-permute-done((bf16[8,4224]{1,0:T(8,128)(2,1)S(1)}, bf16[8,4224]{1,0:T(8,128)(2,1)S(1)}, u32[]{:S(2)}, u32[]{:S(2)}) %collective-permute-start.1) | collective-permute-done | bytes 67616 | tf_op jit(solution)/shard_map/ppermute | solution.py:25
  27.4 0.0 copy-start.9
  27.4 0.0 collective-permute-done.refs_1_
  27.4 0.0 copy-start.10
  27.4 0.0 collective-permute-done.3.refs_5_
  27.4 0.0 copy-start.2
  27.4 0.0 collective-permute-done.5.refs_7_
  27.4 0.0 copy-done
  27.4 0.0 copy-done.1
  27.4 0.0 copy-done.4
  27.4 0.0 copy-done.8
  27.5 0.6 %copy-done.9 = bf16[8,4224]{1,0:T(8,128)(2,1)} copy-done((bf16[8,4224]{1,0:T(8,128)(2,1)}, bf16[8,4224]{1,0:T(8,128)(2,1)S(1)}, u32[]{:S(2)}) %copy-start.9) | copy-done | bytes 67608
  28.0 0.0 copy-done.10
  28.0 0.2 copy-done.2
  28.2 0.0 copy-start.3
  28.2 0.8 %copy-done.3 = bf16[264,1024]{1,0:T(8,128)(2,1)} copy-done((bf16[264,1024]{1,0:T(8,128)(2,1)}, bf16[264,1024]{1,0:T(8,128)(2,1)S(1)}, u32[]{:S(2)}) %copy-start.3) | copy-done | bytes 540696
  29.0 4.3 %shard_map.55 = (bf16[8,4480]{1,0:T(8,128)(2,1)}, bf16[8,4480]{1,0:T(8,128)(2,1)}, bf16[8,4480]{1,0:T(8,128)(2,1)}, bf16[8,4480]{1,0:T(8,128)(2,1)}) custom-call(bf16[8,4224]{1,0:T(8,128)(2,1)} %copy-done.4, bf16[8,4224]{1,0:T(8,128)(2,1)} %copy-done.10, bf16[8,4224]{1,0:T(8,128)(2,1)} %copy-done.9, bf16[8,4224]{1,0:T(8,128)(2,1)} %copy-done.8, ...), custom_call_target="tpu_custom_call" | custom-call | tf_op jit(solution)/shard_map/pallas_call | solution.py:101
  33.3 1.2 %collective-permute-start.6 = (bf16[8,4480]{1,0:T(8,128)(2,1)}, bf16[8,4480]{1,0:T(8,128)(2,1)S(1)}, u32[]{:S(2)}, u32[]{:S(2)}) collective-permute-start(bf16[8,4480]{1,0:T(8,128)(2,1)} %get-tuple-element.10), channel_id=1, source_target_pairs={{0,4},{1,5},{2,6},{3,7},{4,0},{5,1},{6,2},{7,3},{8,12},{9,13},{10,... | collective-permute-start | bytes 215048 | tf_op jit(solution)/shard_map/ppermute | solution.py:25
  34.5 1.9 %collective-permute-start.7 = (bf16[8,4480]{1,0:T(8,128)(2,1)}, bf16[8,4480]{1,0:T(8,128)(2,1)S(1)}, u32[]{:S(2)}, u32[]{:S(2)}) collective-permute-start(bf16[8,4480]{1,0:T(8,128)(2,1)} %get-tuple-element.11), channel_id=1, source_target_pairs={{0,8},{1,9},{2,10},{3,11},{4,12},{5,13},{6,14},{7,15},{8,0},{9,1},... | collective-permute-start | bytes 215048 | tf_op jit(solution)/shard_map/ppermute | solution.py:25
  36.3 1.3 %collective-permute-start.8 = (bf16[8,4480]{1,0:T(8,128)(2,1)}, bf16[8,4480]{1,0:T(8,128)(2,1)S(1)}, u32[]{:S(2)}, u32[]{:S(2)}) collective-permute-start(bf16[8,4480]{1,0:T(8,128)(2,1)} %get-tuple-element.12), channel_id=1, source_target_pairs={{0,12},{1,13},{2,14},{3,15},{4,8},{5,9},{6,10},{7,11},{8,4},{9,5},... | collective-permute-start | bytes 215048 | tf_op jit(solution)/shard_map/ppermute | solution.py:25
  37.7 0.8 %collective-permute-done.6.refs_1_ = bf16[8,4480]{1,0:T(8,128)(2,1)S(1)} collective-permute-done((bf16[8,4480]{1,0:T(8,128)(2,1)}, bf16[8,4480]{1,0:T(8,128)(2,1)S(1)}, u32[]{:S(2)}, u32[]{:S(2)}) %collective-permute-start.6) | collective-permute-done | bytes 71712 | tf_op jit(solution)/shard_map/ppermute | solution.py:25
  38.5 0.0 copy-start.5
  38.5 4.4 %collective-permute-done.7.refs_2_ = bf16[8,4480]{1,0:T(8,128)(2,1)S(1)} collective-permute-done((bf16[8,4480]{1,0:T(8,128)(2,1)}, bf16[8,4480]{1,0:T(8,128)(2,1)S(1)}, u32[]{:S(2)}, u32[]{:S(2)}) %collective-permute-start.7) | collective-permute-done | bytes 71712 | tf_op jit(solution)/shard_map/ppermute | solution.py:25
  42.9 0.0 copy-start.6
  42.9 0.0 collective-permute-done.8.refs_3_
  42.9 0.0 copy-start.7
  42.9 0.0 copy-done.5
  42.9 0.6 %copy-done.6 = bf16[8,4480]{1,0:T(8,128)(2,1)} copy-done((bf16[8,4480]{1,0:T(8,128)(2,1)}, bf16[8,4480]{1,0:T(8,128)(2,1)S(1)}, u32[]{:S(2)}) %copy-start.6) | copy-done | bytes 71704
  43.5 0.0 copy-done.7
  43.6 1.9 %shard_map.56 = bf16[8,4096]{1,0:T(8,128)(2,1)} custom-call(bf16[8,4480]{1,0:T(8,128)(2,1)} %get-tuple-element.9.refs_0_, bf16[8,4480]{1,0:T(8,128)(2,1)} %copy-done.5, bf16[8,4480]{1,0:T(8,128)(2,1)} %copy-done.6, bf16[8,4480]{1,0:T(8,128)(2,1)} %copy-done.7), custom_call_target="tpu_custom_call" | custom-call | tf_op jit(solution)/shard_map/pallas_call | solution.py:138
  (2 shorter events, 0.0 us)
Async XLA Ops:
  0.0 4.9 %copy-start.12 = (s32[8]{0:T(128)S(1)}, s32[8]{0:T(128)}, u32[]{:S(2)}) copy-start(s32[8]{0:T(128)} %param.9) | copy-start | bytes 100
  0.0 17.2 %copy-start.11 = (bf16[8,4096]{1,0:T(8,128)(2,1)S(1)}, bf16[8,4096]{1,0:T(8,128)(2,1)}, u32[]{:S(2)}) copy-start(bf16[8,4096]{1,0:T(8,128)(2,1)} %param.5) | copy-start | bytes 196612
  1.8 25.6 %copy-start = (bf16[264,1024]{1,0:T(8,128)(2,1)}, bf16[264,1024]{1,0:T(8,128)(2,1)S(1)}, u32[]{:S(2)}) copy-start(bf16[264,1024]{1,0:T(8,128)(2,1)S(1)} %fusion.1.refs_4_) | copy-start | bytes 1622020
  1.8 15.3 %collective-permute-start.4 = (bf16[264,1024]{1,0:T(8,128)(2,1)S(1)}, bf16[264,1024]{1,0:T(8,128)(2,1)S(1)}, u32[]{:S(2)}, u32[]{:S(2)}) collective-permute-start(bf16[264,1024]{1,0:T(8,128)(2,1)S(1)} %fusion.1.refs_4_), channel_id=1, source_target_pairs={{0,2},{1,3},{2,0},{3,1},{4,6},{5,7},{6,4},{7,5},{8,10},{9,11},{10,... | collective-permute-start | bytes 1622024 | tf_op jit(solution)/shard_map/ppermute | solution.py:25
  4.9 22.5 %collective-permute-start.3 = (bf16[264,1024]{1,0:T(8,128)(2,1)S(1)}, bf16[264,1024]{1,0:T(8,128)(2,1)S(1)}, u32[]{:S(2)}, u32[]{:S(2)}) collective-permute-start(bf16[264,1024]{1,0:T(8,128)(2,1)S(1)} %fusion.1.refs_4_), channel_id=1, source_target_pairs={{0,1},{1,0},{2,3},{3,2},{4,5},{5,4},{6,7},{7,6},{8,9},{9,8},{10,11... | collective-permute-start | bytes 1622024 | tf_op jit(solution)/shard_map/ppermute | solution.py:25
  17.2 10.3 %copy-start.1 = (bf16[264,1024]{1,0:T(8,128)(2,1)}, bf16[264,1024]{1,0:T(8,128)(2,1)S(1)}, u32[]{:S(2)}) copy-start(bf16[264,1024]{1,0:T(8,128)(2,1)S(1)} %collective-permute-done.4.refs_6_) | copy-start | bytes 1622020
  17.2 10.2 %collective-permute-start.5 = (bf16[264,1024]{1,0:T(8,128)(2,1)S(1)}, bf16[264,1024]{1,0:T(8,128)(2,1)S(1)}, u32[]{:S(2)}, u32[]{:S(2)}) collective-permute-start(bf16[264,1024]{1,0:T(8,128)(2,1)S(1)} %collective-permute-done.4.refs_6_), channel_id=1, source_target_pairs={{0,1},{1,0},{2,3},{3,2},{4,5},{5,4},{6,7},{7,6},{8,9},{9,8},{10,11... | collective-permute-start | bytes 1622024 | tf_op jit(solution)/shard_map/ppermute | solution.py:25
  17.2 10.3 %copy-start.4 = (bf16[8,4224]{1,0:T(8,128)(2,1)}, bf16[8,4224]{1,0:T(8,128)(2,1)S(1)}, u32[]{:S(2)}) copy-start(bf16[8,4224]{1,0:T(8,128)(2,1)S(1)} %pad_maximum_fusion.refs_0_) | copy-start | bytes 202756
  17.2 6.9 %collective-permute-start.2 = (bf16[8,4224]{1,0:T(8,128)(2,1)S(1)}, bf16[8,4224]{1,0:T(8,128)(2,1)S(1)}, u32[]{:S(2)}, u32[]{:S(2)}) collective-permute-start(bf16[8,4224]{1,0:T(8,128)(2,1)S(1)} %pad_maximum_fusion.refs_0_), channel_id=1, source_target_pairs={{0,12},{1,13},{2,14},{3,15},{4,8},{5,9},{6,10},{7,11},{8,4},{9,5},... | collective-permute-start | bytes 202760 | tf_op jit(solution)/shard_map/ppermute | solution.py:25
  21.1 6.3 %collective-permute-start.1 = (bf16[8,4224]{1,0:T(8,128)(2,1)S(1)}, bf16[8,4224]{1,0:T(8,128)(2,1)S(1)}, u32[]{:S(2)}, u32[]{:S(2)}) collective-permute-start(bf16[8,4224]{1,0:T(8,128)(2,1)S(1)} %pad_maximum_fusion.refs_0_), channel_id=1, source_target_pairs={{0,8},{1,9},{2,10},{3,11},{4,12},{5,13},{6,14},{7,15},{8,0},{9,1},... | collective-permute-start | bytes 202760 | tf_op jit(solution)/shard_map/ppermute | solution.py:25
  21.1 6.3 %collective-permute-start = (bf16[8,4224]{1,0:T(8,128)(2,1)S(1)}, bf16[8,4224]{1,0:T(8,128)(2,1)S(1)}, u32[]{:S(2)}, u32[]{:S(2)}) collective-permute-start(bf16[8,4224]{1,0:T(8,128)(2,1)S(1)} %pad_maximum_fusion.refs_0_), channel_id=1, source_target_pairs={{0,4},{1,5},{2,6},{3,7},{4,0},{5,1},{6,2},{7,3},{8,12},{9,13},{10,... | collective-permute-start | bytes 202760 | tf_op jit(solution)/shard_map/ppermute | solution.py:25
  24.1 3.3 %copy-start.8 = (bf16[8,4224]{1,0:T(8,128)(2,1)}, bf16[8,4224]{1,0:T(8,128)(2,1)S(1)}, u32[]{:S(2)}) copy-start(bf16[8,4224]{1,0:T(8,128)(2,1)S(1)} %collective-permute-done.2.refs_3_) | copy-start | bytes 202756
  27.4 0.6 %copy-start.9 = (bf16[8,4224]{1,0:T(8,128)(2,1)}, bf16[8,4224]{1,0:T(8,128)(2,1)S(1)}, u32[]{:S(2)}) copy-start(bf16[8,4224]{1,0:T(8,128)(2,1)S(1)} %collective-permute-done.1.refs_2_) | copy-start | bytes 202756
  27.4 0.7 %copy-start.10 = (bf16[8,4224]{1,0:T(8,128)(2,1)}, bf16[8,4224]{1,0:T(8,128)(2,1)S(1)}, u32[]{:S(2)}) copy-start(bf16[8,4224]{1,0:T(8,128)(2,1)S(1)} %collective-permute-done.refs_1_) | copy-start | bytes 202756
  27.4 0.8 %copy-start.2 = (bf16[264,1024]{1,0:T(8,128)(2,1)}, bf16[264,1024]{1,0:T(8,128)(2,1)S(1)}, u32[]{:S(2)}) copy-start(bf16[264,1024]{1,0:T(8,128)(2,1)S(1)} %collective-permute-done.3.refs_5_) | copy-start | bytes 1622020
  28.2 0.8 %copy-start.3 = (bf16[264,1024]{1,0:T(8,128)(2,1)}, bf16[264,1024]{1,0:T(8,128)(2,1)S(1)}, u32[]{:S(2)}) copy-start(bf16[264,1024]{1,0:T(8,128)(2,1)S(1)} %collective-permute-done.5.refs_7_) | copy-start | bytes 1622020
  33.3 5.2 %collective-permute-start.6 = (bf16[8,4480]{1,0:T(8,128)(2,1)}, bf16[8,4480]{1,0:T(8,128)(2,1)S(1)}, u32[]{:S(2)}, u32[]{:S(2)}) collective-permute-start(bf16[8,4480]{1,0:T(8,128)(2,1)} %get-tuple-element.10), channel_id=1, source_target_pairs={{0,4},{1,5},{2,6},{3,7},{4,0},{5,1},{6,2},{7,3},{8,12},{9,13},{10,... | collective-permute-start | bytes 215048 | tf_op jit(solution)/shard_map/ppermute | solution.py:25
  34.5 8.4 %collective-permute-start.7 = (bf16[8,4480]{1,0:T(8,128)(2,1)}, bf16[8,4480]{1,0:T(8,128)(2,1)S(1)}, u32[]{:S(2)}, u32[]{:S(2)}) collective-permute-start(bf16[8,4480]{1,0:T(8,128)(2,1)} %get-tuple-element.11), channel_id=1, source_target_pairs={{0,8},{1,9},{2,10},{3,11},{4,12},{5,13},{6,14},{7,15},{8,0},{9,1},... | collective-permute-start | bytes 215048 | tf_op jit(solution)/shard_map/ppermute | solution.py:25
  36.3 6.6 %collective-permute-start.8 = (bf16[8,4480]{1,0:T(8,128)(2,1)}, bf16[8,4480]{1,0:T(8,128)(2,1)S(1)}, u32[]{:S(2)}, u32[]{:S(2)}) collective-permute-start(bf16[8,4480]{1,0:T(8,128)(2,1)} %get-tuple-element.12), channel_id=1, source_target_pairs={{0,12},{1,13},{2,14},{3,15},{4,8},{5,9},{6,10},{7,11},{8,4},{9,5},... | collective-permute-start | bytes 215048 | tf_op jit(solution)/shard_map/ppermute | solution.py:25
  38.5 4.5 %copy-start.5 = (bf16[8,4480]{1,0:T(8,128)(2,1)}, bf16[8,4480]{1,0:T(8,128)(2,1)S(1)}, u32[]{:S(2)}) copy-start(bf16[8,4480]{1,0:T(8,128)(2,1)S(1)} %collective-permute-done.6.refs_1_) | copy-start | bytes 215044
  42.9 0.6 %copy-start.6 = (bf16[8,4480]{1,0:T(8,128)(2,1)}, bf16[8,4480]{1,0:T(8,128)(2,1)S(1)}, u32[]{:S(2)}) copy-start(bf16[8,4480]{1,0:T(8,128)(2,1)S(1)} %collective-permute-done.7.refs_2_) | copy-start | bytes 215044
  42.9 0.7 %copy-start.7 = (bf16[8,4480]{1,0:T(8,128)(2,1)}, bf16[8,4480]{1,0:T(8,128)(2,1)S(1)}, u32[]{:S(2)}) copy-start(bf16[8,4480]{1,0:T(8,128)(2,1)S(1)} %collective-permute-done.8.refs_3_) | copy-start | bytes 215044

commit v2 on v1

v2 whole, which is shorter than its diff:
```python
import functools
import math

import jax
import jax.numpy as jnp
from jax import lax
from jax.experimental import pallas as pl
from jax.experimental.pallas import tpu as pltpu
from jax.sharding import PartitionSpec as P


HEADS = 32
KV_HEADS = 4
GROUP = HEADS // KV_HEADS
HEAD_DIM = 128
WIDTH = HEADS * HEAD_DIM
LANES = 128
SHARE = 4
FAR = -(2.0**100)
EXP2_SCALE = math.log2(math.e) / math.sqrt(HEAD_DIM)


def swapped(block, distance):
    devices = lax.axis_size("blk")
    return lax.ppermute(block, "blk", [(i, i ^ distance) for i in range(devices)])


def weights_kernel(n_q, n_kv, *refs):
    q_refs, k_refs = refs[:n_q], refs[n_q : n_q + n_kv]
    page_refs = refs[n_q + n_kv : n_q + 2 * n_kv]
    weight_ref, top_ref = refs[n_q + 2 * n_kv :]
    rows, tokens = q_refs[0].shape[0], k_refs[0].shape[0]
    lane = lax.broadcasted_iota(jnp.int32, (rows, LANES), 1)
    token_lane = lax.broadcasted_iota(jnp.int32, (tokens, LANES), 1).astype(jnp.float32)
    pick = jnp.where(
        lax.broadcasted_iota(jnp.int32, (8, LANES), 0) == 0, 1.0, 0.0
    ).astype(jnp.bfloat16)
    hides = []
    for ref in page_refs:
        pages = jnp.broadcast_to(ref[...], (8, tokens)).astype(jnp.float32)
        column = lax.dot_general(
            pages.astype(jnp.bfloat16),
            pick,
            (((0,), (0,)), ((), ())),
            preferred_element_type=jnp.float32,
        )
        hides.append(jnp.where(column > token_lane, FAR, 0.0).astype(jnp.bfloat16))
    tops = [jnp.zeros((rows, LANES), jnp.float32)] * n_q
    last = [ref[:, WIDTH:].astype(jnp.float32) for ref in q_refs]
    count = n_q * GROUP * rows
    for kv in range(KV_HEADS):
        parts = []
        for i, ref in enumerate(q_refs):
            for g in range(GROUP):
                head = kv * GROUP + g
                q = ref[:, head * HEAD_DIM : (head + 1) * HEAD_DIM].astype(jnp.float32)
                parts.append(jnp.concatenate([q, last[i]], axis=1))
        q_all = jnp.concatenate(parts, axis=0).astype(jnp.bfloat16)
        scores = []
        for ref, hide in zip(k_refs, hides):
            k = ref[:, kv * HEAD_DIM : (kv + 1) * HEAD_DIM]
            scores.append(
                lax.dot_general(
                    q_all,
                    jnp.concatenate([k, hide], axis=1),
                    (((1,), (1,)), ((), ())),
                    preferred_element_type=jnp.float32,
                )
            )
        top = functools.reduce(
            jnp.maximum, [jnp.max(s, axis=1, keepdims=True) for s in scores]
        )
        top = top.astype(jnp.bfloat16).astype(jnp.float32)
        for j, s in enumerate(scores):
            weight_ref[
                kv * count : (kv + 1) * count, j * tokens : (j + 1) * tokens
            ] = jnp.exp2((s - top) * EXP2_SCALE).astype(jnp.bfloat16)
        for i in range(n_q):
            for g in range(GROUP):
                at = slice((i * GROUP + g) * rows, (i * GROUP + g + 1) * rows)
                tops[i] = jnp.where(lane == kv * GROUP + g, top[at], tops[i])
    for i in range(n_q):
        top_ref[i * rows : (i + 1) * rows, :] = tops[i]


def values_kernel(n_q, n_kv, *refs):
    weight_ref, top_ref = refs[:2]
    v_refs, out_refs = refs[2 : 2 + n_kv], refs[2 + n_kv :]
    rows, tokens = out_refs[0].shape[0], v_refs[0].shape[0]
    count = n_q * GROUP * rows
    lane = lax.broadcasted_iota(jnp.int32, (rows, LANES), 1)
    ones = jnp.ones((tokens, LANES), jnp.bfloat16)
    stats = [[jnp.zeros((rows, LANES), jnp.float32)] * 2 for _ in range(n_q)]
    for kv in range(KV_HEADS):
        total = None
        for j, ref in enumerate(v_refs):
            weights = weight_ref[
                kv * count : (kv + 1) * count, j * tokens : (j + 1) * tokens
            ]
            v = jnp.concatenate(
                [ref[:, kv * HEAD_DIM : (kv + 1) * HEAD_DIM], ones], axis=1
            )
            part = jnp.dot(weights, v, preferred_element_type=jnp.float32)
            total = part if total is None else total + part
        for i, ref in enumerate(out_refs):
            for g in range(GROUP):
                head = kv * GROUP + g
                at = slice((i * GROUP + g) * rows, (i * GROUP + g + 1) * rows)
                ref[:, head * HEAD_DIM : (head + 1) * HEAD_DIM] = total[
                    at, :HEAD_DIM
                ].astype(jnp.bfloat16)
                mass = total[at, HEAD_DIM:]
                high = mass.astype(jnp.bfloat16).astype(jnp.float32)
                here = lane == head
                stats[i][0] = jnp.where(here, high, stats[i][0])
                stats[i][1] = jnp.where(here, mass - high, stats[i][1])
    for i, ref in enumerate(out_refs):
        columns = [top_ref[i * rows : (i + 1) * rows, :], *stats[i]]
        for j, column in enumerate(columns):
            ref[:, WIDTH + j * LANES : WIDTH + (j + 1) * LANES] = column.astype(
                jnp.bfloat16
            )


VMEM_BLOCK = pl.BlockSpec(memory_space=pltpu.VMEM)


def weights_call(q_blocks, k_blocks, page_blocks):
    n_q, n_kv = len(q_blocks), len(k_blocks)
    rows, tokens = q_blocks[0].shape[0], k_blocks[0].shape[0]
    return pl.pallas_call(
        functools.partial(weights_kernel, n_q, n_kv),
        out_shape=[
            jax.ShapeDtypeStruct((n_q * HEADS * rows, n_kv * tokens), jnp.bfloat16),
            jax.ShapeDtypeStruct((n_q * rows, LANES), jnp.float32),
        ],
        in_specs=[VMEM_BLOCK] * (n_q + 2 * n_kv),
        out_specs=[VMEM_BLOCK] * 2,
        compiler_params=pltpu.CompilerParams(vmem_limit_bytes=24 << 20),
    )(*q_blocks, *k_blocks, *page_blocks)


def values_call(weights, tops, v_blocks, n_q):
    n_kv = len(v_blocks)
    rows = tops.shape[0] // n_q
    return pl.pallas_call(
        functools.partial(values_kernel, n_q, n_kv),
        out_shape=[jax.ShapeDtypeStruct((rows, WIDTH + 3 * LANES), jnp.bfloat16)] * n_q,
        in_specs=[VMEM_BLOCK] * (2 + n_kv),
        out_specs=[VMEM_BLOCK] * n_q,
        compiler_params=pltpu.CompilerParams(vmem_limit_bytes=24 << 20),
    )(weights, tops, *v_blocks)


def merge_kernel(n, *refs):
    parts, out_ref = refs[:n], refs[n]
    tops, masses = [], []
    for ref in parts:
        stat = [
            ref[:, WIDTH + j * LANES : WIDTH + (j + 1) * LANES].astype(jnp.float32)
            for j in range(3)
        ]
        tops.append(stat[0])
        masses.append(stat[1] + stat[2])
    top = functools.reduce(jnp.maximum, tops)
    factors = [jnp.exp2((t - top) * EXP2_SCALE) for t in tops]
    total = functools.reduce(jnp.add, [f * m for f, m in zip(factors, masses)])
    shares = [f / total for f in factors]
    for head in range(HEADS):
        at = slice(head * HEAD_DIM, (head + 1) * HEAD_DIM)
        value = functools.reduce(
            jnp.add,
            [
                share[:, head : head + 1] * ref[:, at].astype(jnp.float32)
                for share, ref in zip(shares, parts)
            ],
        )
        out_ref[:, at] = value.astype(jnp.bfloat16)


def merge_call(parts):
    rows = parts[0].shape[0]
    return pl.pallas_call(
        functools.partial(merge_kernel, len(parts)),
        out_shape=jax.ShapeDtypeStruct((rows, WIDTH), jnp.bfloat16),
        in_specs=[VMEM_BLOCK] * len(parts),
        out_specs=VMEM_BLOCK,
        compiler_params=pltpu.CompilerParams(vmem_limit_bytes=8 << 20),
    )(*parts)


def pooled(block):
    across = swapped(block, 2)
    beside = swapped(block, 1)
    return [block, beside, across, swapped(across, 1)]


def attend(queries, key_cache, value_cache, tile_page, row_last):
    groups = lax.axis_size("blk") // SHARE
    rows = queries.shape[0]
    page_lane = lax.broadcasted_iota(jnp.int32, (rows, LANES), 1)
    seen = (page_lane == row_last[:, None]).astype(jnp.bfloat16)
    own_q = jnp.concatenate([queries, seen], axis=1)
    k_blocks = pooled(key_cache)
    v_blocks = pooled(value_cache)
    page_blocks = pooled(tile_page.reshape(1, -1))
    q_blocks = [own_q] + [swapped(own_q, SHARE * d) for d in range(1, groups)]
    partials = []
    for start in range(0, groups, 4):
        some = q_blocks[start : start + 4]
        weights, tops = weights_call(some, k_blocks, page_blocks)
        partials += values_call(weights, tops, v_blocks, len(some))
    parts = [partials[0]] + [swapped(partials[d], SHARE * d) for d in range(1, groups)]
    return merge_call(parts)


def solution(mesh):
    placed = (
        P(("parts", "blk"), None),
        P(("parts", "blk"), None),
        P(("parts", "blk"), None),
        P(("parts", "blk")),
        P(("parts", "blk")),
    )
    return jax.shard_map(
        attend, mesh=mesh, in_specs=placed, out_specs=P(("parts", "blk"), None), check_vma=False
    )
```

time: 45.7 us -> 50.1 us (1.096)
  starting transfers between devices: 12 us -> 20.4 us
  Pallas kernels: 6.16 us -> 3.05 us
  waiting for transfers between devices: 23.1 us -> 22.2 us
    ppermute x9 -> x15, starting transfers between devices: 12 us -> 20.4 us  [swapped(): lax.ppermute(block, 'blk', [(i, i ^ distance) for i in range(devices)])]
    pallas_call x1 -> x2, Pallas kernels: 4.26 us -> 2.13 us  [the longest x1 1.41 us: weights_call(): pl.pallas_call(functools.partial(weights_kernel, n_q, n_kv), out_shape=[j...]
    pallas_call x1, Pallas kernels: 1.9 us -> 0.91 us  [merge_call(): pl.pallas_call(functools.partial(merge_kernel, len(parts)), out_shape=jax...]
    ppermute x9 -> x15, waiting for transfers between devices: 23.1 us -> 22.2 us  [swapped(): lax.ppermute(block, 'blk', [(i, i ^ distance) for i in range(devices)])]
    unnamed x26 -> x6, local copies, waits for them, and re-layouts: 2.27 us -> 2.57 us
    concatenate x2 -> x1, other arithmetic: 1.09 us -> 0.84 us  [attend(): own_q = jnp.concatenate([queries, seen], axis=1)]
  transfers between devices with their start and end apart: 9 -> 15, of which waited for: 5 -> 6; matrix products, arithmetic and copies ran while one was open for 0% -> 3% of each run, Pallas kernels for 0% -> 3%
where the time goes in v2:
time: 50.1 us; the launch traced here: 49.9 us
  waiting for transfers between devices  22.2 us (44%)
  starting transfers between devices  20.4 us (41%)
  Pallas kernels  3.05 us (6%)
  local copies, waits for them, and re-layouts  2.57 us (5%)
  other arithmetic  1.57 us (3%)
    ppermute x15, waiting for transfers between devices, swapped(): lax.ppermute(block, 'blk', [(i, i ^ distance) for i in range(devices)])  22.2 us
    ppermute x15, starting transfers between devices, swapped(): lax.ppermute(block, 'blk', [(i, i ^ distance) for i in range(devices)])  20.4 us
    unnamed x6, local copies, waits for them, and re-layouts  2.57 us
    pallas_call x1, Pallas kernels, weights_call(): pl.pallas_call(functools.partial(weights_kernel, n_q, n_kv), out_shape=[j...  1.41 us
  transfers between devices with their start and end apart: 15, of which 6 were waited for; matrix products, arithmetic and copies ran while one was open for 3% of the time, Pallas kernels for 3%

profile of v2, /device:TPU:0, one launch (start us, length us, event | category | flops | bytes accessed | tf_op | source)
XLA Modules:
  0.0 49.9 jit_solution(9734534291487975921)
XLA Ops:
  0.0 3.0 %collective-permute-start.4 = (bf16[256,512]{1,0:T(8,128)(2,1)}, bf16[256,512]{1,0:T(8,128)(2,1)S(1)}, u32[]{:S(2)}, u32[]{:S(2)}) collective-permute-start(bf16[256,512]{1,0:T(8,128)(2,1)} %refs_4_.1), channel_id=1, source_target_pairs={{0,2},{1,3},{2,0},{3,1},{4,6},{5,7},{6,4},{7,5},{8,10},{9,11},{10,... | collective-permute-start | bytes 786440 | tf_op jit(solution)/shard_map/ppermute | solution.py:25
  3.0 0.0 collective-permute-start.10
  3.0 2.0 %collective-permute-start.7 = (s32[1,256]{1,0:T(1,128)}, s32[1,256]{1,0:T(1,128)S(1)}, u32[]{:S(2)}, u32[]{:S(2)}) collective-permute-start(s32[1,256]{1,0:T(1,128)} %bitcast.1), channel_id=1, source_target_pairs={{0,2},{1,3},{2,0},{3,1},{4,6},{5,7},{6,4},{7,5},{8,10},{9,11},{10,... | collective-permute-start | bytes 3080 | tf_op jit(solution)/shard_map/ppermute | solution.py:25
  5.0 0.0 collective-permute-start.6
  5.0 0.5 %collective-permute-start.3 = (bf16[256,512]{1,0:T(8,128)(2,1)}, bf16[256,512]{1,0:T(8,128)(2,1)S(1)}, u32[]{:S(2)}, u32[]{:S(2)}) collective-permute-start(bf16[256,512]{1,0:T(8,128)(2,1)} %refs_4_.1), channel_id=1, source_target_pairs={{0,1},{1,0},{2,3},{3,2},{4,5},{5,4},{6,7},{7,6},{8,9},{9,8},{10,11... | collective-permute-start | bytes 786440 | tf_op jit(solution)/shard_map/ppermute | solution.py:25
  5.5 0.7 %fusion = bf16[8,128]{1,0:T(8,128)(2,1)S(1)} fusion(s32[8]{0:T(128)} %param.9), kind=kLoop, calls=%fused_computation.2 | loop fusion | flops 2048 | bytes 2080 | tf_op jit(solution)/shard_map/convert_element_type | solution.py:202
  6.3 8.9 %collective-permute-done.7.refs_10_ = s32[1,256]{1,0:T(1,128)S(1)} collective-permute-done((s32[1,256]{1,0:T(1,128)}, s32[1,256]{1,0:T(1,128)S(1)}, u32[]{:S(2)}, u32[]{:S(2)}) %collective-permute-start.7) | collective-permute-done | bytes 1056 | tf_op jit(solution)/shard_map/ppermute | solution.py:25
  15.2 0.0 collective-permute-start.9
  15.2 0.0 collective-permute-done.6.refs_9_
  15.2 0.5 %collective-permute-start.8 = (s32[1,256]{1,0:T(1,128)S(1)}, s32[1,256]{1,0:T(1,128)S(1)}, u32[]{:S(2)}, u32[]{:S(2)}) collective-permute-start(s32[1,256]{1,0:T(1,128)S(1)} %collective-permute-done.7.refs_10_), channel_id=1, source_target_pairs={{0,1},{1,0},{2,3},{3,2},{4,5},{5,4},{6,7},{7,6},{8,9},{9,8},{10,11... | collective-permute-start | bytes 3080 | tf_op jit(solution)/shard_map/ppermute | solution.py:25
  15.7 0.0 collective-permute-done.4.refs_6_
  15.7 0.1 collective-permute-start.5
  15.8 0.0 collective-permute-done.10.refs_4_
  15.8 0.4 collective-permute-start.11
  16.2 0.8 %pad_maximum_fusion.refs_0_ = bf16[8,4224]{1,0:T(8,128)(2,1)S(1)} fusion(bf16[8,128]{1,0:T(8,128)(2,1)S(1)} %fusion, bf16[8,4096]{1,0:T(8,128)(2,1)} %param.5), kind=kLoop, calls=%fused_computation | loop fusion | flops 135168 | bytes 135168 | tf_op jit(solution)/shard_map/concatenate | solution.py:203
  17.1 0.0 collective-permute-done.8.refs_11_
  17.1 1.9 %collective-permute-start = (bf16[8,4224]{1,0:T(8,128)(2,1)S(1)}, bf16[8,4224]{1,0:T(8,128)(2,1)S(1)}, u32[]{:S(2)}, u32[]{:S(2)}) collective-permute-start(bf16[8,4224]{1,0:T(8,128)(2,1)S(1)} %pad_maximum_fusion.refs_0_), channel_id=1, source_target_pairs={{0,4},{1,5},{2,6},{3,7},{4,0},{5,1},{6,2},{7,3},{8,12},{9,13},{10,... | collective-permute-start | bytes 202760 | tf_op jit(solution)/shard_map/ppermute | solution.py:25
  18.9 2.5 %collective-permute-done.refs_1_ = bf16[8,4224]{1,0:T(8,128)(2,1)S(1)} collective-permute-done((bf16[8,4224]{1,0:T(8,128)(2,1)S(1)}, bf16[8,4224]{1,0:T(8,128)(2,1)S(1)}, u32[]{:S(2)}, u32[]{:S(2)}) %collective-permute-start) | collective-permute-done | bytes 67616 | tf_op jit(solution)/shard_map/ppermute | solution.py:25
  21.4 2.8 %collective-permute-start.1 = (bf16[8,4224]{1,0:T(8,128)(2,1)S(1)}, bf16[8,4224]{1,0:T(8,128)(2,1)S(1)}, u32[]{:S(2)}, u32[]{:S(2)}) collective-permute-start(bf16[8,4224]{1,0:T(8,128)(2,1)S(1)} %pad_maximum_fusion.refs_0_), channel_id=1, source_target_pairs={{0,8},{1,9},{2,10},{3,11},{4,12},{5,13},{6,14},{7,15},{8,0},{9,1},... | collective-permute-start | bytes 202760 | tf_op jit(solution)/shard_map/ppermute | solution.py:25
  24.2 2.4 %collective-permute-done.1.refs_2_ = bf16[8,4224]{1,0:T(8,128)(2,1)S(1)} collective-permute-done((bf16[8,4224]{1,0:T(8,128)(2,1)S(1)}, bf16[8,4224]{1,0:T(8,128)(2,1)S(1)}, u32[]{:S(2)}, u32[]{:S(2)}) %collective-permute-start.1) | collective-permute-done | bytes 67616 | tf_op jit(solution)/shard_map/ppermute | solution.py:25
  26.6 4.7 %collective-permute-start.2 = (bf16[8,4224]{1,0:T(8,128)(2,1)S(1)}, bf16[8,4224]{1,0:T(8,128)(2,1)S(1)}, u32[]{:S(2)}, u32[]{:S(2)}) collective-permute-start(bf16[8,4224]{1,0:T(8,128)(2,1)S(1)} %pad_maximum_fusion.refs_0_), channel_id=1, source_target_pairs={{0,12},{1,13},{2,14},{3,15},{4,8},{5,9},{6,10},{7,11},{8,4},{9,5},... | collective-permute-start | bytes 202760 | tf_op jit(solution)/shard_map/ppermute | solution.py:25
  31.3 2.3 %collective-permute-done.2.refs_3_ = bf16[8,4224]{1,0:T(8,128)(2,1)S(1)} collective-permute-done((bf16[8,4224]{1,0:T(8,128)(2,1)S(1)}, bf16[8,4224]{1,0:T(8,128)(2,1)S(1)}, u32[]{:S(2)}, u32[]{:S(2)}) %collective-permute-start.2) | collective-permute-done | bytes 67616 | tf_op jit(solution)/shard_map/ppermute | solution.py:25
  33.6 0.0 collective-permute-done.3.refs_5_
  33.6 0.0 collective-permute-done.5.refs_7_
  33.6 0.0 copy-start
  33.6 0.9 %copy-done = bf16[256,512]{1,0:T(8,128)(2,1)S(1)} copy-done((bf16[256,512]{1,0:T(8,128)(2,1)S(1)}, bf16[256,512]{1,0:T(8,128)(2,1)}, u32[]{:S(2)}) %copy-start) | copy-done | bytes 262168
  34.6 0.0 copy-start.2
  34.6 0.7 %copy-done.2 = s32[256]{0:T(256)S(1)} copy-done((s32[256]{0:T(256)S(1)}, s32[256]{0:T(256)}, u32[]{:S(2)}) %copy-start.2) | copy-done | bytes 1048
  35.2 1.4 %shard_map.55 = (bf16[1024,1024]{1,0:T(8,128)(2,1)S(1)}, f32[32,128]{1,0:T(8,128)S(1)}) custom-call(bf16[8,4224]{1,0:T(8,128)(2,1)S(1)} %pad_maximum_fusion.refs_0_, bf16[8,4224]{1,0:T(8,128)(2,1)S(1)} %collective-permute-done.refs_1_, bf16[8,4224]{1,0:T(8,128)(2,1)S(1)} %collective-permute-done.1.refs_2_, ...), custom_call_target="tpu_custom_call" | custom-call | tf_op jit(solution)/shard_map/pallas_call | solution.py:131
  36.7 0.0 collective-permute-done.9.refs_3_
  36.7 0.0 collective-permute-done.11.refs_5_
  36.7 0.0 copy-start.1
  36.7 0.9 %copy-done.1 = bf16[256,512]{1,0:T(8,128)(2,1)S(1)} copy-done((bf16[256,512]{1,0:T(8,128)(2,1)S(1)}, bf16[256,512]{1,0:T(8,128)(2,1)}, u32[]{:S(2)}) %copy-start.1) | copy-done | bytes 262168
  37.6 0.7 %shard_map.56 = (bf16[8,4480]{1,0:T(8,128)(2,1)S(1)}, bf16[8,4480]{1,0:T(8,128)(2,1)S(1)}, bf16[8,4480]{1,0:T(8,128)(2,1)S(1)}, bf16[8,4480]{1,0:T(8,128)(2,1)S(1)}) custom-call(bf16[1024,1024]{1,0:T(8,128)(2,1)S(1)} %get-tuple-element.11.refs_0_, f32[32,128]{1,0:T(8,128)S(1)} %get-tuple-element.12.refs_1_, bf16[256,512]{1,0:T(8,128)(2,1)S(1)} %copy-done.1, ...), custom_call_target="tpu_custom_call" | custom-call | tf_op jit(solution)/shard_map/pallas_call | solution.py:146
  38.4 0.1 collective-permute-start.12
  38.4 4.4 %collective-permute-start.13 = (bf16[8,4480]{1,0:T(8,128)(2,1)S(1)}, bf16[8,4480]{1,0:T(8,128)(2,1)S(1)}, u32[]{:S(2)}, u32[]{:S(2)}) collective-permute-start(bf16[8,4480]{1,0:T(8,128)(2,1)S(1)} %get-tuple-element.15), channel_id=1, source_target_pairs={{0,8},{1,9},{2,10},{3,11},{4,12},{5,13},{6,14},{7,15},{8,0},{9,1},... | collective-permute-start | bytes 215048 | tf_op jit(solution)/shard_map/ppermute | solution.py:25
  42.8 0.0 collective-permute-start.14
  42.8 0.0 collective-permute-done.12.refs_1_
  42.8 3.1 %collective-permute-done.13.refs_2_ = bf16[8,4480]{1,0:T(8,128)(2,1)S(1)} collective-permute-done((bf16[8,4480]{1,0:T(8,128)(2,1)S(1)}, bf16[8,4480]{1,0:T(8,128)(2,1)S(1)}, u32[]{:S(2)}, u32[]{:S(2)}) %collective-permute-start.13) | collective-permute-done | bytes 71712 | tf_op jit(solution)/shard_map/ppermute | solution.py:25
  45.9 3.1 %collective-permute-done.14.refs_3_ = bf16[8,4480]{1,0:T(8,128)(2,1)S(1)} collective-permute-done((bf16[8,4480]{1,0:T(8,128)(2,1)S(1)}, bf16[8,4480]{1,0:T(8,128)(2,1)S(1)}, u32[]{:S(2)}, u32[]{:S(2)}) %collective-permute-start.14) | collective-permute-done | bytes 71712 | tf_op jit(solution)/shard_map/ppermute | solution.py:25
  48.9 0.9 %shard_map.57 = bf16[8,4096]{1,0:T(8,128)(2,1)} custom-call(bf16[8,4480]{1,0:T(8,128)(2,1)S(1)} %get-tuple-element.13.refs_0_, bf16[8,4480]{1,0:T(8,128)(2,1)S(1)} %collective-permute-done.12.refs_1_, bf16[8,4480]{1,0:T(8,128)(2,1)S(1)} %collective-permute-done.13.refs_2_, bf16[8,4480]{1,0:T(8,128)(2,1)S(1)} %collective-permute-done.14.refs_3_), custom_call_target="tpu_custom_call" | custom-call | tf_op jit(solution)/shard_map/pallas_call | solution.py:183
Async XLA Ops:
  0.0 15.7 %collective-permute-start.4 = (bf16[256,512]{1,0:T(8,128)(2,1)}, bf16[256,512]{1,0:T(8,128)(2,1)S(1)}, u32[]{:S(2)}, u32[]{:S(2)}) collective-permute-start(bf16[256,512]{1,0:T(8,128)(2,1)} %refs_4_.1), channel_id=1, source_target_pairs={{0,2},{1,3},{2,0},{3,1},{4,6},{5,7},{6,4},{7,5},{8,10},{9,11},{10,... | collective-permute-start | bytes 786440 | tf_op jit(solution)/shard_map/ppermute | solution.py:25
  3.0 12.8 %collective-permute-start.10 = (bf16[256,512]{1,0:T(8,128)(2,1)}, bf16[256,512]{1,0:T(8,128)(2,1)S(1)}, u32[]{:S(2)}, u32[]{:S(2)}) collective-permute-start(bf16[256,512]{1,0:T(8,128)(2,1)} %refs_2_.1), channel_id=1, source_target_pairs={{0,2},{1,3},{2,0},{3,1},{4,6},{5,7},{6,4},{7,5},{8,10},{9,11},{10,... | collective-permute-start | bytes 786440 | tf_op jit(solution)/shard_map/ppermute | solution.py:25
  3.0 12.2 %collective-permute-start.7 = (s32[1,256]{1,0:T(1,128)}, s32[1,256]{1,0:T(1,128)S(1)}, u32[]{:S(2)}, u32[]{:S(2)}) collective-permute-start(s32[1,256]{1,0:T(1,128)} %bitcast.1), channel_id=1, source_target_pairs={{0,2},{1,3},{2,0},{3,1},{4,6},{5,7},{6,4},{7,5},{8,10},{9,11},{10,... | collective-permute-start | bytes 3080 | tf_op jit(solution)/shard_map/ppermute | solution.py:25
  5.0 10.2 %collective-permute-start.6 = (s32[1,256]{1,0:T(1,128)}, s32[1,256]{1,0:T(1,128)S(1)}, u32[]{:S(2)}, u32[]{:S(2)}) collective-permute-start(s32[1,256]{1,0:T(1,128)} %bitcast.2), channel_id=1, source_target_pairs={{0,1},{1,0},{2,3},{3,2},{4,5},{5,4},{6,7},{7,6},{8,9},{9,8},{10,11... | collective-permute-start | bytes 3080 | tf_op jit(solution)/shard_map/ppermute | solution.py:25
  5.0 28.6 %collective-permute-start.3 = (bf16[256,512]{1,0:T(8,128)(2,1)}, bf16[256,512]{1,0:T(8,128)(2,1)S(1)}, u32[]{:S(2)}, u32[]{:S(2)}) collective-permute-start(bf16[256,512]{1,0:T(8,128)(2,1)} %refs_4_.1), channel_id=1, source_target_pairs={{0,1},{1,0},{2,3},{3,2},{4,5},{5,4},{6,7},{7,6},{8,9},{9,8},{10,11... | collective-permute-start | bytes 786440 | tf_op jit(solution)/shard_map/ppermute | solution.py:25
  15.2 21.5 %collective-permute-start.9 = (bf16[256,512]{1,0:T(8,128)(2,1)}, bf16[256,512]{1,0:T(8,128)(2,1)S(1)}, u32[]{:S(2)}, u32[]{:S(2)}) collective-permute-start(bf16[256,512]{1,0:T(8,128)(2,1)} %refs_2_.1), channel_id=1, source_target_pairs={{0,1},{1,0},{2,3},{3,2},{4,5},{5,4},{6,7},{7,6},{8,9},{9,8},{10,11... | collective-permute-start | bytes 786440 | tf_op jit(solution)/shard_map/ppermute | solution.py:25
  15.2 1.9 %collective-permute-start.8 = (s32[1,256]{1,0:T(1,128)S(1)}, s32[1,256]{1,0:T(1,128)S(1)}, u32[]{:S(2)}, u32[]{:S(2)}) collective-permute-start(s32[1,256]{1,0:T(1,128)S(1)} %collective-permute-done.7.refs_10_), channel_id=1, source_target_pairs={{0,1},{1,0},{2,3},{3,2},{4,5},{5,4},{6,7},{7,6},{8,9},{9,8},{10,11... | collective-permute-start | bytes 3080 | tf_op jit(solution)/shard_map/ppermute | solution.py:25
  15.7 17.9 %collective-permute-start.5 = (bf16[256,512]{1,0:T(8,128)(2,1)S(1)}, bf16[256,512]{1,0:T(8,128)(2,1)S(1)}, u32[]{:S(2)}, u32[]{:S(2)}) collective-permute-start(bf16[256,512]{1,0:T(8,128)(2,1)S(1)} %collective-permute-done.4.refs_6_), channel_id=1, source_target_pairs={{0,1},{1,0},{2,3},{3,2},{4,5},{5,4},{6,7},{7,6},{8,9},{9,8},{10,11... | collective-permute-start | bytes 786440 | tf_op jit(solution)/shard_map/ppermute | solution.py:25
  15.8 20.9 %collective-permute-start.11 = (bf16[256,512]{1,0:T(8,128)(2,1)S(1)}, bf16[256,512]{1,0:T(8,128)(2,1)S(1)}, u32[]{:S(2)}, u32[]{:S(2)}) collective-permute-start(bf16[256,512]{1,0:T(8,128)(2,1)S(1)} %collective-permute-done.10.refs_4_), channel_id=1, source_target_pairs={{0,1},{1,0},{2,3},{3,2},{4,5},{5,4},{6,7},{7,6},{8,9},{9,8},{10,11... | collective-permute-start | bytes 786440 | tf_op jit(solution)/shard_map/ppermute | solution.py:25
  17.1 4.3 %collective-permute-start = (bf16[8,4224]{1,0:T(8,128)(2,1)S(1)}, bf16[8,4224]{1,0:T(8,128)(2,1)S(1)}, u32[]{:S(2)}, u32[]{:S(2)}) collective-permute-start(bf16[8,4224]{1,0:T(8,128)(2,1)S(1)} %pad_maximum_fusion.refs_0_), channel_id=1, source_target_pairs={{0,4},{1,5},{2,6},{3,7},{4,0},{5,1},{6,2},{7,3},{8,12},{9,13},{10,... | collective-permute-start | bytes 202760 | tf_op jit(solution)/shard_map/ppermute | solution.py:25
  21.4 5.2 %collective-permute-start.1 = (bf16[8,4224]{1,0:T(8,128)(2,1)S(1)}, bf16[8,4224]{1,0:T(8,128)(2,1)S(1)}, u32[]{:S(2)}, u32[]{:S(2)}) collective-permute-start(bf16[8,4224]{1,0:T(8,128)(2,1)S(1)} %pad_maximum_fusion.refs_0_), channel_id=1, source_target_pairs={{0,8},{1,9},{2,10},{3,11},{4,12},{5,13},{6,14},{7,15},{8,0},{9,1},... | collective-permute-start | bytes 202760 | tf_op jit(solution)/shard_map/ppermute | solution.py:25
  26.6 7.0 %collective-permute-start.2 = (bf16[8,4224]{1,0:T(8,128)(2,1)S(1)}, bf16[8,4224]{1,0:T(8,128)(2,1)S(1)}, u32[]{:S(2)}, u32[]{:S(2)}) collective-permute-start(bf16[8,4224]{1,0:T(8,128)(2,1)S(1)} %pad_maximum_fusion.refs_0_), channel_id=1, source_target_pairs={{0,12},{1,13},{2,14},{3,15},{4,8},{5,9},{6,10},{7,11},{8,4},{9,5},... | collective-permute-start | bytes 202760 | tf_op jit(solution)/shard_map/ppermute | solution.py:25
  33.6 1.0 %copy-start = (bf16[256,512]{1,0:T(8,128)(2,1)S(1)}, bf16[256,512]{1,0:T(8,128)(2,1)}, u32[]{:S(2)}) copy-start(bf16[256,512]{1,0:T(8,128)(2,1)} %refs_4_.1) | copy-start | bytes 786436
  34.6 0.7 %copy-start.2 = (s32[256]{0:T(256)S(1)}, s32[256]{0:T(256)}, u32[]{:S(2)}) copy-start(s32[256]{0:T(256)} %param.8) | copy-start | bytes 3076
  36.7 1.0 %copy-start.1 = (bf16[256,512]{1,0:T(8,128)(2,1)S(1)}, bf16[256,512]{1,0:T(8,128)(2,1)}, u32[]{:S(2)}) copy-start(bf16[256,512]{1,0:T(8,128)(2,1)} %refs_2_.1) | copy-start | bytes 786436
  38.4 4.5 %collective-permute-start.12 = (bf16[8,4480]{1,0:T(8,128)(2,1)S(1)}, bf16[8,4480]{1,0:T(8,128)(2,1)S(1)}, u32[]{:S(2)}, u32[]{:S(2)}) collective-permute-start(bf16[8,4480]{1,0:T(8,128)(2,1)S(1)} %get-tuple-element.14), channel_id=1, source_target_pairs={{0,4},{1,5},{2,6},{3,7},{4,0},{5,1},{6,2},{7,3},{8,12},{9,13},{10,... | collective-permute-start | bytes 215048 | tf_op jit(solution)/shard_map/ppermute | solution.py:25
  38.4 7.4 %collective-permute-start.13 = (bf16[8,4480]{1,0:T(8,128)(2,1)S(1)}, bf16[8,4480]{1,0:T(8,128)(2,1)S(1)}, u32[]{:S(2)}, u32[]{:S(2)}) collective-permute-start(bf16[8,4480]{1,0:T(8,128)(2,1)S(1)} %get-tuple-element.15), channel_id=1, source_target_pairs={{0,8},{1,9},{2,10},{3,11},{4,12},{5,13},{6,14},{7,15},{8,0},{9,1},... | collective-permute-start | bytes 215048 | tf_op jit(solution)/shard_map/ppermute | solution.py:25
  42.8 6.1 %collective-permute-start.14 = (bf16[8,4480]{1,0:T(8,128)(2,1)S(1)}, bf16[8,4480]{1,0:T(8,128)(2,1)S(1)}, u32[]{:S(2)}, u32[]{:S(2)}) collective-permute-start(bf16[8,4480]{1,0:T(8,128)(2,1)S(1)} %get-tuple-element.16), channel_id=1, source_target_pairs={{0,12},{1,13},{2,14},{3,15},{4,8},{5,9},{6,10},{7,11},{8,4},{9,5},... | collective-permute-start | bytes 215048 | tf_op jit(solution)/shard_map/ppermute | solution.py:25

commit v3 on v2

--- a/solution.py
+++ b/solution.py
@@ -14,6 +14,7 @@
 GROUP = HEADS // KV_HEADS
 HEAD_DIM = 128
 WIDTH = HEADS * HEAD_DIM
+KV_WIDTH = KV_HEADS * HEAD_DIM
 LANES = 128
 SHARE = 4
 FAR = -(2.0**100)
@@ -25,21 +26,78 @@
     return lax.ppermute(block, "blk", [(i, i ^ distance) for i in range(devices)])
 
 
+VMEM_BLOCK = pl.BlockSpec(memory_space=pltpu.VMEM)
+
+
+HBM_BLOCK = pl.BlockSpec(memory_space=pltpu.MemorySpace.HBM)
+
+
+def in_hbm(array):
+    return pltpu.with_memory_space_constraint(array, pltpu.MemorySpace.HBM)
+
+
+def stage_kernel(
+    q_ref, k_ref, v_ref, page_ref, last_ref, q_out, k_out, v_out, page, last, sems
+):
+    rows, tokens = q_ref.shape[0], k_ref.shape[0]
+    moves = (
+        (last_ref, last),
+        (page_ref, page),
+        (q_ref, q_out.at[:, :WIDTH]),
+        (k_ref, k_out.at[:tokens, :]),
+        (v_ref, v_out),
+    )
+    copies = [pltpu.make_async_copy(s, d, sems.at[i]) for i, (s, d) in enumerate(moves)]
+    for copy in copies:
+        copy.start()
+    row = lax.broadcasted_iota(jnp.int32, (rows, LANES), 0)
+    lane = lax.broadcasted_iota(jnp.int32, (rows, LANES), 1)
+    copies[0].wait()
+    seen = functools.reduce(
+        jnp.logical_or, [(row == r) & (lane == last[r]) for r in range(rows)]
+    )
+    q_out[:, WIDTH:] = jnp.where(seen, 1.0, 0.0).astype(jnp.bfloat16)
+    copies[1].wait()
+    filled = jnp.broadcast_to(page[...], (8, tokens)).astype(jnp.float32)
+    k_out[tokens:, :tokens] = filled.astype(jnp.bfloat16)
+    k_out[tokens:, tokens:] = jnp.zeros((8, k_out.shape[1] - tokens), jnp.bfloat16)
+    for copy in copies[2:]:
+        copy.wait()
+
+
+def stage_call(row_last, queries, key_cache, value_cache, pages):
+    rows, tokens = queries.shape[0], key_cache.shape[0]
+    return pl.pallas_call(
+        stage_kernel,
+        out_shape=[
+            jax.ShapeDtypeStruct((rows, WIDTH + LANES), jnp.bfloat16),
+            jax.ShapeDtypeStruct((tokens + 8, KV_WIDTH), jnp.bfloat16),
+            jax.ShapeDtypeStruct(value_cache.shape, jnp.bfloat16),
+        ],
+        in_specs=[HBM_BLOCK] * 5,
+        out_specs=[VMEM_BLOCK] * 3,
+        scratch_shapes=[
+            pltpu.VMEM((1, tokens), jnp.int32),
+            pltpu.SMEM((rows,), jnp.int32),
+            pltpu.SemaphoreType.DMA((5,)),
+        ],
+        compiler_params=pltpu.CompilerParams(vmem_limit_bytes=8 << 20),
+    )(*map(in_hbm, (queries, key_cache, value_cache, pages, row_last)))
+
+
 def weights_kernel(n_q, n_kv, *refs):
     q_refs, k_refs = refs[:n_q], refs[n_q : n_q + n_kv]
-    page_refs = refs[n_q + n_kv : n_q + 2 * n_kv]
-    weight_ref, top_ref = refs[n_q + 2 * n_kv :]
-    rows, tokens = q_refs[0].shape[0], k_refs[0].shape[0]
+    weight_ref, top_ref = refs[n_q + n_kv :]
+    rows, tokens = q_refs[0].shape[0], k_refs[0].shape[0] - 8
     lane = lax.broadcasted_iota(jnp.int32, (rows, LANES), 1)
     token_lane = lax.broadcasted_iota(jnp.int32, (tokens, LANES), 1).astype(jnp.float32)
     pick = jnp.where(
         lax.broadcasted_iota(jnp.int32, (8, LANES), 0) == 0, 1.0, 0.0
     ).astype(jnp.bfloat16)
     hides = []
-    for ref in page_refs:
-        pages = jnp.broadcast_to(ref[...], (8, tokens)).astype(jnp.float32)
+    for ref in k_refs:
         column = lax.dot_general(
-            pages.astype(jnp.bfloat16),
+            ref[tokens:, :tokens],
             pick,
             (((0,), (0,)), ((), ())),
             preferred_element_type=jnp.float32,
@@ -58,7 +116,7 @@
         q_all = jnp.concatenate(parts, axis=0).astype(jnp.bfloat16)
         scores = []
         for ref, hide in zip(k_refs, hides):
-            k = ref[:, kv * HEAD_DIM : (kv + 1) * HEAD_DIM]
+            k = ref[:tokens, kv * HEAD_DIM : (kv + 1) * HEAD_DIM]
             scores.append(
                 lax.dot_general(
                     q_all,
@@ -90,7 +148,7 @@
     count = n_q * GROUP * rows
     lane = lax.broadcasted_iota(jnp.int32, (rows, LANES), 1)
     ones = jnp.ones((tokens, LANES), jnp.bfloat16)
-    stats = [[jnp.zeros((rows, LANES), jnp.float32)] * 2 for _ in range(n_q)]
+    stats = [top_ref[i * rows : (i + 1) * rows, :] for i in range(n_q)]
     for kv in range(KV_HEADS):
         total = None
         for j, ref in enumerate(v_refs):
@@ -111,33 +169,25 @@
                 ].astype(jnp.bfloat16)
                 mass = total[at, HEAD_DIM:]
                 high = mass.astype(jnp.bfloat16).astype(jnp.float32)
-                here = lane == head
-                stats[i][0] = jnp.where(here, high, stats[i][0])
-                stats[i][1] = jnp.where(here, mass - high, stats[i][1])
-    for i, ref in enumerate(out_refs):
-        columns = [top_ref[i * rows : (i + 1) * rows, :], *stats[i]]
-        for j, column in enumerate(columns):
-            ref[:, WIDTH + j * LANES : WIDTH + (j + 1) * LANES] = column.astype(
-                jnp.bfloat16
-            )
-
-
-VMEM_BLOCK = pl.BlockSpec(memory_space=pltpu.VMEM)
-
-
-def weights_call(q_blocks, k_blocks, page_blocks):
+                stats[i] = jnp.where(lane == HEADS + head, high, stats[i])
+                stats[i] = jnp.where(lane == 2 * HEADS + head, mass - high, stats[i])
+    for stat, ref in zip(stats, out_refs):
+        ref[:, WIDTH:] = stat.astype(jnp.bfloat16)
+
+
+def weights_call(q_blocks, k_blocks):
     n_q, n_kv = len(q_blocks), len(k_blocks)
-    rows, tokens = q_blocks[0].shape[0], k_blocks[0].shape[0]
+    rows, tokens = q_blocks[0].shape[0], k_blocks[0].shape[0] - 8
     return pl.pallas_call(
         functools.partial(weights_kernel, n_q, n_kv),
         out_shape=[
             jax.ShapeDtypeStruct((n_q * HEADS * rows, n_kv * tokens), jnp.bfloat16),
             jax.ShapeDtypeStruct((n_q * rows, LANES), jnp.float32),
         ],
-        in_specs=[VMEM_BLOCK] * (n_q + 2 * n_kv),
+        in_specs=[VMEM_BLOCK] * (n_q + n_kv),
         out_specs=[VMEM_BLOCK] * 2,
         compiler_params=pltpu.CompilerParams(vmem_limit_bytes=24 << 20),
-    )(*q_blocks, *k_blocks, *page_blocks)
+    )(*q_blocks, *k_blocks)
 
 
 def values_call(weights, tops, v_blocks, n_q):
@@ -145,7 +195,7 @@
     rows = tops.shape[0] // n_q
     return pl.pallas_call(
         functools.partial(values_kernel, n_q, n_kv),
-        out_shape=[jax.ShapeDtypeStruct((rows, WIDTH + 3 * LANES), jnp.bfloat16)] * n_q,
+        out_shape=[jax.ShapeDtypeStruct((rows, WIDTH + LANES), jnp.bfloat16)] * n_q,
         in_specs=[VMEM_BLOCK] * (2 + n_kv),
         out_specs=[VMEM_BLOCK] * n_q,
         compiler_params=pltpu.CompilerParams(vmem_limit_bytes=24 << 20),
@@ -156,12 +206,11 @@
     parts, out_ref = refs[:n], refs[n]
     tops, masses = [], []
     for ref in parts:
-        stat = [
-            ref[:, WIDTH + j * LANES : WIDTH + (j + 1) * LANES].astype(jnp.float32)
-            for j in range(3)
-        ]
-        tops.append(stat[0])
-        masses.append(stat[1] + stat[2])
+        stat = ref[:, WIDTH:].astype(jnp.float32)
+        tops.append(stat)
+        masses.append(
+            pltpu.roll(stat, LANES - HEADS, 1) + pltpu.roll(stat, LANES - 2 * HEADS, 1)
+        )
     top = functools.reduce(jnp.maximum, tops)
     factors = [jnp.exp2((t - top) * EXP2_SCALE) for t in tops]
     total = functools.reduce(jnp.add, [f * m for f, m in zip(factors, masses)])
@@ -189,26 +238,23 @@
     )(*parts)
 
 
-def pooled(block):
+def pooled(block, own):
     across = swapped(block, 2)
     beside = swapped(block, 1)
-    return [block, beside, across, swapped(across, 1)]
+    return [own, beside, across, swapped(across, 1)]
 
 
 def attend(queries, key_cache, value_cache, tile_page, row_last):
     groups = lax.axis_size("blk") // SHARE
-    rows = queries.shape[0]
-    page_lane = lax.broadcasted_iota(jnp.int32, (rows, LANES), 1)
-    seen = (page_lane == row_last[:, None]).astype(jnp.bfloat16)
-    own_q = jnp.concatenate([queries, seen], axis=1)
-    k_blocks = pooled(key_cache)
-    v_blocks = pooled(value_cache)
-    page_blocks = pooled(tile_page.reshape(1, -1))
+    pages = tile_page.reshape(1, -1)
+    own_q, own_k, own_v = stage_call(row_last, queries, key_cache, value_cache, pages)
+    k_blocks = pooled(own_k, own_k)
+    v_blocks = pooled(value_cache, own_v)
     q_blocks = [own_q] + [swapped(own_q, SHARE * d) for d in range(1, groups)]
     partials = []
     for start in range(0, groups, 4):
         some = q_blocks[start : start + 4]
-        weights, tops = weights_call(some, k_blocks, page_blocks)
+        weights, tops = weights_call(some, k_blocks)
         partials += values_call(weights, tops, v_blocks, len(some))
     parts = [partials[0]] + [swapped(partials[d], SHARE * d) for d in range(1, groups)]
     return merge_call(parts)

time: 50.1 us -> 44.5 us (0.89)
  starting transfers between devices: 20.4 us -> 15.2 us
  waiting for transfers between devices: 22.2 us -> 24.8 us
  local copies, waits for them, and re-layouts: 2.57 us -> 0 us
  other arithmetic: 1.57 us -> 0 us
  Pallas kernels: 3.05 us -> 4.22 us
    ppermute x15 -> x12, starting transfers between devices: 20.4 us -> 15.2 us  [swapped(): lax.ppermute(block, 'blk', [(i, i ^ distance) for i in range(devices)])]
    ppermute x15 -> x12, waiting for transfers between devices: 22.2 us -> 24.8 us  [swapped(): lax.ppermute(block, 'blk', [(i, i ^ distance) for i in range(devices)])]
    unnamed x6 -> x0, local copies, waits for them, and re-layouts: 2.57 us -> none
    pallas_call x0 -> x1, Pallas kernels: none -> 1.13 us  [stage_call(): pl.pallas_call(stage_kernel, out_shape=[jax.ShapeDtypeStruct((rows, WIDTH...]
    concatenate x1 -> x0, other arithmetic: 0.84 us -> none  [attend(): own_q = jnp.concatenate([queries, seen], axis=1)]
    convert_element_type x1 -> x0, other arithmetic: 0.73 us -> none  [attend(): seen = (page_lane == row_last[:, None]).astype(jnp.bfloat16)]
  transfers between devices with their start and end apart: 15 -> 12, of which waited for: 6 -> 8; matrix products, arithmetic and copies ran while one was open for 3% -> 0% of each run, Pallas kernels for 3% -> 3%
where the time goes in v3:
time: 44.5 us; the launch traced here: 44.3 us
  waiting for transfers between devices  24.8 us (56%)
  starting transfers between devices  15.2 us (34%)
  Pallas kernels  4.22 us (9%)
    ppermute x12, waiting for transfers between devices, swapped(): lax.ppermute(block, 'blk', [(i, i ^ distance) for i in range(devices)])  24.8 us
    ppermute x12, starting transfers between devices, swapped(): lax.ppermute(block, 'blk', [(i, i ^ distance) for i in range(devices)])  15.2 us
    pallas_call x1, Pallas kernels, weights_call(): pl.pallas_call(functools.partial(weights_kernel, n_q, n_kv), out_shape=[j...  1.4 us
    pallas_call x1, Pallas kernels, stage_call(): pl.pallas_call(stage_kernel, out_shape=[jax.ShapeDtypeStruct((rows, WIDTH...  1.13 us
    pallas_call x1, Pallas kernels, merge_call(): pl.pallas_call(functools.partial(merge_kernel, len(parts)), out_shape=jax...  0.97 us
  transfers between devices with their start and end apart: 12, of which 8 were waited for; matrix products, arithmetic and copies ran while one was open for 0% of the time, Pallas kernels for 3%

profile of v3, /device:TPU:0, one launch (start us, length us, event | category | flops | bytes accessed | tf_op | source)
XLA Modules:
  0.0 44.3 jit_solution(376313126183459619)
XLA Ops:
  0.0 1.1 %shard_map.55 = (bf16[8,4224]{1,0:T(8,128)(2,1)S(1)}, bf16[264,512]{1,0:T(8,128)(2,1)S(1)}, bf16[256,512]{1,0:T(8,128)(2,1)S(1)}) custom-call(bf16[8,4096]{1,0:T(8,128)(2,1)} %q_ref.1, bf16[256,512]{1,0:T(8,128)(2,1)} %k_ref.1, bf16[256,512]{1,0:T(8,128)(2,1)} %v_ref.1, s32[1,256]{1,0:T(1,128)} %bitcast.1, s32[8]{0:T(128)} %last_ref.1), custom_call_target="tpu_custom_call" | custom-call | tf_op jit(solution)/shard_map/pallas_call | solution.py:70
  1.1 3.1 %collective-permute-start.4 = (bf16[264,512]{1,0:T(8,128)(2,1)S(1)}, bf16[264,512]{1,0:T(8,128)(2,1)S(1)}, u32[]{:S(2)}, u32[]{:S(2)}) collective-permute-start(bf16[264,512]{1,0:T(8,128)(2,1)S(1)} %get-tuple-element.15.refs_4_), channel_id=1, source_target_pairs={{0,2},{1,3},{2,0},{3,1},{4,6},{5,7},{6,4},{7,5},{8,10},{9,11},{10,... | collective-permute-start | bytes 811016 | tf_op jit(solution)/shard_map/ppermute | solution.py:26
  4.2 0.1 collective-permute-start.7
  4.3 0.0 collective-permute-start.3
  4.3 7.2 %collective-permute-done.4.refs_6_ = bf16[264,512]{1,0:T(8,128)(2,1)S(1)} collective-permute-done((bf16[264,512]{1,0:T(8,128)(2,1)S(1)}, bf16[264,512]{1,0:T(8,128)(2,1)S(1)}, u32[]{:S(2)}, u32[]{:S(2)}) %collective-permute-start.4) | collective-permute-done | bytes 270368 | tf_op jit(solution)/shard_map/ppermute | solution.py:26
  11.5 0.0 collective-permute-start.5
  11.5 0.5 %collective-permute-start.6 = (bf16[256,512]{1,0:T(8,128)(2,1)}, bf16[256,512]{1,0:T(8,128)(2,1)S(1)}, u32[]{:S(2)}, u32[]{:S(2)}) collective-permute-start(bf16[256,512]{1,0:T(8,128)(2,1)} %v_ref.1), channel_id=1, source_target_pairs={{0,1},{1,0},{2,3},{3,2},{4,5},{5,4},{6,7},{7,6},{8,9},{9,8},{10,11... | collective-permute-start | bytes 786440 | tf_op jit(solution)/shard_map/ppermute | solution.py:26
  12.0 4.3 %collective-permute-done.7.refs_4_ = bf16[256,512]{1,0:T(8,128)(2,1)S(1)} collective-permute-done((bf16[256,512]{1,0:T(8,128)(2,1)}, bf16[256,512]{1,0:T(8,128)(2,1)S(1)}, u32[]{:S(2)}, u32[]{:S(2)}) %collective-permute-start.7) | collective-permute-done | bytes 262176 | tf_op jit(solution)/shard_map/ppermute | solution.py:26
  16.3 0.0 collective-permute-start.8
  16.3 1.8 %collective-permute-start = (bf16[8,4224]{1,0:T(8,128)(2,1)S(1)}, bf16[8,4224]{1,0:T(8,128)(2,1)S(1)}, u32[]{:S(2)}, u32[]{:S(2)}) collective-permute-start(bf16[8,4224]{1,0:T(8,128)(2,1)S(1)} %get-tuple-element.14.refs_0_), channel_id=1, source_target_pairs={{0,4},{1,5},{2,6},{3,7},{4,0},{5,1},{6,2},{7,3},{8,12},{9,13},{10,... | collective-permute-start | bytes 202760 | tf_op jit(solution)/shard_map/ppermute | solution.py:26
  18.1 2.8 %collective-permute-done.refs_1_ = bf16[8,4224]{1,0:T(8,128)(2,1)S(1)} collective-permute-done((bf16[8,4224]{1,0:T(8,128)(2,1)S(1)}, bf16[8,4224]{1,0:T(8,128)(2,1)S(1)}, u32[]{:S(2)}, u32[]{:S(2)}) %collective-permute-start) | collective-permute-done | bytes 67616 | tf_op jit(solution)/shard_map/ppermute | solution.py:26
  20.9 2.8 %collective-permute-start.1 = (bf16[8,4224]{1,0:T(8,128)(2,1)S(1)}, bf16[8,4224]{1,0:T(8,128)(2,1)S(1)}, u32[]{:S(2)}, u32[]{:S(2)}) collective-permute-start(bf16[8,4224]{1,0:T(8,128)(2,1)S(1)} %get-tuple-element.14.refs_0_), channel_id=1, source_target_pairs={{0,8},{1,9},{2,10},{3,11},{4,12},{5,13},{6,14},{7,15},{8,0},{9,1},... | collective-permute-start | bytes 202760 | tf_op jit(solution)/shard_map/ppermute | solution.py:26
  23.7 3.7 %collective-permute-done.1.refs_2_ = bf16[8,4224]{1,0:T(8,128)(2,1)S(1)} collective-permute-done((bf16[8,4224]{1,0:T(8,128)(2,1)S(1)}, bf16[8,4224]{1,0:T(8,128)(2,1)S(1)}, u32[]{:S(2)}, u32[]{:S(2)}) %collective-permute-start.1) | collective-permute-done | bytes 67616 | tf_op jit(solution)/shard_map/ppermute | solution.py:26
  27.4 3.2 %collective-permute-start.2 = (bf16[8,4224]{1,0:T(8,128)(2,1)S(1)}, bf16[8,4224]{1,0:T(8,128)(2,1)S(1)}, u32[]{:S(2)}, u32[]{:S(2)}) collective-permute-start(bf16[8,4224]{1,0:T(8,128)(2,1)S(1)} %get-tuple-element.14.refs_0_), channel_id=1, source_target_pairs={{0,12},{1,13},{2,14},{3,15},{4,8},{5,9},{6,10},{7,11},{8,4},{9,5},... | collective-permute-start | bytes 202760 | tf_op jit(solution)/shard_map/ppermute | solution.py:26
  30.6 2.9 %collective-permute-done.2.refs_3_ = bf16[8,4224]{1,0:T(8,128)(2,1)S(1)} collective-permute-done((bf16[8,4224]{1,0:T(8,128)(2,1)S(1)}, bf16[8,4224]{1,0:T(8,128)(2,1)S(1)}, u32[]{:S(2)}, u32[]{:S(2)}) %collective-permute-start.2) | collective-permute-done | bytes 67616 | tf_op jit(solution)/shard_map/ppermute | solution.py:26
  33.5 0.0 collective-permute-done.3.refs_5_
  33.5 0.0 collective-permute-done.5.refs_7_
  33.5 1.4 %shard_map.56 = (bf16[1024,1024]{1,0:T(8,128)(2,1)S(1)}, f32[32,128]{1,0:T(8,128)S(1)}) custom-call(bf16[8,4224]{1,0:T(8,128)(2,1)S(1)} %get-tuple-element.14.refs_0_, bf16[8,4224]{1,0:T(8,128)(2,1)S(1)} %collective-permute-done.refs_1_, bf16[8,4224]{1,0:T(8,128)(2,1)S(1)} %collective-permute-done.1.refs_2_, ...), custom_call_target="tpu_custom_call" | custom-call | tf_op jit(solution)/shard_map/pallas_call | solution.py:181
  34.9 0.0 collective-permute-done.6.refs_3_
  34.9 0.0 collective-permute-done.8.refs_5_
  34.9 0.7 %shard_map.57 = (bf16[8,4224]{1,0:T(8,128)(2,1)S(1)}, bf16[8,4224]{1,0:T(8,128)(2,1)S(1)}, bf16[8,4224]{1,0:T(8,128)(2,1)S(1)}, bf16[8,4224]{1,0:T(8,128)(2,1)S(1)}) custom-call(bf16[1024,1024]{1,0:T(8,128)(2,1)S(1)} %get-tuple-element.16.refs_0_, f32[32,128]{1,0:T(8,128)S(1)} %get-tuple-element.17.refs_1_, bf16[256,512]{1,0:T(8,128)(2,1)S(1)} %get-tuple-element.18.refs_2_, ...), custom_call_target="tpu_custom_call" | custom-call | tf_op jit(solution)/shard_map/pallas_call | solution.py:196
  35.6 0.1 collective-permute-start.10
  35.7 3.3 %collective-permute-start.11 = (bf16[8,4224]{1,0:T(8,128)(2,1)S(1)}, bf16[8,4224]{1,0:T(8,128)(2,1)S(1)}, u32[]{:S(2)}, u32[]{:S(2)}) collective-permute-start(bf16[8,4224]{1,0:T(8,128)(2,1)S(1)} %get-tuple-element.22), channel_id=1, source_target_pairs={{0,12},{1,13},{2,14},{3,15},{4,8},{5,9},{6,10},{7,11},{8,4},{9,5},... | collective-permute-start | bytes 202760 | tf_op jit(solution)/shard_map/ppermute | solution.py:26
  39.0 0.5 %collective-permute-start.9 = (bf16[8,4224]{1,0:T(8,128)(2,1)S(1)}, bf16[8,4224]{1,0:T(8,128)(2,1)S(1)}, u32[]{:S(2)}, u32[]{:S(2)}) collective-permute-start(bf16[8,4224]{1,0:T(8,128)(2,1)S(1)} %get-tuple-element.20), channel_id=1, source_target_pairs={{0,4},{1,5},{2,6},{3,7},{4,0},{5,1},{6,2},{7,3},{8,12},{9,13},{10,... | collective-permute-start | bytes 202760 | tf_op jit(solution)/shard_map/ppermute | solution.py:26
  39.5 2.2 %collective-permute-done.10.refs_2_ = bf16[8,4224]{1,0:T(8,128)(2,1)S(1)} collective-permute-done((bf16[8,4224]{1,0:T(8,128)(2,1)S(1)}, bf16[8,4224]{1,0:T(8,128)(2,1)S(1)}, u32[]{:S(2)}, u32[]{:S(2)}) %collective-permute-start.10) | collective-permute-done | bytes 67616 | tf_op jit(solution)/shard_map/ppermute | solution.py:26
  41.7 1.0 %collective-permute-done.11.refs_3_ = bf16[8,4224]{1,0:T(8,128)(2,1)S(1)} collective-permute-done((bf16[8,4224]{1,0:T(8,128)(2,1)S(1)}, bf16[8,4224]{1,0:T(8,128)(2,1)S(1)}, u32[]{:S(2)}, u32[]{:S(2)}) %collective-permute-start.11) | collective-permute-done | bytes 67616 | tf_op jit(solution)/shard_map/ppermute | solution.py:26
  42.6 0.7 %collective-permute-done.9.refs_1_ = bf16[8,4224]{1,0:T(8,128)(2,1)S(1)} collective-permute-done((bf16[8,4224]{1,0:T(8,128)(2,1)S(1)}, bf16[8,4224]{1,0:T(8,128)(2,1)S(1)}, u32[]{:S(2)}, u32[]{:S(2)}) %collective-permute-start.9) | collective-permute-done | bytes 67616 | tf_op jit(solution)/shard_map/ppermute | solution.py:26
  43.4 1.0 %shard_map.58 = bf16[8,4096]{1,0:T(8,128)(2,1)} custom-call(bf16[8,4224]{1,0:T(8,128)(2,1)S(1)} %get-tuple-element.19.refs_0_, bf16[8,4224]{1,0:T(8,128)(2,1)S(1)} %collective-permute-done.9.refs_1_, bf16[8,4224]{1,0:T(8,128)(2,1)S(1)} %collective-permute-done.10.refs_2_, bf16[8,4224]{1,0:T(8,128)(2,1)S(1)} %collective-permute-done.11.refs_3_), custom_call_target="tpu_custom_call" | custom-call | tf_op jit(solution)/shard_map/pallas_call | solution.py:232
Async XLA Ops:
  1.1 10.4 %collective-permute-start.4 = (bf16[264,512]{1,0:T(8,128)(2,1)S(1)}, bf16[264,512]{1,0:T(8,128)(2,1)S(1)}, u32[]{:S(2)}, u32[]{:S(2)}) collective-permute-start(bf16[264,512]{1,0:T(8,128)(2,1)S(1)} %get-tuple-element.15.refs_4_), channel_id=1, source_target_pairs={{0,2},{1,3},{2,0},{3,1},{4,6},{5,7},{6,4},{7,5},{8,10},{9,11},{10,... | collective-permute-start | bytes 811016 | tf_op jit(solution)/shard_map/ppermute | solution.py:26
  4.2 12.1 %collective-permute-start.7 = (bf16[256,512]{1,0:T(8,128)(2,1)}, bf16[256,512]{1,0:T(8,128)(2,1)S(1)}, u32[]{:S(2)}, u32[]{:S(2)}) collective-permute-start(bf16[256,512]{1,0:T(8,128)(2,1)} %v_ref.1), channel_id=1, source_target_pairs={{0,2},{1,3},{2,0},{3,1},{4,6},{5,7},{6,4},{7,5},{8,10},{9,11},{10,... | collective-permute-start | bytes 786440 | tf_op jit(solution)/shard_map/ppermute | solution.py:26
  4.3 29.2 %collective-permute-start.3 = (bf16[264,512]{1,0:T(8,128)(2,1)S(1)}, bf16[264,512]{1,0:T(8,128)(2,1)S(1)}, u32[]{:S(2)}, u32[]{:S(2)}) collective-permute-start(bf16[264,512]{1,0:T(8,128)(2,1)S(1)} %get-tuple-element.15.refs_4_), channel_id=1, source_target_pairs={{0,1},{1,0},{2,3},{3,2},{4,5},{5,4},{6,7},{7,6},{8,9},{9,8},{10,11... | collective-permute-start | bytes 811016 | tf_op jit(solution)/shard_map/ppermute | solution.py:26
  11.5 22.0 %collective-permute-start.5 = (bf16[264,512]{1,0:T(8,128)(2,1)S(1)}, bf16[264,512]{1,0:T(8,128)(2,1)S(1)}, u32[]{:S(2)}, u32[]{:S(2)}) collective-permute-start(bf16[264,512]{1,0:T(8,128)(2,1)S(1)} %collective-permute-done.4.refs_6_), channel_id=1, source_target_pairs={{0,1},{1,0},{2,3},{3,2},{4,5},{5,4},{6,7},{7,6},{8,9},{9,8},{10,11... | collective-permute-start | bytes 811016 | tf_op jit(solution)/shard_map/ppermute | solution.py:26
  11.5 23.4 %collective-permute-start.6 = (bf16[256,512]{1,0:T(8,128)(2,1)}, bf16[256,512]{1,0:T(8,128)(2,1)S(1)}, u32[]{:S(2)}, u32[]{:S(2)}) collective-permute-start(bf16[256,512]{1,0:T(8,128)(2,1)} %v_ref.1), channel_id=1, source_target_pairs={{0,1},{1,0},{2,3},{3,2},{4,5},{5,4},{6,7},{7,6},{8,9},{9,8},{10,11... | collective-permute-start | bytes 786440 | tf_op jit(solution)/shard_map/ppermute | solution.py:26
  16.3 18.6 %collective-permute-start.8 = (bf16[256,512]{1,0:T(8,128)(2,1)S(1)}, bf16[256,512]{1,0:T(8,128)(2,1)S(1)}, u32[]{:S(2)}, u32[]{:S(2)}) collective-permute-start(bf16[256,512]{1,0:T(8,128)(2,1)S(1)} %collective-permute-done.7.refs_4_), channel_id=1, source_target_pairs={{0,1},{1,0},{2,3},{3,2},{4,5},{5,4},{6,7},{7,6},{8,9},{9,8},{10,11... | collective-permute-start | bytes 786440 | tf_op jit(solution)/shard_map/ppermute | solution.py:26
  16.3 4.6 %collective-permute-start = (bf16[8,4224]{1,0:T(8,128)(2,1)S(1)}, bf16[8,4224]{1,0:T(8,128)(2,1)S(1)}, u32[]{:S(2)}, u32[]{:S(2)}) collective-permute-start(bf16[8,4224]{1,0:T(8,128)(2,1)S(1)} %get-tuple-element.14.refs_0_), channel_id=1, source_target_pairs={{0,4},{1,5},{2,6},{3,7},{4,0},{5,1},{6,2},{7,3},{8,12},{9,13},{10,... | collective-permute-start | bytes 202760 | tf_op jit(solution)/shard_map/ppermute | solution.py:26
  20.9 6.5 %collective-permute-start.1 = (bf16[8,4224]{1,0:T(8,128)(2,1)S(1)}, bf16[8,4224]{1,0:T(8,128)(2,1)S(1)}, u32[]{:S(2)}, u32[]{:S(2)}) collective-permute-start(bf16[8,4224]{1,0:T(8,128)(2,1)S(1)} %get-tuple-element.14.refs_0_), channel_id=1, source_target_pairs={{0,8},{1,9},{2,10},{3,11},{4,12},{5,13},{6,14},{7,15},{8,0},{9,1},... | collective-permute-start | bytes 202760 | tf_op jit(solution)/shard_map/ppermute | solution.py:26
  27.4 6.1 %collective-permute-start.2 = (bf16[8,4224]{1,0:T(8,128)(2,1)S(1)}, bf16[8,4224]{1,0:T(8,128)(2,1)S(1)}, u32[]{:S(2)}, u32[]{:S(2)}) collective-permute-start(bf16[8,4224]{1,0:T(8,128)(2,1)S(1)} %get-tuple-element.14.refs_0_), channel_id=1, source_target_pairs={{0,12},{1,13},{2,14},{3,15},{4,8},{5,9},{6,10},{7,11},{8,4},{9,5},... | collective-permute-start | bytes 202760 | tf_op jit(solution)/shard_map/ppermute | solution.py:26
  35.6 6.0 %collective-permute-start.10 = (bf16[8,4224]{1,0:T(8,128)(2,1)S(1)}, bf16[8,4224]{1,0:T(8,128)(2,1)S(1)}, u32[]{:S(2)}, u32[]{:S(2)}) collective-permute-start(bf16[8,4224]{1,0:T(8,128)(2,1)S(1)} %get-tuple-element.21), channel_id=1, source_target_pairs={{0,8},{1,9},{2,10},{3,11},{4,12},{5,13},{6,14},{7,15},{8,0},{9,1},... | collective-permute-start | bytes 202760 | tf_op jit(solution)/shard_map/ppermute | solution.py:26
  35.7 6.9 %collective-permute-start.11 = (bf16[8,4224]{1,0:T(8,128)(2,1)S(1)}, bf16[8,4224]{1,0:T(8,128)(2,1)S(1)}, u32[]{:S(2)}, u32[]{:S(2)}) collective-permute-start(bf16[8,4224]{1,0:T(8,128)(2,1)S(1)} %get-tuple-element.22), channel_id=1, source_target_pairs={{0,12},{1,13},{2,14},{3,15},{4,8},{5,9},{6,10},{7,11},{8,4},{9,5},... | collective-permute-start | bytes 202760 | tf_op jit(solution)/shard_map/ppermute | solution.py:26
  39.0 4.4 %collective-permute-start.9 = (bf16[8,4224]{1,0:T(8,128)(2,1)S(1)}, bf16[8,4224]{1,0:T(8,128)(2,1)S(1)}, u32[]{:S(2)}, u32[]{:S(2)}) collective-permute-start(bf16[8,4224]{1,0:T(8,128)(2,1)S(1)} %get-tuple-element.20), channel_id=1, source_target_pairs={{0,4},{1,5},{2,6},{3,7},{4,0},{5,1},{6,2},{7,3},{8,12},{9,13},{10,... | collective-permute-start | bytes 202760 | tf_op jit(solution)/shard_map/ppermute | solution.py:26

commit v4 on v3

--- a/solution.py
+++ b/solution.py
@@ -14,7 +14,6 @@
 GROUP = HEADS // KV_HEADS
 HEAD_DIM = 128
 WIDTH = HEADS * HEAD_DIM
-KV_WIDTH = KV_HEADS * HEAD_DIM
 LANES = 128
 SHARE = 4
 FAR = -(2.0**100)
@@ -37,14 +36,14 @@
 
 
 def stage_kernel(
-    q_ref, k_ref, v_ref, page_ref, last_ref, q_out, k_out, v_out, page, last, sems
+    q_ref, k_ref, v_ref, page_ref, last_ref, q_out, k_out, v_out, page_out, last, sems
 ):
-    rows, tokens = q_ref.shape[0], k_ref.shape[0]
+    rows = q_ref.shape[0]
     moves = (
         (last_ref, last),
-        (page_ref, page),
         (q_ref, q_out.at[:, :WIDTH]),
-        (k_ref, k_out.at[:tokens, :]),
+        (page_ref, page_out),
+        (k_ref, k_out),
         (v_ref, v_out),
     )
     copies = [pltpu.make_async_copy(s, d, sems.at[i]) for i, (s, d) in enumerate(moves)]
@@ -57,47 +56,42 @@
         jnp.logical_or, [(row == r) & (lane == last[r]) for r in range(rows)]
     )
     q_out[:, WIDTH:] = jnp.where(seen, 1.0, 0.0).astype(jnp.bfloat16)
-    copies[1].wait()
-    filled = jnp.broadcast_to(page[...], (8, tokens)).astype(jnp.float32)
-    k_out[tokens:, :tokens] = filled.astype(jnp.bfloat16)
-    k_out[tokens:, tokens:] = jnp.zeros((8, k_out.shape[1] - tokens), jnp.bfloat16)
-    for copy in copies[2:]:
+    for copy in copies[1:]:
         copy.wait()
 
 
 def stage_call(row_last, queries, key_cache, value_cache, pages):
-    rows, tokens = queries.shape[0], key_cache.shape[0]
+    rows = queries.shape[0]
     return pl.pallas_call(
         stage_kernel,
         out_shape=[
             jax.ShapeDtypeStruct((rows, WIDTH + LANES), jnp.bfloat16),
-            jax.ShapeDtypeStruct((tokens + 8, KV_WIDTH), jnp.bfloat16),
+            jax.ShapeDtypeStruct(key_cache.shape, jnp.bfloat16),
             jax.ShapeDtypeStruct(value_cache.shape, jnp.bfloat16),
+            jax.ShapeDtypeStruct(pages.shape, jnp.int32),
         ],
         in_specs=[HBM_BLOCK] * 5,
-        out_specs=[VMEM_BLOCK] * 3,
-        scratch_shapes=[
-            pltpu.VMEM((1, tokens), jnp.int32),
-            pltpu.SMEM((rows,), jnp.int32),
-            pltpu.SemaphoreType.DMA((5,)),
-        ],
+        out_specs=[VMEM_BLOCK] * 4,
+        scratch_shapes=[pltpu.SMEM((rows,), jnp.int32), pltpu.SemaphoreType.DMA((5,))],
         compiler_params=pltpu.CompilerParams(vmem_limit_bytes=8 << 20),
     )(*map(in_hbm, (queries, key_cache, value_cache, pages, row_last)))
 
 
 def weights_kernel(n_q, n_kv, *refs):
     q_refs, k_refs = refs[:n_q], refs[n_q : n_q + n_kv]
-    weight_ref, top_ref = refs[n_q + n_kv :]
-    rows, tokens = q_refs[0].shape[0], k_refs[0].shape[0] - 8
+    page_refs = refs[n_q + n_kv : n_q + 2 * n_kv]
+    weight_ref, top_ref = refs[n_q + 2 * n_kv :]
+    rows, tokens = q_refs[0].shape[0], k_refs[0].shape[0]
     lane = lax.broadcasted_iota(jnp.int32, (rows, LANES), 1)
     token_lane = lax.broadcasted_iota(jnp.int32, (tokens, LANES), 1).astype(jnp.float32)
     pick = jnp.where(
         lax.broadcasted_iota(jnp.int32, (8, LANES), 0) == 0, 1.0, 0.0
     ).astype(jnp.bfloat16)
     hides = []
-    for ref in k_refs:
+    for ref in page_refs:
+        pages = jnp.broadcast_to(ref[...], (8, tokens)).astype(jnp.float32)
         column = lax.dot_general(
-            ref[tokens:, :tokens],
+            pages.astype(jnp.bfloat16),
             pick,
             (((0,), (0,)), ((), ())),
             preferred_element_type=jnp.float32,
@@ -116,7 +110,7 @@
         q_all = jnp.concatenate(parts, axis=0).astype(jnp.bfloat16)
         scores = []
         for ref, hide in zip(k_refs, hides):
-            k = ref[:tokens, kv * HEAD_DIM : (kv + 1) * HEAD_DIM]
+            k = ref[:, kv * HEAD_DIM : (kv + 1) * HEAD_DIM]
             scores.append(
                 lax.dot_general(
                     q_all,
@@ -141,25 +135,36 @@
         top_ref[i * rows : (i + 1) * rows, :] = tops[i]
 
 
-def values_kernel(n_q, n_kv, *refs):
-    weight_ref, top_ref = refs[:2]
-    v_refs, out_refs = refs[2 : 2 + n_kv], refs[2 + n_kv :]
-    rows, tokens = out_refs[0].shape[0], v_refs[0].shape[0]
+def weighted(weight_ref, rows, refs, first, kv):
+    tokens = refs[0].shape[0]
+    ones = jnp.ones((tokens, LANES), jnp.bfloat16)
+    parts = []
+    for j, ref in enumerate(refs, first):
+        v = jnp.concatenate(
+            [ref[:, kv * HEAD_DIM : (kv + 1) * HEAD_DIM], ones], axis=1
+        )
+        weights = weight_ref[rows, j * tokens : (j + 1) * tokens]
+        parts.append(jnp.dot(weights, v, preferred_element_type=jnp.float32))
+    return functools.reduce(jnp.add, parts)
+
+
+def early_kernel(weight_ref, *refs):
+    v_refs, sum_ref = refs[:-1], refs[-1]
+    count = weight_ref.shape[0] // KV_HEADS
+    for kv in range(KV_HEADS):
+        rows = slice(kv * count, (kv + 1) * count)
+        sum_ref[rows, :] = weighted(weight_ref, rows, v_refs, 0, kv)
+
+
+def late_kernel(n_q, weight_ref, top_ref, sum_ref, v_ref, *out_refs):
+    rows, tokens = out_refs[0].shape[0], v_ref.shape[0]
+    block = weight_ref.shape[1] // tokens - 1
     count = n_q * GROUP * rows
     lane = lax.broadcasted_iota(jnp.int32, (rows, LANES), 1)
-    ones = jnp.ones((tokens, LANES), jnp.bfloat16)
     stats = [top_ref[i * rows : (i + 1) * rows, :] for i in range(n_q)]
     for kv in range(KV_HEADS):
-        total = None
-        for j, ref in enumerate(v_refs):
-            weights = weight_ref[
-                kv * count : (kv + 1) * count, j * tokens : (j + 1) * tokens
-            ]
-            v = jnp.concatenate(
-                [ref[:, kv * HEAD_DIM : (kv + 1) * HEAD_DIM], ones], axis=1
-            )
-            part = jnp.dot(weights, v, preferred_element_type=jnp.float32)
-            total = part if total is None else total + part
+        span = slice(kv * count, (kv + 1) * count)
+        total = sum_ref[span, :] + weighted(weight_ref, span, [v_ref], block, kv)
         for i, ref in enumerate(out_refs):
             for g in range(GROUP):
                 head = kv * GROUP + g
@@ -175,31 +180,40 @@
         ref[:, WIDTH:] = stat.astype(jnp.bfloat16)
 
 
-def weights_call(q_blocks, k_blocks):
+def weights_call(q_blocks, k_blocks, page_blocks):
     n_q, n_kv = len(q_blocks), len(k_blocks)
-    rows, tokens = q_blocks[0].shape[0], k_blocks[0].shape[0] - 8
+    rows, tokens = q_blocks[0].shape[0], k_blocks[0].shape[0]
     return pl.pallas_call(
         functools.partial(weights_kernel, n_q, n_kv),
         out_shape=[
             jax.ShapeDtypeStruct((n_q * HEADS * rows, n_kv * tokens), jnp.bfloat16),
             jax.ShapeDtypeStruct((n_q * rows, LANES), jnp.float32),
         ],
-        in_specs=[VMEM_BLOCK] * (n_q + n_kv),
+        in_specs=[VMEM_BLOCK] * (n_q + 2 * n_kv),
         out_specs=[VMEM_BLOCK] * 2,
         compiler_params=pltpu.CompilerParams(vmem_limit_bytes=24 << 20),
-    )(*q_blocks, *k_blocks)
-
-
-def values_call(weights, tops, v_blocks, n_q):
-    n_kv = len(v_blocks)
+    )(*q_blocks, *k_blocks, *page_blocks)
+
+
+def early_call(weights, v_blocks):
+    return pl.pallas_call(
+        early_kernel,
+        out_shape=jax.ShapeDtypeStruct((weights.shape[0], 2 * LANES), jnp.float32),
+        in_specs=[VMEM_BLOCK] * (1 + len(v_blocks)),
+        out_specs=VMEM_BLOCK,
+        compiler_params=pltpu.CompilerParams(vmem_limit_bytes=24 << 20),
+    )(weights, *v_blocks)
+
+
+def late_call(weights, tops, sums, v_block, n_q):
     rows = tops.shape[0] // n_q
     return pl.pallas_call(
-        functools.partial(values_kernel, n_q, n_kv),
+        functools.partial(late_kernel, n_q),
         out_shape=[jax.ShapeDtypeStruct((rows, WIDTH + LANES), jnp.bfloat16)] * n_q,
-        in_specs=[VMEM_BLOCK] * (2 + n_kv),
+        in_specs=[VMEM_BLOCK] * 4,
         out_specs=[VMEM_BLOCK] * n_q,
         compiler_params=pltpu.CompilerParams(vmem_limit_bytes=24 << 20),
-    )(weights, tops, *v_blocks)
+    )(weights, tops, sums, v_block)
 
 
 def merge_kernel(n, *refs):
@@ -247,15 +261,19 @@
 def attend(queries, key_cache, value_cache, tile_page, row_last):
     groups = lax.axis_size("blk") // SHARE
     pages = tile_page.reshape(1, -1)
-    own_q, own_k, own_v = stage_call(row_last, queries, key_cache, value_cache, pages)
-    k_blocks = pooled(own_k, own_k)
+    own_q, own_k, own_v, own_page = stage_call(
+        row_last, queries, key_cache, value_cache, pages
+    )
+    k_blocks = pooled(key_cache, own_k)
     v_blocks = pooled(value_cache, own_v)
+    page_blocks = pooled(pages, own_page)
     q_blocks = [own_q] + [swapped(own_q, SHARE * d) for d in range(1, groups)]
     partials = []
     for start in range(0, groups, 4):
         some = q_blocks[start : start + 4]
-        weights, tops = weights_call(some, k_blocks)
-        partials += values_call(weights, tops, v_blocks, len(some))
+        weights, tops = weights_call(some, k_blocks, page_blocks)
+        sums = early_call(weights, v_blocks[:-1])
+        partials += late_call(weights, tops, sums, v_blocks[-1], len(some))
     parts = [partials[0]] + [swapped(partials[d], SHARE * d) for d in range(1, groups)]
     return merge_call(parts)
 

time: 44.5 us -> 52.3 us (1.18)
  waiting for transfers between devices: 24.8 us -> 29.6 us
  starting transfers between devices: 15.2 us -> 18 us
    ppermute x12 -> x15, waiting for transfers between devices: 24.8 us -> 29.6 us  [swapped(): lax.ppermute(block, 'blk', [(i, i ^ distance) for i in range(devices)])]
    ppermute x12 -> x15, starting transfers between devices: 15.2 us -> 18 us  [swapped(): lax.ppermute(block, 'blk', [(i, i ^ distance) for i in range(devices)])]
  transfers between devices with their start and end apart: 12 -> 15, of which waited for: 8 -> 10; matrix products, arithmetic and copies ran while one was open for 0% -> 0% of each run, Pallas kernels for 3% -> 6%
where the time goes in v4:
time: 52.3 us; the launch traced here: 52.1 us
  waiting for transfers between devices  29.6 us (57%)
  starting transfers between devices  18 us (34%)
  Pallas kernels  4.41 us (8%)
    ppermute x15, waiting for transfers between devices, swapped(): lax.ppermute(block, 'blk', [(i, i ^ distance) for i in range(devices)])  29.6 us
    ppermute x15, starting transfers between devices, swapped(): lax.ppermute(block, 'blk', [(i, i ^ distance) for i in range(devices)])  18 us
    pallas_call x1, Pallas kernels, weights_call(): pl.pallas_call(functools.partial(weights_kernel, n_q, n_kv), out_shape=[j...  1.41 us
    pallas_call x1, Pallas kernels, stage_call(): pl.pallas_call(stage_kernel, out_shape=[jax.ShapeDtypeStruct((rows, WIDTH...  1.13 us
  transfers between devices with their start and end apart: 15, of which 10 were waited for; matrix products, arithmetic and copies ran while one was open for 0% of the time, Pallas kernels for 6%

profile of v4, /device:TPU:0, one launch (start us, length us, event | category | flops | bytes accessed | tf_op | source)
XLA Modules:
  0.0 52.1 jit_solution(10588319457577984782)
XLA Ops:
  0.0 3.0 %collective-permute-start.4 = (bf16[256,512]{1,0:T(8,128)(2,1)}, bf16[256,512]{1,0:T(8,128)(2,1)S(1)}, u32[]{:S(2)}, u32[]{:S(2)}) collective-permute-start(bf16[256,512]{1,0:T(8,128)(2,1)} %k_ref.1), channel_id=1, source_target_pairs={{0,2},{1,3},{2,0},{3,1},{4,6},{5,7},{6,4},{7,5},{8,10},{9,11},{10,... | collective-permute-start | bytes 786440 | tf_op jit(solution)/shard_map/ppermute | solution.py:25
  3.0 0.0 collective-permute-start.10
  3.0 0.0 collective-permute-start.3
  3.0 7.3 %collective-permute-done.4.refs_6_ = bf16[256,512]{1,0:T(8,128)(2,1)S(1)} collective-permute-done((bf16[256,512]{1,0:T(8,128)(2,1)}, bf16[256,512]{1,0:T(8,128)(2,1)S(1)}, u32[]{:S(2)}, u32[]{:S(2)}) %collective-permute-start.4) | collective-permute-done | bytes 262176 | tf_op jit(solution)/shard_map/ppermute | solution.py:25
  10.4 0.0 collective-permute-start.5
  10.4 0.5 collective-permute-start.9
  10.9 4.3 %collective-permute-done.10.refs_2_ = bf16[256,512]{1,0:T(8,128)(2,1)S(1)} collective-permute-done((bf16[256,512]{1,0:T(8,128)(2,1)}, bf16[256,512]{1,0:T(8,128)(2,1)S(1)}, u32[]{:S(2)}, u32[]{:S(2)}) %collective-permute-start.10) | collective-permute-done | bytes 262176 | tf_op jit(solution)/shard_map/ppermute | solution.py:25
  15.1 0.0 collective-permute-start.11
  15.1 0.5 collective-permute-start.6
  15.6 1.0 %collective-permute-done.6.refs_9_ = s32[1,256]{1,0:T(1,128)S(1)} collective-permute-done((s32[1,256]{1,0:T(1,128)}, s32[1,256]{1,0:T(1,128)S(1)}, u32[]{:S(2)}, u32[]{:S(2)}) %collective-permute-start.6) | collective-permute-done | bytes 1056 | tf_op jit(solution)/shard_map/ppermute | solution.py:25
  16.7 1.7 %collective-permute-start.7 = (s32[1,256]{1,0:T(1,128)}, s32[1,256]{1,0:T(1,128)S(1)}, u32[]{:S(2)}, u32[]{:S(2)}) collective-permute-start(s32[1,256]{1,0:T(1,128)} %bitcast.2), channel_id=1, source_target_pairs={{0,2},{1,3},{2,0},{3,1},{4,6},{5,7},{6,4},{7,5},{8,10},{9,11},{10,... | collective-permute-start | bytes 3080 | tf_op jit(solution)/shard_map/ppermute | solution.py:25
  18.4 2.0 %collective-permute-done.7.refs_10_ = s32[1,256]{1,0:T(1,128)S(1)} collective-permute-done((s32[1,256]{1,0:T(1,128)}, s32[1,256]{1,0:T(1,128)S(1)}, u32[]{:S(2)}, u32[]{:S(2)}) %collective-permute-start.7) | collective-permute-done | bytes 1056 | tf_op jit(solution)/shard_map/ppermute | solution.py:25
  20.5 0.0 collective-permute-start.8
  20.5 1.1 %shard_map.55 = (bf16[8,4224]{1,0:T(8,128)(2,1)S(1)}, bf16[256,512]{1,0:T(8,128)(2,1)S(1)}, bf16[256,512]{1,0:T(8,128)(2,1)S(1)}, s32[1,256]{1,0:T(1,128)S(1)}) custom-call(bf16[8,4096]{1,0:T(8,128)(2,1)} %q_ref.1, bf16[256,512]{1,0:T(8,128)(2,1)} %k_ref.1, bf16[256,512]{1,0:T(8,128)(2,1)} %v_ref.1, s32[1,256]{1,0:T(1,128)} %bitcast.3, s32[8]{0:T(128)} %last_ref.1), custom_call_target="tpu_custom_call" | custom-call | tf_op jit(solution)/shard_map/pallas_call | solution.py:65
  21.6 0.0 collective-permute-done.8.refs_11_
  21.6 1.9 %collective-permute-start = (bf16[8,4224]{1,0:T(8,128)(2,1)S(1)}, bf16[8,4224]{1,0:T(8,128)(2,1)S(1)}, u32[]{:S(2)}, u32[]{:S(2)}) collective-permute-start(bf16[8,4224]{1,0:T(8,128)(2,1)S(1)} %get-tuple-element.15.refs_0_), channel_id=1, source_target_pairs={{0,4},{1,5},{2,6},{3,7},{4,0},{5,1},{6,2},{7,3},{8,12},{9,13},{10,... | collective-permute-start | bytes 202760 | tf_op jit(solution)/shard_map/ppermute | solution.py:25
  23.5 2.8 %collective-permute-done.refs_1_ = bf16[8,4224]{1,0:T(8,128)(2,1)S(1)} collective-permute-done((bf16[8,4224]{1,0:T(8,128)(2,1)S(1)}, bf16[8,4224]{1,0:T(8,128)(2,1)S(1)}, u32[]{:S(2)}, u32[]{:S(2)}) %collective-permute-start) | collective-permute-done | bytes 67616 | tf_op jit(solution)/shard_map/ppermute | solution.py:25
  26.3 2.8 %collective-permute-start.1 = (bf16[8,4224]{1,0:T(8,128)(2,1)S(1)}, bf16[8,4224]{1,0:T(8,128)(2,1)S(1)}, u32[]{:S(2)}, u32[]{:S(2)}) collective-permute-start(bf16[8,4224]{1,0:T(8,128)(2,1)S(1)} %get-tuple-element.15.refs_0_), channel_id=1, source_target_pairs={{0,8},{1,9},{2,10},{3,11},{4,12},{5,13},{6,14},{7,15},{8,0},{9,1},... | collective-permute-start | bytes 202760 | tf_op jit(solution)/shard_map/ppermute | solution.py:25
  29.0 3.7 %collective-permute-done.1.refs_2_ = bf16[8,4224]{1,0:T(8,128)(2,1)S(1)} collective-permute-done((bf16[8,4224]{1,0:T(8,128)(2,1)S(1)}, bf16[8,4224]{1,0:T(8,128)(2,1)S(1)}, u32[]{:S(2)}, u32[]{:S(2)}) %collective-permute-start.1) | collective-permute-done | bytes 67616 | tf_op jit(solution)/shard_map/ppermute | solution.py:25
  32.8 3.2 %collective-permute-start.2 = (bf16[8,4224]{1,0:T(8,128)(2,1)S(1)}, bf16[8,4224]{1,0:T(8,128)(2,1)S(1)}, u32[]{:S(2)}, u32[]{:S(2)}) collective-permute-start(bf16[8,4224]{1,0:T(8,128)(2,1)S(1)} %get-tuple-element.15.refs_0_), channel_id=1, source_target_pairs={{0,12},{1,13},{2,14},{3,15},{4,8},{5,9},{6,10},{7,11},{8,4},{9,5},... | collective-permute-start | bytes 202760 | tf_op jit(solution)/shard_map/ppermute | solution.py:25
  36.0 2.9 %collective-permute-done.2.refs_3_ = bf16[8,4224]{1,0:T(8,128)(2,1)S(1)} collective-permute-done((bf16[8,4224]{1,0:T(8,128)(2,1)S(1)}, bf16[8,4224]{1,0:T(8,128)(2,1)S(1)}, u32[]{:S(2)}, u32[]{:S(2)}) %collective-permute-start.2) | collective-permute-done | bytes 67616 | tf_op jit(solution)/shard_map/ppermute | solution.py:25
  38.9 0.0 collective-permute-done.3.refs_5_
  38.9 0.0 collective-permute-done.5.refs_7_
  38.9 1.4 %shard_map.56 = (bf16[1024,1024]{1,0:T(8,128)(2,1)S(1)}, f32[32,128]{1,0:T(8,128)S(1)}) custom-call(bf16[8,4224]{1,0:T(8,128)(2,1)S(1)} %get-tuple-element.15.refs_0_, bf16[8,4224]{1,0:T(8,128)(2,1)S(1)} %collective-permute-done.refs_1_, bf16[8,4224]{1,0:T(8,128)(2,1)S(1)} %collective-permute-done.1.refs_2_, ...), custom_call_target="tpu_custom_call" | custom-call | tf_op jit(solution)/shard_map/pallas_call | solution.py:186
  40.3 0.0 collective-permute-done.9.refs_1_
  40.3 0.6 %shard_map.57.sum_ref = f32[1024,256]{1,0:T(8,128)S(1)} custom-call(bf16[1024,1024]{1,0:T(8,128)(2,1)S(1)} %get-tuple-element.18.weight_ref, bf16[256,512]{1,0:T(8,128)(2,1)S(1)} %get-tuple-element.20.refs_0_, bf16[256,512]{1,0:T(8,128)(2,1)S(1)} %collective-permute-done.9.refs_1_, bf16[256,512]{1,0:T(8,128)(2,1)S(1)} %collective-permute-done.10.refs_2_), custom_call_target="tpu_custom_call" | custom-call | tf_op jit(solution)/shard_map/pallas_call | solution.py:199
  40.9 0.0 collective-permute-done.11.v_ref
  40.9 0.3 shard_map.58
  41.2 0.1 collective-permute-start.12
  41.3 3.8 %collective-permute-start.13 = (bf16[8,4224]{1,0:T(8,128)(2,1)S(1)}, bf16[8,4224]{1,0:T(8,128)(2,1)S(1)}, u32[]{:S(2)}, u32[]{:S(2)}) collective-permute-start(bf16[8,4224]{1,0:T(8,128)(2,1)S(1)} %get-tuple-element.23), channel_id=1, source_target_pairs={{0,8},{1,9},{2,10},{3,11},{4,12},{5,13},{6,14},{7,15},{8,0},{9,1},... | collective-permute-start | bytes 202760 | tf_op jit(solution)/shard_map/ppermute | solution.py:25
  45.0 0.6 %collective-permute-start.14 = (bf16[8,4224]{1,0:T(8,128)(2,1)S(1)}, bf16[8,4224]{1,0:T(8,128)(2,1)S(1)}, u32[]{:S(2)}, u32[]{:S(2)}) collective-permute-start(bf16[8,4224]{1,0:T(8,128)(2,1)S(1)} %get-tuple-element.24), channel_id=1, source_target_pairs={{0,12},{1,13},{2,14},{3,15},{4,8},{5,9},{6,10},{7,11},{8,4},{9,5},... | collective-permute-start | bytes 202760 | tf_op jit(solution)/shard_map/ppermute | solution.py:25
  45.7 0.1 collective-permute-done.12.refs_1_
  45.7 3.0 %collective-permute-done.13.refs_2_ = bf16[8,4224]{1,0:T(8,128)(2,1)S(1)} collective-permute-done((bf16[8,4224]{1,0:T(8,128)(2,1)S(1)}, bf16[8,4224]{1,0:T(8,128)(2,1)S(1)}, u32[]{:S(2)}, u32[]{:S(2)}) %collective-permute-start.13) | collective-permute-done | bytes 67616 | tf_op jit(solution)/shard_map/ppermute | solution.py:25
  48.8 2.4 %collective-permute-done.14.refs_3_ = bf16[8,4224]{1,0:T(8,128)(2,1)S(1)} collective-permute-done((bf16[8,4224]{1,0:T(8,128)(2,1)S(1)}, bf16[8,4224]{1,0:T(8,128)(2,1)S(1)}, u32[]{:S(2)}, u32[]{:S(2)}) %collective-permute-start.14) | collective-permute-done | bytes 67616 | tf_op jit(solution)/shard_map/ppermute | solution.py:25
  51.1 1.0 %shard_map.59 = bf16[8,4096]{1,0:T(8,128)(2,1)} custom-call(bf16[8,4224]{1,0:T(8,128)(2,1)S(1)} %get-tuple-element.21.refs_0_, bf16[8,4224]{1,0:T(8,128)(2,1)S(1)} %collective-permute-done.12.refs_1_, bf16[8,4224]{1,0:T(8,128)(2,1)S(1)} %collective-permute-done.13.refs_2_, bf16[8,4224]{1,0:T(8,128)(2,1)S(1)} %collective-permute-done.14.refs_3_), custom_call_target="tpu_custom_call" | custom-call | tf_op jit(solution)/shard_map/pallas_call | solution.py:246
Async XLA Ops:
  0.0 10.4 %collective-permute-start.4 = (bf16[256,512]{1,0:T(8,128)(2,1)}, bf16[256,512]{1,0:T(8,128)(2,1)S(1)}, u32[]{:S(2)}, u32[]{:S(2)}) collective-permute-start(bf16[256,512]{1,0:T(8,128)(2,1)} %k_ref.1), channel_id=1, source_target_pairs={{0,2},{1,3},{2,0},{3,1},{4,6},{5,7},{6,4},{7,5},{8,10},{9,11},{10,... | collective-permute-start | bytes 786440 | tf_op jit(solution)/shard_map/ppermute | solution.py:25
  3.0 12.1 %collective-permute-start.10 = (bf16[256,512]{1,0:T(8,128)(2,1)}, bf16[256,512]{1,0:T(8,128)(2,1)S(1)}, u32[]{:S(2)}, u32[]{:S(2)}) collective-permute-start(bf16[256,512]{1,0:T(8,128)(2,1)} %v_ref.1), channel_id=1, source_target_pairs={{0,2},{1,3},{2,0},{3,1},{4,6},{5,7},{6,4},{7,5},{8,10},{9,11},{10,... | collective-permute-start | bytes 786440 | tf_op jit(solution)/shard_map/ppermute | solution.py:25
  3.0 35.8 %collective-permute-start.3 = (bf16[256,512]{1,0:T(8,128)(2,1)}, bf16[256,512]{1,0:T(8,128)(2,1)S(1)}, u32[]{:S(2)}, u32[]{:S(2)}) collective-permute-start(bf16[256,512]{1,0:T(8,128)(2,1)} %k_ref.1), channel_id=1, source_target_pairs={{0,1},{1,0},{2,3},{3,2},{4,5},{5,4},{6,7},{7,6},{8,9},{9,8},{10,11... | collective-permute-start | bytes 786440 | tf_op jit(solution)/shard_map/ppermute | solution.py:25
  10.4 28.5 %collective-permute-start.5 = (bf16[256,512]{1,0:T(8,128)(2,1)S(1)}, bf16[256,512]{1,0:T(8,128)(2,1)S(1)}, u32[]{:S(2)}, u32[]{:S(2)}) collective-permute-start(bf16[256,512]{1,0:T(8,128)(2,1)S(1)} %collective-permute-done.4.refs_6_), channel_id=1, source_target_pairs={{0,1},{1,0},{2,3},{3,2},{4,5},{5,4},{6,7},{7,6},{8,9},{9,8},{10,11... | collective-permute-start | bytes 786440 | tf_op jit(solution)/shard_map/ppermute | solution.py:25
  10.4 29.9 %collective-permute-start.9 = (bf16[256,512]{1,0:T(8,128)(2,1)}, bf16[256,512]{1,0:T(8,128)(2,1)S(1)}, u32[]{:S(2)}, u32[]{:S(2)}) collective-permute-start(bf16[256,512]{1,0:T(8,128)(2,1)} %v_ref.1), channel_id=1, source_target_pairs={{0,1},{1,0},{2,3},{3,2},{4,5},{5,4},{6,7},{7,6},{8,9},{9,8},{10,11... | collective-permute-start | bytes 786440 | tf_op jit(solution)/shard_map/ppermute | solution.py:25
  15.1 25.7 %collective-permute-start.11 = (bf16[256,512]{1,0:T(8,128)(2,1)S(1)}, bf16[256,512]{1,0:T(8,128)(2,1)S(1)}, u32[]{:S(2)}, u32[]{:S(2)}) collective-permute-start(bf16[256,512]{1,0:T(8,128)(2,1)S(1)} %collective-permute-done.10.refs_2_), channel_id=1, source_target_pairs={{0,1},{1,0},{2,3},{3,2},{4,5},{5,4},{6,7},{7,6},{8,9},{9,8},{10,11... | collective-permute-start | bytes 786440 | tf_op jit(solution)/shard_map/ppermute | solution.py:25
  15.1 1.5 %collective-permute-start.6 = (s32[1,256]{1,0:T(1,128)}, s32[1,256]{1,0:T(1,128)S(1)}, u32[]{:S(2)}, u32[]{:S(2)}) collective-permute-start(s32[1,256]{1,0:T(1,128)} %bitcast.1), channel_id=1, source_target_pairs={{0,1},{1,0},{2,3},{3,2},{4,5},{5,4},{6,7},{7,6},{8,9},{9,8},{10,11... | collective-permute-start | bytes 3080 | tf_op jit(solution)/shard_map/ppermute | solution.py:25
  16.7 3.8 %collective-permute-start.7 = (s32[1,256]{1,0:T(1,128)}, s32[1,256]{1,0:T(1,128)S(1)}, u32[]{:S(2)}, u32[]{:S(2)}) collective-permute-start(s32[1,256]{1,0:T(1,128)} %bitcast.2), channel_id=1, source_target_pairs={{0,2},{1,3},{2,0},{3,1},{4,6},{5,7},{6,4},{7,5},{8,10},{9,11},{10,... | collective-permute-start | bytes 3080 | tf_op jit(solution)/shard_map/ppermute | solution.py:25
  20.5 1.2 %collective-permute-start.8 = (s32[1,256]{1,0:T(1,128)S(1)}, s32[1,256]{1,0:T(1,128)S(1)}, u32[]{:S(2)}, u32[]{:S(2)}) collective-permute-start(s32[1,256]{1,0:T(1,128)S(1)} %collective-permute-done.7.refs_10_), channel_id=1, source_target_pairs={{0,1},{1,0},{2,3},{3,2},{4,5},{5,4},{6,7},{7,6},{8,9},{9,8},{10,11... | collective-permute-start | bytes 3080 | tf_op jit(solution)/shard_map/ppermute | solution.py:25
  21.6 4.7 %collective-permute-start = (bf16[8,4224]{1,0:T(8,128)(2,1)S(1)}, bf16[8,4224]{1,0:T(8,128)(2,1)S(1)}, u32[]{:S(2)}, u32[]{:S(2)}) collective-permute-start(bf16[8,4224]{1,0:T(8,128)(2,1)S(1)} %get-tuple-element.15.refs_0_), channel_id=1, source_target_pairs={{0,4},{1,5},{2,6},{3,7},{4,0},{5,1},{6,2},{7,3},{8,12},{9,13},{10,... | collective-permute-start | bytes 202760 | tf_op jit(solution)/shard_map/ppermute | solution.py:25
  26.3 6.5 %collective-permute-start.1 = (bf16[8,4224]{1,0:T(8,128)(2,1)S(1)}, bf16[8,4224]{1,0:T(8,128)(2,1)S(1)}, u32[]{:S(2)}, u32[]{:S(2)}) collective-permute-start(bf16[8,4224]{1,0:T(8,128)(2,1)S(1)} %get-tuple-element.15.refs_0_), channel_id=1, source_target_pairs={{0,8},{1,9},{2,10},{3,11},{4,12},{5,13},{6,14},{7,15},{8,0},{9,1},... | collective-permute-start | bytes 202760 | tf_op jit(solution)/shard_map/ppermute | solution.py:25
  32.8 6.1 %collective-permute-start.2 = (bf16[8,4224]{1,0:T(8,128)(2,1)S(1)}, bf16[8,4224]{1,0:T(8,128)(2,1)S(1)}, u32[]{:S(2)}, u32[]{:S(2)}) collective-permute-start(bf16[8,4224]{1,0:T(8,128)(2,1)S(1)} %get-tuple-element.15.refs_0_), channel_id=1, source_target_pairs={{0,12},{1,13},{2,14},{3,15},{4,8},{5,9},{6,10},{7,11},{8,4},{9,5},... | collective-permute-start | bytes 202760 | tf_op jit(solution)/shard_map/ppermute | solution.py:25
  41.2 4.5 %collective-permute-start.12 = (bf16[8,4224]{1,0:T(8,128)(2,1)S(1)}, bf16[8,4224]{1,0:T(8,128)(2,1)S(1)}, u32[]{:S(2)}, u32[]{:S(2)}) collective-permute-start(bf16[8,4224]{1,0:T(8,128)(2,1)S(1)} %get-tuple-element.22), channel_id=1, source_target_pairs={{0,4},{1,5},{2,6},{3,7},{4,0},{5,1},{6,2},{7,3},{8,12},{9,13},{10,... | collective-permute-start | bytes 202760 | tf_op jit(solution)/shard_map/ppermute | solution.py:25
  41.3 7.5 %collective-permute-start.13 = (bf16[8,4224]{1,0:T(8,128)(2,1)S(1)}, bf16[8,4224]{1,0:T(8,128)(2,1)S(1)}, u32[]{:S(2)}, u32[]{:S(2)}) collective-permute-start(bf16[8,4224]{1,0:T(8,128)(2,1)S(1)} %get-tuple-element.23), channel_id=1, source_target_pairs={{0,8},{1,9},{2,10},{3,11},{4,12},{5,13},{6,14},{7,15},{8,0},{9,1},... | collective-permute-start | bytes 202760 | tf_op jit(solution)/shard_map/ppermute | solution.py:25
  45.0 6.1 %collective-permute-start.14 = (bf16[8,4224]{1,0:T(8,128)(2,1)S(1)}, bf16[8,4224]{1,0:T(8,128)(2,1)S(1)}, u32[]{:S(2)}, u32[]{:S(2)}) collective-permute-start(bf16[8,4224]{1,0:T(8,128)(2,1)S(1)} %get-tuple-element.24), channel_id=1, source_target_pairs={{0,12},{1,13},{2,14},{3,15},{4,8},{5,9},{6,10},{7,11},{8,4},{9,5},... | collective-permute-start | bytes 202760 | tf_op jit(solution)/shard_map/ppermute | solution.py:25
